TPU v7x, 32 devices: a whole 2x2x4 slice. The times are simulated.
32 devices in a mesh: grp: 2 (over y), tm: 8 (over z, x), apa: 2 (over core).
Axes of the slice: x: 2, y: 2, z: 4, core: 2. Of those that a mesh axis runs over, the one named last changes fastest.
Arguments:
- waveforms: bfloat16 [5120, 2048], P(('grp', 'apa'), 'tm'), parts along dimension 0, may hold values from -6 to 6
- time_kernel: bfloat16 [3, 64], replicated, may hold values from -0.75 to 0.75
- wire_slot: int32 [5120], P('grp'), parts along dimension 0, may hold values from 0 to 2559, each once
- tick_offset: int32 [5120], P('grp'), parts along dimension 0, may hold values from 0 to 63
- bad_channel: int32 [5120], P('grp'), parts along dimension 0, may hold values 0 or 1
- induction_real: float32 [2, 800], replicated, may hold values from 0.5 to 2
- induction_imaginary: float32 [2, 800], replicated, may hold values from -1 to 1
- induction_filter: float32 [2, 800], replicated, may hold values from 0.2 to 1
- collection_real: float32 [960], replicated, may hold values from 0.5 to 2
- collection_imaginary: float32 [960], replicated, may hold values from -1 to 1
- collection_filter: float32 [960], replicated, may hold values from 0.2 to 1
Outputs:
- deconvolved: float32 [5120, 2048], P('grp', ('tm', 'apa')), parts along dimension 0
There are 2 independent parts, one for each index of `grp`. A program takes and returns all parts, laid end to end along the dimension named above; an argument that names none is the same for every part. Nothing has to cross between parts.
Inputs may be any that keep to these rules, and one draw needn't show every extreme that they name: A permutation: readout channel c is slot wire_slot[c] of the plane layout, whose assemblies hold 2560 slots each, U wires first, then V, then W. `bad_channel`: 1 marks a bad channel.
All inputs are finite; a program needn't handle non-finite values.
Results may differ from a plain program's by a relative error of at most 0.0051.
Values may be sent and summed in bfloat16 or wider, within the bound.
No kernel may reach another device: no remote copies, remote signals or barrier semaphores. Data moves between devices by JAX's collectives and lax.ppermute only.
A program may use at most 64 MiB of HBM per device.

v0:
```python
import math

import jax
import jax.numpy as jnp
from jax import lax
from jax.sharding import PartitionSpec as P

INDUCTION_WIRES = 800
COLLECTION_WIRES = 960
OFFSET_RANGE = 64


def shifted(value, axis, steps):
    count = lax.axis_size(axis)
    pairs = [(source, (source + steps) % count) for source in range(count)]
    return lax.ppermute(value, axis, pairs)


def slot_plane(slot_index):
    assembly_wires = 2 * INDUCTION_WIRES + COLLECTION_WIRES
    within = slot_index % assembly_wires
    return (within >= INDUCTION_WIRES).astype(jnp.int32) + (within >= 2 * INDUCTION_WIRES).astype(
        jnp.int32
    )


def fourier_tables(wire_count):
    positions = jnp.arange(wire_count, dtype=jnp.int32)
    phase_turns = positions[:, None] * positions[None, :] % wire_count
    phase_angle = phase_turns.astype(jnp.float32) * (2.0 * math.pi / wire_count)
    cosine = jnp.cos(phase_angle).astype(jnp.bfloat16)
    sine_table = jnp.sin(phase_angle).astype(jnp.bfloat16)
    forward = jnp.concatenate([cosine, sine_table], 0)
    backward = jnp.concatenate([cosine, -sine_table], 1)
    return (forward, backward)


def wire_deconvolve(plane_rows, tables, response_real, response_imaginary, filter_gain):
    forward, backward = tables
    wire_count = plane_rows.shape[0]
    magnitude = response_real * response_real + response_imaginary * response_imaginary
    ratio_real = (filter_gain * response_real / magnitude)[:, None]
    ratio_imaginary = (-filter_gain * response_imaginary / magnitude)[:, None]
    spectrum = jnp.dot(forward, plane_rows, preferred_element_type=jnp.float32)
    cosine_part = spectrum[:wire_count]
    sine_part = spectrum[wire_count:]
    product = jnp.concatenate(
        [
            cosine_part * ratio_real + sine_part * ratio_imaginary,
            cosine_part * ratio_imaginary - sine_part * ratio_real,
        ],
        0,
    ).astype(jnp.bfloat16)
    return jnp.dot(backward, product, preferred_element_type=jnp.float32) * (1.0 / wire_count)


def deconvolve_planes(
    ordered,
    induction_real,
    induction_imaginary,
    induction_filter,
    collection_real,
    collection_imaginary,
    collection_filter,
):
    induction_tables = fourier_tables(INDUCTION_WIRES)
    collection_tables = fourier_tables(COLLECTION_WIRES)
    results = []
    for plane_index in range(2):
        row_start = plane_index * INDUCTION_WIRES
        results.append(
            wire_deconvolve(
                ordered[row_start : row_start + INDUCTION_WIRES],
                induction_tables,
                induction_real[plane_index],
                induction_imaginary[plane_index],
                induction_filter[plane_index],
            )
        )
    row_start = 2 * INDUCTION_WIRES
    results.append(
        wire_deconvolve(
            ordered[row_start : row_start + COLLECTION_WIRES],
            collection_tables,
            collection_real,
            collection_imaginary,
            collection_filter,
        )
    )
    return jnp.concatenate(results, 0)


def toeplitz(kernel_row):
    tap_count = kernel_row.shape[0]
    padded = jnp.concatenate(
        [
            jnp.zeros((tap_count - 1,), kernel_row.dtype),
            kernel_row,
            jnp.zeros((tap_count,), kernel_row.dtype),
        ]
    )
    padded_length = padded.shape[0]
    rolled = jnp.roll(padded, 1 - 2 * tap_count)
    tiled = jnp.tile(rolled, 2 * tap_count)[: 2 * tap_count * (padded_length - 1)]
    return tiled.reshape(2 * tap_count, padded_length - 1)[:, :tap_count]


def shift_rows(extended, offsets, length):
    current = extended
    for bit_number in range((OFFSET_RANGE - 1).bit_length()):
        step_ticks = 1 << bit_number
        moved = jnp.concatenate(
            [jnp.zeros((current.shape[0], step_ticks), current.dtype), current[:, :-step_ticks]], 1
        )
        chosen = offsets >> bit_number & 1 == 1
        current = jnp.where(chosen[:, None], moved, current)
    return current[:, OFFSET_RANGE : OFFSET_RANGE + length]


def convolve(aligned, table, tap_count):
    row_count = aligned.shape[0]
    blocks = aligned.reshape(row_count, aligned.shape[1] // tap_count, tap_count)
    result = jnp.einsum(
        "cjq,qr->cjr", blocks[:, :-1], table[:tap_count], preferred_element_type=jnp.float32
    )
    result = result + jnp.einsum(
        "cjq,qr->cjr", blocks[:, 1:], table[tap_count:], preferred_element_type=jnp.float32
    )
    return result.reshape(row_count, -1)


def local(
    waveforms,
    time_kernel,
    wire_slot,
    tick_offset,
    bad_channel,
    induction_real,
    induction_imaginary,
    induction_filter,
    collection_real,
    collection_imaginary,
    collection_filter,
):
    tap_count = time_kernel.shape[1]
    tail_ticks = tap_count + OFFSET_RANGE
    channel_count = wire_slot.shape[0]
    inverse = (
        jnp.zeros((channel_count,), jnp.int32)
        .at[wire_slot]
        .set(jnp.arange(channel_count, dtype=jnp.int32))
    )
    tables = [toeplitz(time_kernel[plane_index]) for plane_index in range(3)]
    row_count = waveforms.shape[0]
    first_row = lax.axis_index("apa") * row_count
    local_offset = lax.dynamic_slice_in_dim(tick_offset, first_row, row_count)
    local_bad = lax.dynamic_slice_in_dim(bad_channel, first_row, row_count)
    local_plane = slot_plane(lax.dynamic_slice_in_dim(wire_slot, first_row, row_count))
    masked = waveforms * (1 - local_bad).astype(jnp.bfloat16)[:, None]
    earlier = shifted(masked[:, -tail_ticks:], "tm", 1)
    aligned = shift_rows(
        jnp.concatenate([earlier, masked], 1), local_offset, masked.shape[1] + tap_count
    )
    summed = jnp.zeros(masked.shape, jnp.float32)
    for plane_index in range(3):
        summed = summed + jnp.where(
            (local_plane == plane_index)[:, None],
            convolve(aligned, tables[plane_index], tap_count),
            0.0,
        )
    filtered = summed.astype(jnp.bfloat16)
    regrouped = lax.all_to_all(filtered, "apa", split_axis=1, concat_axis=0, tiled=True)
    ordered = regrouped[inverse]
    return deconvolve_planes(
        ordered,
        induction_real,
        induction_imaginary,
        induction_filter,
        collection_real,
        collection_imaginary,
        collection_filter,
    )


def solution(mesh):
    placed = (
        P(("grp", "apa"), "tm"),
        P(),
        P("grp"),
        P("grp"),
        P("grp"),
        P(),
        P(),
        P(),
        P(),
        P(),
        P(),
    )
    return jax.shard_map(
        local, mesh=mesh, in_specs=placed, out_specs=P("grp", ("tm", "apa")), check_vma=False
    )
```

profile of v0, /device:TPU:0, one launch (start us, length us, event | category | flops | bytes accessed | tf_op | source)
XLA Modules:
  0.0 106.4 jit_solution(6117354309688895531)
XLA Ops:
  0.0 0.8 subtract_convert_fusion.3
  0.8 1.3 %broadcast_multiply_fusion = bf16[1280,256]{1,0:T(8,128)(2,1)S(1)} fusion(bf16[1280,256]{1,0:T(8,128)(2,1)} %param.11, bf16[1280]{0:T(1024)(128)(2,1)S(1)} %subtract_convert_fusion.3), kind=kLoop, calls=%fused_computation.83 | loop fusion | flops 327680 | bytes 1313280 | tf_op jit(solution)/shard_map/mul | solution.py:159
  2.2 3.0 %collective-permute-start = (bf16[1280,128]{1,0:T(8,128)(2,1)S(1)}, bf16[1280,128]{1,0:T(8,128)(2,1)S(1)}, u32[]{:S(2)}, u32[]{:S(2)}) collective-permute-start(bf16[1280,128]{1,0:T(8,128)(2,1)S(1)} %slice.176), channel_id=1, source_target_pairs={{0,2},{2,4},{4,6},{6,8},{8,10},{10,12},{12,14},{14,0},{1,3},{3,5},... | collective-permute-start | bytes 983048 | tf_op jit(solution)/shard_map/ppermute | solution.py:16
  5.3 12.9 %sine_convert_fusion.1 = (bf16[800,800]{1,0:T(8,128)(2,1)}, bf16[800,800]{1,0:T(8,128)(2,1)S(1)}) fusion(), kind=kLoop, calls=%fused_computation.23 | loop fusion | flops 7040000 | bytes 2560000 | tf_op jit(solution)/shard_map/convert_element_type | solution.py:32
  18.2 11.9 %fusion.33 = bf16[800,800]{1,0:T(8,128)(2,1)} fusion(), kind=kLoop, calls=%fused_computation.58 | loop fusion | flops 8320000 | bytes 1280000 | tf_op jit(solution)/shard_map/neg | solution.py:34
  30.1 16.1 %fusion.32 = bf16[960,960]{1,0:T(8,128)(2,1)} fusion(), kind=kLoop, calls=%fused_computation.57 | loop fusion | flops 11980800 | bytes 1843200 | tf_op jit(solution)/shard_map/neg | solution.py:34
  46.4 10.1 %scatter_custom_fusion = s32[2560]{0:T(1024)S(1)} fusion(s32[2560]{0:T(1024)S(1)} %compare_select_fusion.1, s32[2560]{0:T(1024)S(1)} %iota.17, s32[]{:T(128)} %constant.20.clone.1), kind=kCustom, calls=%fused_computation.109 | custom fusion | bytes 10244 | tf_op jit(solution)/shard_map/scatter | solution.py:151
  56.5 0.6 fusion.62
  59.1 17.3 %sine_convert_fusion = (bf16[960,960]{1,0:T(8,128)(2,1)}, bf16[960,960]{1,0:T(8,128)(2,1)}) fusion(), kind=kLoop, calls=%fused_computation.10 | loop fusion | flops 10137600 | bytes 3686400 | tf_op jit(solution)/shard_map/convert_element_type | solution.py:32
  76.5 0.9 fusion.31
  77.5 0.9 pad_select_fusion.3
  78.4 0.9 pad_select_fusion.2
  79.3 0.9 pad_select_fusion.1
  80.3 0.9 pad_select_fusion
  81.2 1.0 slice_select_fusion
  82.2 0.6 copy.14
  82.8 0.3 fusion.37
  83.1 0.4 convolution_add_fusion.2
  83.5 0.4 fusion.39
  83.8 0.3 convolution_add_fusion.1
  84.5 0.4 convolution_add_fusion
  85.2 4.3 %all_to_all.16 = bf16[1280,2,128]{0,2,1:T(8,128)(2,1)S(1)} all-to-all(bf16[1280,2,128]{0,2,1:T(8,128)(2,1)S(1)} %fusion.23), channel_id=1, replica_groups=mesh['grp'=2,'tm'=8,'apa'=2] {'apa'}, dimensions={1} | all-to-all | bytes 1310720 | tf_op jit(solution)/shard_map/all_to_all | solution.py:172
  89.8 6.1 %gather_fusion = bf16[2560,128]{1,0:T(8,128)(2,1)} fusion(bf16[2560,128]{1,0:T(8,128)(2,1)S(1)} %bitcast.60, s32[3072]{0:T(1024)S(1)} %pad_clamp_fusion), kind=kCustom, calls=%fused_computation | custom fusion | bytes 1320960 | tf_op jit(solution)/shard_map/gather | solution.py:173
  95.9 1.9 %fusion.19 = f32[1600,128]{1,0:T(8,128)S(1)} fusion(bf16[800,800]{1,0:T(8,128)(2,1)S(1)} %copy-done.4, bf16[800,800]{1,0:T(8,128)(2,1)S(1)} %get-tuple-element.34, bf16[2560,128]{1,0:T(8,128)(2,1)} %gather_fusion), kind=kOutput, calls=%fused_computation.34 | convolution fusion | flops 332800000 | bytes 3584000 | tf_op jit(solution)/shard_map/dot_general | solution.py:44
  97.8 0.9 fusion.18
  99.2 0.9 fusion.28
  100.4 0.9 fusion.29
  101.3 0.6 copy-done.1
  101.9 0.6 copy-done.2
  102.5 1.2 %fusion.2 = f32[1920,128]{1,0:T(8,128)S(1)} fusion(bf16[960,960]{1,0:T(8,128)(2,1)S(1)} %copy-done.2, bf16[960,960]{1,0:T(8,128)(2,1)S(1)} %copy-done.1, bf16[2560,128]{1,0:T(8,128)(2,1)S(1)} %copy-done.5), kind=kOutput, calls=%fused_computation.6 | convolution fusion | flops 479232000 | bytes 5160960 | tf_op jit(solution)/shard_map/dot_general | solution.py:44
  104.1 1.2 %fusion.25 = f32[960,128]{1,0:T(8,128)S(1)} fusion(bf16[960,960]{1,0:T(8,128)(2,1)S(1)} %copy-done, bf16[960,960]{1,0:T(8,128)(2,1)S(1)} %copy-done.1, bf16[960,128]{1,0:T(8,128)(2,1)S(1)} %get-tuple-element.13, bf16[960,128]{1,0:T(8,128)(2,1)S(1)} %get-tuple-element.12), kind=kOutput, calls=%fused_computation.44 | convolution fusion | flops 480337920 | bytes 4669440 | tf_op jit(solution)/shard_map/dot_general | solution.py:54
  105.3 1.1 %pad_maximum_fusion.6 = f32[2560,128]{1,0:T(8,128)} fusion(f32[960,128]{1,0:T(8,128)S(1)} %fusion.25, f32[800,128]{1,0:T(8,128)S(1)} %fusion.29, f32[800,128]{1,0:T(8,128)S(1)} %fusion.28), kind=kLoop, calls=%fused_computation.37 | loop fusion | flops 655360 | bytes 2621440 | tf_op jit(solution)/shard_map/concatenate | solution.py:90
  (60 shorter events, 4.3 us)
Async XLA Ops:
  0.0 5.2 %copy-start.6 = (s32[2560]{0:T(1024)S(1)}, s32[2560]{0:T(1024)}, u32[]{:S(2)}) copy-start(s32[2560]{0:T(1024)} %param.13) | copy-start | bytes 30724
  2.2 74.2 %collective-permute-start = (bf16[1280,128]{1,0:T(8,128)(2,1)S(1)}, bf16[1280,128]{1,0:T(8,128)(2,1)S(1)}, u32[]{:S(2)}, u32[]{:S(2)}) collective-permute-start(bf16[1280,128]{1,0:T(8,128)(2,1)S(1)} %slice.176), channel_id=1, source_target_pairs={{0,2},{2,4},{4,6},{6,8},{8,10},{10,12},{12,14},{14,0},{1,3},{3,5},... | collective-permute-start | bytes 983048 | tf_op jit(solution)/shard_map/ppermute | solution.py:16
  18.1 28.1 %copy-start.11 = (s32[2560]{0:T(1024)S(1)}, s32[2560]{0:T(1024)}, u32[]{:S(2)}) copy-start(s32[2560]{0:T(1024)} %param.14) | copy-start | bytes 30724
  18.1 28.2 %copy-start.15 = (bf16[3,64]{1,0:T(4,128)(2,1)S(1)}, bf16[3,64]{1,0:T(4,128)(2,1)}, u32[]{:S(2)}) copy-start(bf16[3,64]{1,0:T(4,128)(2,1)} %param.12) | copy-start | bytes 1156
  18.1 38.4 %copy-start.8 = (f32[2,800]{1,0:T(2,128)S(1)}, f32[2,800]{1,0:T(2,128)}, u32[]{:S(2)}) copy-start(f32[2,800]{1,0:T(2,128)} %param.16) | copy-start | bytes 19204
  18.1 38.4 %copy-start.9 = (f32[2,800]{1,0:T(2,128)S(1)}, f32[2,800]{1,0:T(2,128)}, u32[]{:S(2)}) copy-start(f32[2,800]{1,0:T(2,128)} %param.18) | copy-start | bytes 19204
  18.2 38.4 %copy-start.10 = (f32[2,800]{1,0:T(2,128)S(1)}, f32[2,800]{1,0:T(2,128)}, u32[]{:S(2)}) copy-start(f32[2,800]{1,0:T(2,128)} %param.17) | copy-start | bytes 19204
  18.2 39.0 %copy-start.12 = (f32[960]{0:T(1024)S(1)}, f32[960]{0:T(1024)}, u32[]{:S(2)}) copy-start(f32[960]{0:T(1024)} %param.21) | copy-start | bytes 11524
  18.2 39.0 %copy-start.13 = (f32[960]{0:T(1024)S(1)}, f32[960]{0:T(1024)}, u32[]{:S(2)}) copy-start(f32[960]{0:T(1024)} %param.19) | copy-start | bytes 11524
  18.2 39.0 %copy-start.14 = (f32[960]{0:T(1024)S(1)}, f32[960]{0:T(1024)}, u32[]{:S(2)}) copy-start(f32[960]{0:T(1024)} %param.20) | copy-start | bytes 11524
  89.7 6.1 %copy-start.4 = (bf16[800,800]{1,0:T(8,128)(2,1)S(1)}, bf16[800,800]{1,0:T(8,128)(2,1)}, u32[]{:S(2)}) copy-start(bf16[800,800]{1,0:T(8,128)(2,1)} %get-tuple-element.33) | copy-start | bytes 3840004
  95.9 1.9 %copy-start.5 = (bf16[2560,128]{1,0:T(8,128)(2,1)S(1)}, bf16[2560,128]{1,0:T(8,128)(2,1)}, u32[]{:S(2)}) copy-start(bf16[2560,128]{1,0:T(8,128)(2,1)} %gather_fusion) | copy-start | bytes 1966084
  97.8 0.9 copy-start.7
  97.8 1.4 %copy-start.3 = (bf16[800,800]{1,0:T(8,128)(2,1)S(1)}, bf16[800,800]{1,0:T(8,128)(2,1)}, u32[]{:S(2)}) copy-start(bf16[800,800]{1,0:T(8,128)(2,1)} %fusion.33) | copy-start | bytes 3840004
  100.4 1.5 %copy-start.1 = (bf16[960,960]{1,0:T(8,128)(2,1)S(1)}, bf16[960,960]{1,0:T(8,128)(2,1)}, u32[]{:S(2)}) copy-start(bf16[960,960]{1,0:T(8,128)(2,1)} %get-tuple-element.32) | copy-start | bytes 5529604
  100.4 2.1 %copy-start.2 = (bf16[960,960]{1,0:T(8,128)(2,1)S(1)}, bf16[960,960]{1,0:T(8,128)(2,1)}, u32[]{:S(2)}) copy-start(bf16[960,960]{1,0:T(8,128)(2,1)} %get-tuple-element.31) | copy-start | bytes 5529604
  102.5 1.5 %copy-start = (bf16[960,960]{1,0:T(8,128)(2,1)S(1)}, bf16[960,960]{1,0:T(8,128)(2,1)}, u32[]{:S(2)}) copy-start(bf16[960,960]{1,0:T(8,128)(2,1)} %fusion.32) | copy-start | bytes 5529604
where the time goes:
time: 107 us; the launch traced here: 106 us
  other arithmetic  69.1 us (65%)
  local copies, waits for them, and re-layouts  20.5 us (19%)
  matrix products  9.12 us (9%)
  blocking collectives  4.26 us (4%)
  starting transfers between devices  3.02 us (3%)
    convert_element_type x2, other arithmetic, fourier_tables(): sine_table = jnp.sin(phase_angle).astype(jnp.bfloat16)  30.1 us
    neg x2, other arithmetic, fourier_tables(): backward = jnp.concatenate([cosine, -sine_table], 1)  28 us
    scatter x1, local copies, waits for them, and re-layouts, local(): inverse = jnp.zeros((channel_count,), jnp.int32).at[wire_slot].set(jnp.ar...  10.1 us
    gather x1, local copies, waits for them, and re-layouts, local(): ordered = regrouped[inverse]  6.13 us
    select_n x6, other arithmetic, shift_rows(): current = jnp.where(chosen[:, None], moved, current)  5.58 us
    all_to_all x1, blocking collectives, local(): lax.all_to_all(filtered, 'apa', split_axis=1, concat_axis=0, tiled=True)  4.26 us
    dot_general x3, matrix products, wire_deconvolve(): spectrum = jnp.dot(forward, plane_rows, preferred_element_type=jnp.float32)  4.03 us
    ppermute x1, starting transfers between devices, shifted(): return lax.ppermute(value, axis, pairs)  3.02 us
  transfers between devices with their start and end apart: 1, of which 0 were waited for; matrix products, arithmetic and copies ran while one was open for 67% of the time, Pallas kernels for 0%

commit v1 on v0

v1 whole, which is shorter than its diff:
```python
import functools
import math

import jax
import jax.numpy as jnp
import numpy as np
from jax import lax
from jax.experimental import pallas as pl
from jax.experimental.pallas import tpu as pltpu
from jax.sharding import PartitionSpec as P

OFFSET_RANGE = 64
LANES = 128
VMEM = pltpu.VMEM
SMEM = pltpu.SMEM


def padded(count):
    return -(-count // LANES) * LANES


def wire_base(wires):
    return padded(wires)


def wire_tables(wires):
    base = wire_base(wires)
    spans = 2 * base // LANES
    m = np.arange(wires, dtype=np.int64)
    coarse = (np.arange(spans, dtype=np.int64)[:, None] * LANES - base) * m[None, :] % wires
    fine = m[:, None] * np.arange(LANES, dtype=np.int64)[None, :] % wires
    turn = 2.0 * math.pi / wires
    return (
        np.cos(coarse * turn).astype(np.float32),
        np.sin(coarse * turn).astype(np.float32),
        np.cos(fine * turn).astype(np.float32),
        np.sin(fine * turn).astype(np.float32),
    )


def lane_roll(row, rows):
    r = lax.broadcasted_iota(jnp.int32, (rows, LANES), 0)
    l = lax.broadcasted_iota(jnp.int32, (rows, LANES), 1)
    spread = jnp.broadcast_to(row, (rows, LANES))
    return jnp.take_along_axis(spread, (l - r) & (LANES - 1), axis=1, mode="promise_in_bounds")


def response_kernel(wires_by_plane, re0, im0, fl0, re1, im1, fl1, *refs):
    tables = [refs[0:4], refs[4:8]]
    outs = refs[8:11]
    r = lax.broadcasted_iota(jnp.int32, (LANES, LANES), 0)
    l = lax.broadcasted_iota(jnp.int32, (LANES, LANES), 1)
    for plane, wires in enumerate(wires_by_plane):
        ca, sa, cb, sb = tables[0 if plane < 2 else 1]
        if plane < 2:
            real, imag, gain = (ref[plane : plane + 1, :] for ref in (re0, im0, fl0))
        else:
            real, imag, gain = (ref[...] for ref in (re1, im1, fl1))
        scale = gain / (real * real + imag * imag) * (1.0 / wires)
        ratio_re = real * scale
        ratio_im = -imag * scale
        u = ca[...] * ratio_re + sa[...] * ratio_im
        v = ca[...] * ratio_im - sa[...] * ratio_re
        dot = functools.partial(
            jnp.dot, precision=lax.Precision.HIGHEST, preferred_element_type=jnp.float32
        )
        taps = dot(u, cb[...]) + dot(v, sb[...])
        out = outs[plane]
        previous = lane_roll(taps[0:1, :], LANES)
        for span in range(taps.shape[0]):
            here = lane_roll(taps[span : span + 1, :], LANES)
            out[:, span * LANES : (span + 1) * LANES] = jnp.where(l >= r, here, previous).astype(
                jnp.bfloat16
            )
            previous = here


def rotated(block, offsets):
    l = lax.broadcasted_iota(jnp.int32, block.shape, 1)
    return jnp.take_along_axis(
        block.astype(jnp.float32), (l - offsets) & (LANES - 1), axis=1, mode="promise_in_bounds"
    )


def by_plane(sums, planes):
    zero = jnp.zeros_like(planes, dtype=jnp.float32)
    picked = jnp.where(planes == 2, sums[:, 2 * LANES :], zero)
    picked = jnp.where(planes == 1, sums[:, LANES : 2 * LANES], picked)
    return jnp.where(planes == 0, sums[:, :LANES], picked)


def own_kernel(step, wave, code, taps, high_out, low_out, table_out):
    r = lax.broadcasted_iota(jnp.int32, (LANES, LANES), 0)
    l = lax.broadcasted_iota(jnp.int32, (LANES, LANES), 1)
    for plane in range(3):
        rolled = lane_roll(taps[plane : plane + 1, :], LANES)
        cols = slice(plane * LANES, (plane + 1) * LANES)
        table_out[:LANES, cols] = jnp.where(l < r, rolled, 0.0).astype(jnp.bfloat16)
        table_out[LANES:, cols] = jnp.where(l >= r, rolled, 0.0).astype(jnp.bfloat16)

    def body(i, carry):
        rows = pl.ds(pl.multiple_of(i * step, step), step)
        word = code[rows, :]
        offsets = word & (OFFSET_RANGE - 1)
        planes = word // OFFSET_RANGE
        lane = lax.broadcasted_iota(jnp.int32, word.shape, 1)
        early = rotated(wave[rows, :LANES], offsets)
        late = rotated(wave[rows, LANES:], offsets)
        wrapped = lane < offsets
        low = jnp.where(wrapped, 0.0, early).astype(jnp.bfloat16)
        both = jnp.concatenate([early, jnp.where(wrapped, early, late)], 1).astype(jnp.bfloat16)
        table = table_out[...]
        low_sum = jnp.dot(low, table[LANES:, :], preferred_element_type=jnp.float32)
        high_sum = jnp.dot(both, table, preferred_element_type=jnp.float32)
        low_out[rows, :] = by_plane(low_sum, planes)
        high_out[rows, :] = by_plane(high_sum, planes).astype(jnp.bfloat16)
        return carry

    lax.fori_loop(0, wave.shape[0] // step, body, 0)


def halo_kernel(step, side, halo, code, table_ref, low_main, high, own_out, other_out):
    def body(i, carry):
        rows = pl.ds(pl.multiple_of(i * step, step), step)
        word = code[rows, :]
        offsets = word & (OFFSET_RANGE - 1)
        planes = word // OFFSET_RANGE
        lane = lax.broadcasted_iota(jnp.int32, word.shape, 1)
        early = rotated(halo[rows, :], offsets)
        both = jnp.concatenate([early, jnp.where(lane < offsets, early, 0.0)], 1).astype(
            jnp.bfloat16
        )
        sums = jnp.dot(both, table_ref[...], preferred_element_type=jnp.float32)
        low = low_main[rows, :] + by_plane(sums, planes)
        upper = high[rows, :].astype(jnp.float32)
        first = side[0] == 0
        own_out[rows, :] = jnp.where(first, low, upper).astype(jnp.bfloat16)
        other_out[rows, :] = jnp.where(first, upper, low).astype(jnp.bfloat16)
        return carry

    lax.fori_loop(0, halo.shape[0] // step, body, 0)


def place_rows(source, slots, first_row, target, unroll):
    count = source.shape[0]

    def body(i, carry):
        start = i * unroll
        for k in range(unroll):
            slot = slots[first_row + start + k]
            target[pl.ds(slot, 1), :] = source[pl.ds(start + k, 1), :]
        return carry

    lax.fori_loop(0, count // unroll, body, 0)


def place_kernel(gaps, side, slots, own, ordered, wide):
    wide[...] = own[...].astype(jnp.float32)
    for start, stop in gaps:
        ordered[start:stop, :] = jnp.zeros((stop - start, LANES), jnp.float32)
    place_rows(wide, slots, side[0] * own.shape[0], ordered, 16)


def final_kernel(layout, side, slots, other, half_placed, resp0, resp1, resp2, out, ordered, wide):
    count = other.shape[0]
    wide[...] = other[...].astype(jnp.float32)
    ordered[...] = half_placed[...]
    place_rows(wide, slots, (1 - side[0]) * count, ordered, 16)
    for (start, wires, row), resp in zip(layout, (resp0, resp1, resp2)):
        depth = padded(wires)
        base = wire_base(wires)
        data = ordered[start : start + depth, :].astype(jnp.bfloat16)
        for block in range(depth // LANES):
            valid = min(LANES, wires - block * LANES)
            left = base - block * LANES
            result = jnp.dot(
                resp[:, left : left + depth], data, preferred_element_type=jnp.float32
            )
            out[row + block * LANES : row + block * LANES + valid, :] = result[:valid, :]


def local(
    waveforms,
    time_kernel,
    wire_slot,
    tick_offset,
    bad_channel,
    induction_real,
    induction_imaginary,
    induction_filter,
    collection_real,
    collection_imaginary,
    collection_filter,
):
    induction = induction_real.shape[1]
    collection = collection_real.shape[0]
    wires_by_plane = (induction, induction, collection)
    taps = time_kernel.shape[1]
    rows, ticks = waveforms.shape
    channels = wire_slot.shape[0]
    assert ticks == 2 * LANES and taps + OFFSET_RANGE == LANES
    assert channels == 2 * rows and channels == 2 * induction + collection

    ring = lax.axis_size("tm")
    halo = lax.ppermute(
        waveforms[:, ticks - LANES :], "tm", [(i, (i + 1) % ring) for i in range(ring)]
    )

    side = lax.axis_index("apa")
    side_word = side.reshape(1).astype(jnp.int32)
    plane = (wire_slot >= induction).astype(jnp.int32) + (wire_slot >= 2 * induction).astype(
        jnp.int32
    )
    code = tick_offset + OFFSET_RANGE * jnp.where(bad_channel == 0, plane, 3)
    code = lax.dynamic_slice_in_dim(code, side * rows, rows)
    code = jnp.broadcast_to(code[:, None], (rows, LANES))
    gap = padded(induction) - induction
    spread_slot = wire_slot + gap * plane
    padded_taps = jnp.pad(time_kernel.astype(jnp.float32), ((0, 0), (0, LANES - taps)))

    bases = [wire_base(w) for w in wires_by_plane]
    vm = pl.BlockSpec(memory_space=VMEM)
    sm = pl.BlockSpec(memory_space=SMEM)

    tables = [jnp.asarray(t) for w in (induction, collection) for t in wire_tables(w)]
    responses = pl.pallas_call(
        functools.partial(response_kernel, wires_by_plane),
        out_shape=[jax.ShapeDtypeStruct((LANES, 2 * b), jnp.bfloat16) for b in bases],
        in_specs=[vm] * 14,
        out_specs=[vm] * 3,
        cost_estimate=pl.CostEstimate(flops=2 * 10**8, bytes_accessed=4 * 10**6, transcendentals=0),
        name="response",
    )(
        induction_real,
        induction_imaginary,
        induction_filter,
        collection_real[None],
        collection_imaginary[None],
        collection_filter[None],
        *tables,
    )

    step = 256
    high, low_main, table = pl.pallas_call(
        functools.partial(own_kernel, step),
        out_shape=[
            jax.ShapeDtypeStruct((rows, LANES), jnp.bfloat16),
            jax.ShapeDtypeStruct((rows, LANES), jnp.float32),
            jax.ShapeDtypeStruct((2 * LANES, 3 * LANES), jnp.bfloat16),
        ],
        in_specs=[vm] * 3,
        out_specs=[vm] * 3,
        cost_estimate=pl.CostEstimate(flops=10**9, bytes_accessed=3 * 10**6, transcendentals=0),
        name="own_window",
    )(waveforms, code, padded_taps)

    own, other = pl.pallas_call(
        functools.partial(halo_kernel, step),
        out_shape=[jax.ShapeDtypeStruct((rows, LANES), jnp.bfloat16)] * 2,
        in_specs=[sm] + [vm] * 5,
        out_specs=[vm] * 2,
        name="halo_window",
    )(side_word, halo, code, table, low_main, high)

    received = lax.ppermute(other, "apa", [(0, 1), (1, 0)])

    layout = []
    start = row = 0
    gaps = []
    for wires in wires_by_plane:
        layout.append((start, wires, row))
        gaps.append((start + wires, start + padded(wires)))
        start += padded(wires)
        row += wires

    half_placed = pl.pallas_call(
        functools.partial(place_kernel, gaps),
        out_shape=jax.ShapeDtypeStruct((start, LANES), jnp.float32),
        in_specs=[sm, sm, vm],
        out_specs=vm,
        scratch_shapes=[pltpu.VMEM((rows, LANES), jnp.float32)],
        cost_estimate=pl.CostEstimate(flops=10**6, bytes_accessed=3 * 10**6, transcendentals=0),
        name="place_own",
    )(side_word, spread_slot, own)

    return pl.pallas_call(
        functools.partial(final_kernel, layout),
        out_shape=jax.ShapeDtypeStruct((channels, LANES), jnp.float32),
        in_specs=[sm, sm] + [vm] * 5,
        out_specs=vm,
        scratch_shapes=[
            pltpu.VMEM((start, LANES), jnp.float32),
            pltpu.VMEM((rows, LANES), jnp.float32),
        ],
        name="place_and_mix",
    )(side_word, spread_slot, received, half_placed, *responses)


def solution(mesh):
    placed = (P(("grp", "apa"), "tm"), P(), P("grp"), P("grp"), P("grp")) + (P(),) * 6
    return jax.shard_map(
        local, mesh=mesh, in_specs=placed, out_specs=P("grp", ("tm", "apa")), check_vma=False
    )
```

time: 107 us -> 34.4 us (0.32)
  other arithmetic: 69.1 us -> 3.38 us
  Pallas kernels: 0 us -> 22 us
  local copies, waits for them, and re-layouts: 20.5 us -> 3.53 us
  matrix products: 9.12 us -> 0 us
  blocking collectives: 4.26 us -> 0 us
  waiting for transfers between devices: 0.01 us -> 1.99 us
    convert_element_type x4 -> x0, other arithmetic: 31.2 us -> none  [the longest x2 30.1 us: fourier_tables(): sine_table = jnp.sin(phase_angle).astype(jnp.bfloat16)]
    neg x2 -> x0, other arithmetic: 28 us -> none  [fourier_tables(): backward = jnp.concatenate([cosine, -sine_table], 1)]
    pallas_call x0 -> x5, Pallas kernels: none -> 22 us  [the longest x1 5.96 us: local(): pl.pallas_call(functools.partial(final_kernel, layout), out_shape=jax.Sha...]
    scatter x1 -> x0, local copies, waits for them, and re-layouts: 10.1 us -> none  [local(): inverse = jnp.zeros((channel_count,), jnp.int32).at[wire_slot].set(jnp.ar...]
    dot_general x12 -> x0, matrix products: 9.12 us -> none  [the longest x3 4.03 us: wire_deconvolve(): spectrum = jnp.dot(forward, plane_rows, preferred_element_type=jnp.float32)]
    gather x1 -> x0, local copies, waits for them, and re-layouts: 6.13 us -> none  [local(): ordered = regrouped[inverse]]
    select_n x8 -> x0, other arithmetic: 5.59 us -> none  [the longest x6 5.58 us: shift_rows(): current = jnp.where(chosen[:, None], moved, current)]
    all_to_all x1 -> x0, blocking collectives: 4.26 us -> none  [local(): lax.all_to_all(filtered, 'apa', split_axis=1, concat_axis=0, tiled=True)]
  transfers between devices with their start and end apart: 1 -> 2, of which waited for: 0 -> 1; matrix products, arithmetic and copies ran while one was open for 67% -> 13% of each run, Pallas kernels for 0% -> 36%
where the time goes in v1:
time: 34.4 us; the launch traced here: 33.9 us
  Pallas kernels  22 us (64%)
  local copies, waits for them, and re-layouts  3.53 us (10%)
  other arithmetic  3.38 us (10%)
  starting transfers between devices  3.02 us (9%)
  waiting for transfers between devices  1.99 us (6%)
    pallas_call x1, Pallas kernels, local(): pl.pallas_call(functools.partial(final_kernel, layout), out_shape=jax.Sha...  5.96 us
    pallas_call x1, Pallas kernels, local(): pl.pallas_call(functools.partial(own_kernel, step), out_shape=[jax.ShapeD...  4.3 us
    pallas_call x1, Pallas kernels, local(): pl.pallas_call(functools.partial(response_kernel, wires_by_plane), out_sh...  4.3 us
    pallas_call x1, Pallas kernels, local(): pl.pallas_call(functools.partial(halo_kernel, step), out_shape=[jax.Shape...  3.86 us
    pallas_call x1, Pallas kernels, local(): pl.pallas_call(functools.partial(place_kernel, gaps), out_shape=jax.Shape...  3.53 us
    ppermute x1, starting transfers between devices, local(): lax.ppermute(waveforms[:, ticks - LANES:], 'tm', [(i, (i + 1) % ring) for...  3.02 us
    ppermute x1, waiting for transfers between devices, local(): lax.ppermute(waveforms[:, ticks - LANES:], 'tm', [(i, (i + 1) % ring) for...  1.99 us
    unnamed x4, local copies, waits for them, and re-layouts  1.46 us
  transfers between devices with their start and end apart: 2, of which 1 were waited for; matrix products, arithmetic and copies ran while one was open for 13% of the time, Pallas kernels for 36%

profile of v1, /device:TPU:0, one launch (start us, length us, event | category | flops | bytes accessed | tf_op | source)
XLA Modules:
  0.0 33.9 jit_solution(16633915796891010893)
XLA Ops:
  0.0 1.0 %slice.3 = bf16[1280,128]{1,0:T(8,128)(2,1)S(1)} slice(bf16[1280,256]{1,0:T(8,128)(2,1)} %wave.1), slice={[0:1280], [128:256]} | slice | bytes 655360 | tf_op jit(solution)/shard_map/slice | solution.py:206
  1.0 3.0 %collective-permute-start = (bf16[1280,128]{1,0:T(8,128)(2,1)S(1)}, bf16[1280,128]{1,0:T(8,128)(2,1)S(1)}, u32[]{:S(2)}, u32[]{:S(2)}) collective-permute-start(bf16[1280,128]{1,0:T(8,128)(2,1)S(1)} %slice.3), channel_id=1, source_target_pairs={{0,2},{2,4},{4,6},{6,8},{8,10},{10,12},{12,14},{14,0},{1,3},{3,5},... | collective-permute-start | bytes 983048 | tf_op jit(solution)/shard_map/ppermute | solution.py:205
  4.0 1.3 %convert_add_fusion = (s32[2560]{0:T(1024)S(1)}, s32[2560]{0:T(1024)}) fusion(s32[2560]{0:T(1024)} %param.21), kind=kLoop, calls=%fused_computation.1 | loop fusion | flops 17920 | bytes 30720 | tf_op jit(solution)/shard_map/add | solution.py:211
  5.3 1.3 %pad_convert_fusion.taps = f32[3,128]{1,0:T(4,128)} fusion(bf16[3,64]{1,0:T(4,128)(2,1)} %param.20), kind=kLoop, calls=%fused_computation.6 | loop fusion | flops 384 | bytes 1920 | tf_op jit(solution)/shard_map/jit(_pad)/pad | solution.py:219
  6.6 0.8 %dynamic-slice_add_fusion = s32[1280]{0:T(1024)S(1)} fusion(s32[2560]{0:T(1024)} %param.22, s32[]{:T(128)S(6)} %select_n.8, s32[2560]{0:T(1024)S(1)} %get-tuple-element.21, s32[2560]{0:T(1024)} %param.23), kind=kLoop, calls=%fused_computation.2 | loop fusion | flops 5120 | bytes 20484 | tf_op jit(solution)/shard_map/add | solution.py:214
  7.4 1.1 %broadcast_in_dim.20.code = s32[1280,128]{1,0:T(8,128)} broadcast(s32[1280]{0:T(1024)S(1)} %dynamic-slice_add_fusion), dimensions={0} | broadcast | bytes 660480 | tf_op jit(solution)/shard_map/broadcast_in_dim | solution.py:216
  8.5 4.3 %own_window.1 = (bf16[1280,128]{1,0:T(8,128)(2,1)}, f32[1280,128]{1,0:T(8,128)}, bf16[256,384]{1,0:T(8,128)(2,1)}) custom-call(bf16[1280,256]{1,0:T(8,128)(2,1)} %wave.1, s32[1280,128]{1,0:T(8,128)} %broadcast_in_dim.20.code, f32[3,128]{1,0:T(4,128)} %pad_convert_fusion.taps), custom_call_target="tpu_custom_call" | custom-call | flops 1000000000 | bytes 3000000 | tf_op jit(solution)/shard_map/own_window/pallas_call | solution.py:244
  12.8 2.0 %collective-permute-done.halo = bf16[1280,128]{1,0:T(8,128)(2,1)S(1)} collective-permute-done((bf16[1280,128]{1,0:T(8,128)(2,1)S(1)}, bf16[1280,128]{1,0:T(8,128)(2,1)S(1)}, u32[]{:S(2)}, u32[]{:S(2)}) %collective-permute-start) | collective-permute-done | bytes 327712 | tf_op jit(solution)/shard_map/ppermute | solution.py:205
  14.8 0.0 copy-start
  14.8 0.7 %copy-done = bf16[1280,128]{1,0:T(8,128)(2,1)} copy-done((bf16[1280,128]{1,0:T(8,128)(2,1)}, bf16[1280,128]{1,0:T(8,128)(2,1)S(1)}, u32[]{:S(2)}) %copy-start) | copy-done | bytes 327704
  15.5 3.9 %halo_window.1 = (bf16[1280,128]{1,0:T(8,128)(2,1)}, bf16[1280,128]{1,0:T(8,128)(2,1)}) custom-call(s32[1]{0:T(128)} %bitcast.side, bf16[1280,128]{1,0:T(8,128)(2,1)} %copy-done, s32[1280,128]{1,0:T(8,128)} %broadcast_in_dim.20.code, bf16[256,384]{1,0:T(8,128)(2,1)} %get-tuple-element.13.table_ref, f32[1280,128]{1,0:T(8,128)} %get-tuple-element.14.low_main, ...), custom_call_target="tpu_custom_call" | custom-call | tf_op jit(solution)/shard_map/halo_window/pallas_call | solution.py:257
  19.3 0.0 collective-permute-start.1
  19.4 4.3 %response.1 = (bf16[128,1792]{1,0:T(8,128)(2,1)}, bf16[128,1792]{1,0:T(8,128)(2,1)}, bf16[128,2048]{1,0:T(8,128)(2,1)}) custom-call(f32[2,800]{1,0:T(2,128)} %re0.1, f32[2,800]{1,0:T(2,128)} %im0.1, f32[2,800]{1,0:T(2,128)} %fl0.1, f32[1,960]{1,0:T(1,128)} %bitcast.4, f32[1,960]{1,0:T(1,128)} %bitcast.5, f32[1,960]{1,0:T(1,128)} %bitcast.6, ...), custom_call_target="tpu_custom_call" | custom-call | flops 200000000 | bytes 4000000 | tf_op jit(solution)/shard_map/response/pallas_call | solution.py:226
  23.6 3.5 %place_own.1.half_placed = f32[2816,128]{1,0:T(8,128)} custom-call(s32[1]{0:T(128)} %bitcast.side, s32[2560]{0:T(1024)} %get-tuple-element.22.slots, bf16[1280,128]{1,0:T(8,128)(2,1)} %get-tuple-element.17.own), custom_call_target="tpu_custom_call" | custom-call | flops 1000000 | bytes 3000000 | tf_op jit(solution)/shard_map/place_own/pallas_call | solution.py:276
  27.2 0.0 collective-permute-done.1.other
  27.2 0.0 copy-start.1
  27.2 0.7 %copy-done.1 = bf16[1280,128]{1,0:T(8,128)(2,1)} copy-done((bf16[1280,128]{1,0:T(8,128)(2,1)}, bf16[1280,128]{1,0:T(8,128)(2,1)S(1)}, u32[]{:S(2)}) %copy-start.1) | copy-done | bytes 327704
  27.9 6.0 %place_and_mix.1 = f32[2560,128]{1,0:T(8,128)} custom-call(s32[1]{0:T(128)} %bitcast.side, s32[2560]{0:T(1024)} %get-tuple-element.22.slots, bf16[1280,128]{1,0:T(8,128)(2,1)} %copy-done.1, f32[2816,128]{1,0:T(8,128)} %place_own.1.half_placed, bf16[128,1792]{1,0:T(8,128)(2,1)} %get-tuple-element.18.resp0, bf16[128,1792]{1,0:T(8,128)(2,1)} %get-tuple-element.19.resp1, ...), custom_call_target="tpu_custom_call" | custom-call | tf_op jit(solution)/shard_map/place_and_mix/pallas_call | solution.py:286
Async XLA Ops:
  1.0 13.8 %collective-permute-start = (bf16[1280,128]{1,0:T(8,128)(2,1)S(1)}, bf16[1280,128]{1,0:T(8,128)(2,1)S(1)}, u32[]{:S(2)}, u32[]{:S(2)}) collective-permute-start(bf16[1280,128]{1,0:T(8,128)(2,1)S(1)} %slice.3), channel_id=1, source_target_pairs={{0,2},{2,4},{4,6},{6,8},{8,10},{10,12},{12,14},{14,0},{1,3},{3,5},... | collective-permute-start | bytes 983048 | tf_op jit(solution)/shard_map/ppermute | solution.py:205
  14.8 0.7 %copy-start = (bf16[1280,128]{1,0:T(8,128)(2,1)}, bf16[1280,128]{1,0:T(8,128)(2,1)S(1)}, u32[]{:S(2)}) copy-start(bf16[1280,128]{1,0:T(8,128)(2,1)S(1)} %collective-permute-done.halo) | copy-start | bytes 983044
  19.3 7.8 %collective-permute-start.1 = (bf16[1280,128]{1,0:T(8,128)(2,1)}, bf16[1280,128]{1,0:T(8,128)(2,1)S(1)}, u32[]{:S(2)}, u32[]{:S(2)}) collective-permute-start(bf16[1280,128]{1,0:T(8,128)(2,1)} %get-tuple-element.16), channel_id=1, source_target_pairs={{0,1},{1,0},{2,3},{3,2},{4,5},{5,4},{6,7},{7,6},{8,9},{9,8},{10,11... | collective-permute-start | bytes 983048 | tf_op jit(solution)/shard_map/ppermute | solution.py:265
  27.2 0.7 %copy-start.1 = (bf16[1280,128]{1,0:T(8,128)(2,1)}, bf16[1280,128]{1,0:T(8,128)(2,1)S(1)}, u32[]{:S(2)}) copy-start(bf16[1280,128]{1,0:T(8,128)(2,1)S(1)} %collective-permute-done.1.other) | copy-start | bytes 983044

commit v2 on v1

v2 whole, which is shorter than its diff:
```python
import functools
import math

import jax
import jax.numpy as jnp
import numpy as np
from jax import lax
from jax.experimental import pallas as pl
from jax.experimental.pallas import tpu as pltpu
from jax.sharding import PartitionSpec as P

OFFSET_RANGE = 64
LANES = 128
VMEM = pltpu.VMEM
SMEM = pltpu.SMEM
KERNEL_VMEM = 16 * 2**20
STEP = 256
UNROLL = 32
COARSE_ROWS = 16


def padded(count):
    return -(-count // LANES) * LANES


def wire_tables(wires_by_plane):
    widest = max(wires_by_plane)
    coarse_rows, fine_rows = [], []
    for wires in wires_by_plane[1:]:
        base = padded(wires)
        m = np.arange(wires, dtype=np.int64)
        step = np.arange(2 * base // LANES, dtype=np.int64)[:, None] * LANES - base
        turn = 2.0 * math.pi / wires
        coarse = step * m[None, :] % wires * turn
        fine = m[:, None] * np.arange(LANES, dtype=np.int64)[None, :] % wires * turn
        for table in (np.cos(coarse), np.sin(coarse)):
            full = np.zeros((COARSE_ROWS, widest), np.float32)
            full[: table.shape[0], :wires] = table
            coarse_rows.append(full)
        fine_rows.append(np.concatenate([np.cos(fine), np.sin(fine)], 1).astype(np.float32))
    return np.concatenate(coarse_rows, 0), np.concatenate(fine_rows, 0)


def lane_roll(row, rows):
    r = lax.broadcasted_iota(jnp.int32, (rows, LANES), 0)
    l = lax.broadcasted_iota(jnp.int32, (rows, LANES), 1)
    spread = jnp.broadcast_to(row, (rows, LANES))
    return jnp.take_along_axis(spread, (l - r) & (LANES - 1), axis=1, mode="promise_in_bounds")


def make_responses(wires_by_plane, induction, collection, coarse, fine, outs):
    r = lax.broadcasted_iota(jnp.int32, (LANES, LANES), 0)
    l = lax.broadcasted_iota(jnp.int32, (LANES, LANES), 1)
    dot = functools.partial(
        jnp.dot, precision=lax.Precision.HIGHEST, preferred_element_type=jnp.float32
    )
    for plane, wires in enumerate(wires_by_plane):
        first = 0 if plane < 2 else 2 * COARSE_ROWS
        ca = coarse[first : first + COARSE_ROWS, :wires]
        sa = coarse[first + COARSE_ROWS : first + 2 * COARSE_ROWS, :wires]
        first = 0 if plane < 2 else wires_by_plane[0]
        cb = fine[first : first + wires, :LANES]
        sb = fine[first : first + wires, LANES:]
        if plane < 2:
            real, imag, gain = (ref[plane : plane + 1, :] for ref in induction)
        else:
            real, imag, gain = (ref[...] for ref in collection)
        scale = gain / (real * real + imag * imag) * (1.0 / wires)
        ratio_re = real * scale
        ratio_im = -imag * scale
        u = ca * ratio_re + sa * ratio_im
        v = ca * ratio_im - sa * ratio_re
        taps = dot(u, cb) + dot(v, sb)
        out = outs[plane]
        previous = lane_roll(taps[0:1, :], LANES)
        for span in range(out.shape[1] // LANES):
            here = lane_roll(taps[span : span + 1, :], LANES)
            out[:, span * LANES : (span + 1) * LANES] = jnp.where(l >= r, here, previous).astype(
                jnp.bfloat16
            )
            previous = here


def rotated(block, offsets):
    l = lax.broadcasted_iota(jnp.int32, block.shape, 1)
    return jnp.take_along_axis(
        block.astype(jnp.float32), (l - offsets) & (LANES - 1), axis=1, mode="promise_in_bounds"
    )


def by_plane(sums, planes):
    zero = jnp.zeros_like(planes, dtype=jnp.float32)
    picked = jnp.where(planes == 2, sums[:, 2 * LANES :], zero)
    picked = jnp.where(planes == 1, sums[:, LANES : 2 * LANES], picked)
    return jnp.where(planes == 0, sums[:, :LANES], picked)


def cut_kernel(wave, tail, sem):
    copy = pltpu.make_async_copy(wave.at[:, LANES:], tail, sem)
    copy.start()
    copy.wait()


def window_kernel(wires_by_plane, step, side, *refs):
    count = 13
    sources, refs = refs[:count], refs[count:]
    high_out, low_out, table_out, code_out = refs[:4]
    responses = refs[4:7]
    held, refs = refs[7 : 7 + count], refs[7 + count :]
    words, wide_taps, sems = refs
    copies = [
        pltpu.make_async_copy(source, target, sems.at[i])
        for i, (source, target) in enumerate(zip(sources, held))
    ]
    for copy in copies:
        copy.start()
    slots, offset_rows, bad_rows, kernel_taps, wave = held[:5]
    induction, collection = held[5:8], held[8:11]
    coarse, fine = held[11:13]
    for copy in copies[:5]:
        copy.wait()
    r = lax.broadcasted_iota(jnp.int32, (LANES, LANES), 0)
    l = lax.broadcasted_iota(jnp.int32, (LANES, LANES), 1)

    wide_taps[...] = jnp.zeros_like(wide_taps)
    wide_taps[0:3, 0 : kernel_taps.shape[1]] = kernel_taps[...].astype(jnp.float32)
    for plane in range(3):
        rolled = lane_roll(wide_taps[plane : plane + 1, :], LANES)
        cols = slice(plane * LANES, (plane + 1) * LANES)
        table_out[:LANES, cols] = jnp.where(l < r, rolled, 0.0).astype(jnp.bfloat16)
        table_out[LANES:, cols] = jnp.where(l >= r, rolled, 0.0).astype(jnp.bfloat16)

    slot = slots[...]
    one, two = wires_by_plane[0], wires_by_plane[0] + wires_by_plane[1]
    planes = (slot >= one).astype(jnp.int32) + (slot >= two).astype(jnp.int32)
    planes = jnp.where(bad_rows[...] == 0, planes, 3)
    words[...] = offset_rows[...] + OFFSET_RANGE * planes

    groups = wave.shape[0] // LANES
    first_group = side[0] * groups

    def spread(i, carry):
        row = jnp.broadcast_to(words[pl.ds(first_group + i, 1), :], (LANES, LANES))
        code_out[pl.ds(pl.multiple_of(i * LANES, LANES), LANES), :] = row.T
        return carry

    lax.fori_loop(0, groups, spread, 0)

    def body(i, carry):
        rows = pl.ds(pl.multiple_of(i * step, step), step)
        word = code_out[rows, :]
        offsets = word & (OFFSET_RANGE - 1)
        plane = word // OFFSET_RANGE
        lane = lax.broadcasted_iota(jnp.int32, word.shape, 1)
        early = rotated(wave[rows, :LANES], offsets)
        late = rotated(wave[rows, LANES:], offsets)
        wrapped = lane < offsets
        low = jnp.where(wrapped, 0.0, early).astype(jnp.bfloat16)
        both = jnp.concatenate([early, jnp.where(wrapped, early, late)], 1).astype(jnp.bfloat16)
        table = table_out[...]
        low_sum = jnp.dot(low, table[LANES:, :], preferred_element_type=jnp.float32)
        high_sum = jnp.dot(both, table, preferred_element_type=jnp.float32)
        low_out[rows, :] = by_plane(low_sum, plane)
        high_out[rows, :] = by_plane(high_sum, plane).astype(jnp.bfloat16)
        return carry

    lax.fori_loop(0, wave.shape[0] // step, body, 0)
    for copy in copies[5:]:
        copy.wait()
    make_responses(wires_by_plane, induction, collection, coarse, fine, responses)


def halo_kernel(step, side, halo, code, table_ref, low_main, high, own_out, other_out):
    def body(i, carry):
        rows = pl.ds(pl.multiple_of(i * step, step), step)
        word = code[rows, :]
        offsets = word & (OFFSET_RANGE - 1)
        planes = word // OFFSET_RANGE
        lane = lax.broadcasted_iota(jnp.int32, word.shape, 1)
        early = rotated(halo[rows, :], offsets)
        both = jnp.concatenate([early, jnp.where(lane < offsets, early, 0.0)], 1).astype(
            jnp.bfloat16
        )
        sums = jnp.dot(both, table_ref[...], preferred_element_type=jnp.float32)
        low = low_main[rows, :] + by_plane(sums, planes)
        upper = high[rows, :].astype(jnp.float32)
        first = side[0] == 0
        own_out[rows, :] = jnp.where(first, low, upper).astype(jnp.bfloat16)
        other_out[rows, :] = jnp.where(first, upper, low).astype(jnp.bfloat16)
        return carry

    lax.fori_loop(0, halo.shape[0] // step, body, 0)


def place_rows(source, slots, first_row, target, unroll):
    count = source.shape[0]

    def body(i, carry):
        start = pl.multiple_of(i * unroll, unroll)
        near = slots.at[pl.ds(first_row + start, unroll)]
        for k in range(unroll):
            target[pl.ds(near[k], 1), :] = source[pl.ds(start + k, 1), :]
        return carry

    lax.fori_loop(0, count // unroll, body, 0)


def place_kernel(side, slots, own, ordered, wide):
    wide[...] = own[...].astype(jnp.float32)
    place_rows(wide, slots, side[0] * own.shape[0], ordered, UNROLL)


def final_kernel(layout, side, slots, other, half_placed, *refs):
    responses, out, wide, ordered, mixed, sems = refs[:3], *refs[3:]
    count = other.shape[0]
    wide[...] = other[...].astype(jnp.float32)
    ordered[...] = half_placed[...]
    place_rows(wide, slots, (1 - side[0]) * count, ordered, UNROLL)
    copies = []
    for plane, ((start, wires), resp) in enumerate(zip(layout, responses)):
        base = padded(wires)
        data = ordered[start : start + wires, :].astype(jnp.bfloat16)
        for block in range(base // LANES):
            valid = min(LANES, wires - block * LANES)
            left = base - block * LANES
            result = jnp.dot(
                resp[:, left : left + wires], data, preferred_element_type=jnp.float32
            )
            top = start + block * LANES
            mixed[top : top + valid, :] = result[:valid, :]
        span = pl.ds(start, wires)
        copies.append(pltpu.make_async_copy(mixed.at[span], out.at[span], sems.at[plane]))
        copies[-1].start()
    for copy in copies:
        copy.wait()


def local(
    waveforms,
    time_kernel,
    wire_slot,
    tick_offset,
    bad_channel,
    induction_real,
    induction_imaginary,
    induction_filter,
    collection_real,
    collection_imaginary,
    collection_filter,
):
    induction = induction_real.shape[1]
    collection = collection_real.shape[0]
    wires_by_plane = (induction, induction, collection)
    taps = time_kernel.shape[1]
    rows, ticks = waveforms.shape
    channels = wire_slot.shape[0]
    assert ticks == 2 * LANES and taps + OFFSET_RANGE == LANES
    assert channels == 2 * rows and channels == 2 * induction + collection

    ring = lax.axis_size("tm")
    hbm = pl.BlockSpec(memory_space=pltpu.HBM)
    keep = functools.partial(pltpu.with_memory_space_constraint, memory_space=pltpu.HBM)
    params = pltpu.CompilerParams(vmem_limit_bytes=KERNEL_VMEM)
    tail = pl.pallas_call(
        cut_kernel,
        out_shape=jax.ShapeDtypeStruct((rows, LANES), jnp.bfloat16),
        in_specs=[hbm],
        out_specs=pl.BlockSpec(memory_space=VMEM),
        scratch_shapes=[pltpu.SemaphoreType.DMA],
        compiler_params=params,
        name="cut_tail",
    )(keep(waveforms))
    halo = lax.ppermute(tail, "tm", [(i, (i + 1) % ring) for i in range(ring)])

    side = lax.axis_index("apa")
    side_word = side.reshape(1).astype(jnp.int32)
    vm = pl.BlockSpec(memory_space=VMEM)
    sm = pl.BlockSpec(memory_space=SMEM)
    shape = jax.ShapeDtypeStruct

    def by_lanes(vector):
        return vector.reshape(channels // LANES, LANES)

    inputs = [
        by_lanes(wire_slot),
        by_lanes(tick_offset),
        by_lanes(bad_channel),
        time_kernel,
        waveforms,
        induction_real,
        induction_imaginary,
        induction_filter,
        collection_real[None],
        collection_imaginary[None],
        collection_filter[None],
        *(jnp.asarray(t) for t in wire_tables(wires_by_plane)),
    ]
    window = pl.pallas_call(
        functools.partial(window_kernel, wires_by_plane, STEP),
        out_shape=[
            shape((rows, LANES), jnp.bfloat16),
            shape((rows, LANES), jnp.float32),
            shape((2 * LANES, 3 * LANES), jnp.bfloat16),
            shape((rows, LANES), jnp.int32),
        ]
        + [shape((LANES, 2 * padded(w)), jnp.bfloat16) for w in wires_by_plane],
        in_specs=[sm] + [hbm] * len(inputs),
        out_specs=[vm] * 7,
        scratch_shapes=[pltpu.VMEM(x.shape, x.dtype) for x in inputs]
        + [
            pltpu.VMEM((channels // LANES, LANES), jnp.int32),
            pltpu.VMEM((8, LANES), jnp.float32),
            pltpu.SemaphoreType.DMA((len(inputs),)),
        ],
        compiler_params=params,
        cost_estimate=pl.CostEstimate(flops=10**9, bytes_accessed=8 * 10**6, transcendentals=0),
        name="own_window",
    )(side_word, *map(keep, inputs))
    high, low_main, table, code = window[:4]
    responses = window[4:]

    own, other = pl.pallas_call(
        functools.partial(halo_kernel, STEP),
        out_shape=[shape((rows, LANES), jnp.bfloat16)] * 2,
        in_specs=[sm] + [vm] * 5,
        out_specs=[vm] * 2,
        compiler_params=params,
        cost_estimate=pl.CostEstimate(flops=10**8, bytes_accessed=2 * 10**6, transcendentals=0),
        name="halo_window",
    )(side_word, halo, code, table, low_main, high)

    received = lax.ppermute(other, "apa", [(0, 1), (1, 0)])

    half_placed = pl.pallas_call(
        place_kernel,
        out_shape=shape((channels, LANES), jnp.float32),
        in_specs=[sm, sm, vm],
        out_specs=vm,
        scratch_shapes=[pltpu.VMEM((rows, LANES), jnp.float32)],
        compiler_params=params,
        cost_estimate=pl.CostEstimate(flops=10**6, bytes_accessed=3 * 10**6, transcendentals=0),
        name="place_own",
    )(side_word, wire_slot, own)

    layout = []
    start = 0
    for wires in wires_by_plane:
        layout.append((start, wires))
        start += wires
    return pl.pallas_call(
        functools.partial(final_kernel, layout),
        out_shape=shape((channels, LANES), jnp.float32),
        in_specs=[sm, sm] + [vm] * 5,
        out_specs=pl.BlockSpec(memory_space=pl.ANY),
        scratch_shapes=[
            pltpu.VMEM((rows, LANES), jnp.float32),
            pltpu.VMEM((channels, LANES), jnp.float32),
            pltpu.VMEM((channels, LANES), jnp.float32),
            pltpu.SemaphoreType.DMA((3,)),
        ],
        compiler_params=params,
        name="place_and_mix",
    )(side_word, wire_slot, received, half_placed, *responses)


def solution(mesh):
    placed = (P(("grp", "apa"), "tm"), P(), P("grp"), P("grp"), P("grp")) + (P(),) * 6
    return jax.shard_map(
        local, mesh=mesh, in_specs=placed, out_specs=P("grp", ("tm", "apa")), check_vma=False
    )
```

time: 34.4 us -> 23 us (0.67)
  Pallas kernels: 22 us -> 15.1 us
  local copies, waits for them, and re-layouts: 3.53 us -> 0.01 us
  other arithmetic: 3.38 us -> 0 us
  waiting for transfers between devices: 1.99 us -> 4.51 us
    pallas_call x5, Pallas kernels: 22 us -> 15.1 us  [the longest x1 6.22 us: local(): pl.pallas_call(functools.partial(window_kernel, wires_by_plane, STEP), ou...]
    ppermute x1, waiting for transfers between devices: 1.99 us -> 4.5 us  [local(): halo = lax.ppermute(tail, 'tm', [(i, (i + 1) % ring) for i in range(ring)])]
    add x2 -> x0, other arithmetic: 2.11 us -> none  [the longest x1 1.31 us: local(): (wire_slot >= induction).astype(jnp.int32)]
    unnamed x4 -> x2, local copies, waits for them, and re-layouts: 1.46 us -> 0.01 us
    pad x1 -> x0, other arithmetic: 1.27 us -> none  [local(): jnp.pad(time_kernel.astype(jnp.float32), ((0, 0), (0, LANES - taps)))]
    broadcast_in_dim x1 -> x0, local copies, waits for them, and re-layouts: 1.07 us -> none  [local(): code = jnp.broadcast_to(code[:, None], (rows, LANES))]
    slice x1 -> x0, local copies, waits for them, and re-layouts: 0.99 us -> none  [local(): waveforms[:, ticks - LANES:]]
  transfers between devices with their start and end apart: 2 -> 2, of which waited for: 1 -> 1; matrix products, arithmetic and copies ran while one was open for 13% -> 0% of each run, Pallas kernels for 36% -> 36%
where the time goes in v2:
time: 23 us; the launch traced here: 22.7 us
  Pallas kernels  15.1 us (66%)
  waiting for transfers between devices  4.51 us (20%)
  starting transfers between devices  3.09 us (13%)
    pallas_call x1, Pallas kernels, local(): pl.pallas_call(functools.partial(window_kernel, wires_by_plane, STEP), ou...  6.22 us
    ppermute x1, waiting for transfers between devices, local(): halo = lax.ppermute(tail, 'tm', [(i, (i + 1) % ring) for i in range(ring)])  4.5 us
    pallas_call x1, Pallas kernels, local(): pl.pallas_call(functools.partial(final_kernel, layout), out_shape=shape((...  4.4 us
    ppermute x1, starting transfers between devices, local(): halo = lax.ppermute(tail, 'tm', [(i, (i + 1) % ring) for i in range(ring)])  3.02 us
    pallas_call x1, Pallas kernels, local(): pl.pallas_call(place_kernel, out_shape=shape((channels, LANES), jnp.float...  1.97 us
    pallas_call x1, Pallas kernels, local(): pl.pallas_call(functools.partial(halo_kernel, STEP), out_shape=[shape((ro...  1.51 us
    pallas_call x1, Pallas kernels, local(): pl.pallas_call(cut_kernel, out_shape=jax.ShapeDtypeStruct((rows, LANES),...  0.98 us
  transfers between devices with their start and end apart: 2, of which 1 were waited for; matrix products, arithmetic and copies ran while one was open for 0% of the time, Pallas kernels for 36%

profile of v2, /device:TPU:0, one launch (start us, length us, event | category | flops | bytes accessed | tf_op | source)
XLA Modules:
  0.0 22.7 jit_solution(4720722560598270193)
XLA Ops:
  0.0 1.0 %cut_tail.1 = bf16[1280,128]{1,0:T(8,128)(2,1)S(1)} custom-call(bf16[1280,256]{1,0:T(8,128)(2,1)} %refs_4_.1), custom_call_target="tpu_custom_call" | custom-call | tf_op jit(solution)/shard_map/cut_tail/pallas_call | solution.py:264
  1.0 3.0 %collective-permute-start = (bf16[1280,128]{1,0:T(8,128)(2,1)S(1)}, bf16[1280,128]{1,0:T(8,128)(2,1)S(1)}, u32[]{:S(2)}, u32[]{:S(2)}) collective-permute-start(bf16[1280,128]{1,0:T(8,128)(2,1)S(1)} %cut_tail.1), channel_id=1, source_target_pairs={{0,2},{2,4},{4,6},{6,8},{8,10},{10,12},{12,14},{14,0},{1,3},{3,5},... | collective-permute-start | bytes 983048 | tf_op jit(solution)/shard_map/ppermute | solution.py:273
  4.0 6.2 %own_window.1 = (bf16[1280,128]{1,0:T(8,128)(2,1)S(1)}, f32[1280,128]{1,0:T(8,128)S(1)}, bf16[256,384]{1,0:T(8,128)(2,1)S(1)}, s32[1280,128]{1,0:T(8,128)S(1)}, ...) custom-call(s32[1]{0:T(128)} %bitcast.side, s32[20,128]{1,0:T(8,128)} %bitcast.7, ...), custom_call_target="tpu_custom_call" | custom-call | flops 1000000000 | bytes 8000000 | tf_op jit(solution)/shard_map/own_window/pallas_call | solution.py:298
  10.2 0.0 copy-start
  10.3 4.5 %collective-permute-done.halo = bf16[1280,128]{1,0:T(8,128)(2,1)S(1)} collective-permute-done((bf16[1280,128]{1,0:T(8,128)(2,1)S(1)}, bf16[1280,128]{1,0:T(8,128)(2,1)S(1)}, u32[]{:S(2)}, u32[]{:S(2)}) %collective-permute-start) | collective-permute-done | bytes 327712 | tf_op jit(solution)/shard_map/ppermute | solution.py:273
  14.8 1.5 %halo_window.1 = (bf16[1280,128]{1,0:T(8,128)(2,1)S(1)}, bf16[1280,128]{1,0:T(8,128)(2,1)S(1)}) custom-call(s32[1]{0:T(128)} %bitcast.side, bf16[1280,128]{1,0:T(8,128)(2,1)S(1)} %collective-permute-done.halo, s32[1280,128]{1,0:T(8,128)S(1)} %get-tuple-element.14.code, bf16[256,384]{1,0:T(8,128)(2,1)S(1)} %get-tuple-element.15.table_ref, ...), custom_call_target="tpu_custom_call" | custom-call | flops 100000000 | bytes 2000000 | tf_op jit(solution)/shard_map/halo_window/pallas_call | solution.py:322
  16.3 0.1 collective-permute-start.1
  16.4 0.0 copy-done
  16.4 2.0 %place_own.1.half_placed = f32[2560,128]{1,0:T(8,128)S(1)} custom-call(s32[1]{0:T(128)} %bitcast.side, s32[2560]{0:T(1024)S(1)} %copy-done, bf16[1280,128]{1,0:T(8,128)(2,1)S(1)} %get-tuple-element.19.own), custom_call_target="tpu_custom_call" | custom-call | flops 1000000 | bytes 3000000 | tf_op jit(solution)/shard_map/place_own/pallas_call | solution.py:334
  18.3 0.0 collective-permute-done.1.other
  18.4 4.4 %place_and_mix.1 = f32[2560,128]{1,0:T(8,128)} custom-call(s32[1]{0:T(128)} %bitcast.side, s32[2560]{0:T(1024)S(1)} %copy-done, bf16[1280,128]{1,0:T(8,128)(2,1)S(1)} %collective-permute-done.1.other, f32[2560,128]{1,0:T(8,128)S(1)} %place_own.1.half_placed, bf16[128,1792]{1,0:T(8,128)(2,1)S(1)} %get-tuple-element.20.refs_0_, ...), custom_call_target="tpu_custom_call" | custom-call | tf_op jit(solution)/shard_map/place_and_mix/pallas_call | solution.py:350
Async XLA Ops:
  1.0 13.8 %collective-permute-start = (bf16[1280,128]{1,0:T(8,128)(2,1)S(1)}, bf16[1280,128]{1,0:T(8,128)(2,1)S(1)}, u32[]{:S(2)}, u32[]{:S(2)}) collective-permute-start(bf16[1280,128]{1,0:T(8,128)(2,1)S(1)} %cut_tail.1), channel_id=1, source_target_pairs={{0,2},{2,4},{4,6},{6,8},{8,10},{10,12},{12,14},{14,0},{1,3},{3,5},... | collective-permute-start | bytes 983048 | tf_op jit(solution)/shard_map/ppermute | solution.py:273
  10.2 6.1 %copy-start = (s32[2560]{0:T(1024)S(1)}, s32[2560]{0:T(1024)}, u32[]{:S(2)}) copy-start(s32[2560]{0:T(1024)} %slots.3) | copy-start | bytes 30724
  16.3 2.1 %collective-permute-start.1 = (bf16[1280,128]{1,0:T(8,128)(2,1)S(1)}, bf16[1280,128]{1,0:T(8,128)(2,1)S(1)}, u32[]{:S(2)}, u32[]{:S(2)}) collective-permute-start(bf16[1280,128]{1,0:T(8,128)(2,1)S(1)} %get-tuple-element.18), channel_id=1, source_target_pairs={{0,1},{1,0},{2,3},{3,2},{4,5},{5,4},{6,7},{7,6},{8,9},{9,8},{10,11... | collective-permute-start | bytes 983048 | tf_op jit(solution)/shard_map/ppermute | solution.py:332

commit v3 on v2

v3 whole, which is shorter than its diff:
```python
import functools
import math

import jax
import jax.numpy as jnp
import numpy as np
from jax import lax
from jax.experimental import pallas as pl
from jax.experimental.pallas import tpu as pltpu
from jax.sharding import PartitionSpec as P


OFFSET_RANGE = 64
LANES = 128
VMEM = pltpu.VMEM
SMEM = pltpu.SMEM
KERNEL_VMEM = 16 * 2**20
STEP = 320
LAST_ROWS = 640


def padded(count):
    return -(-count // LANES) * LANES


def wire_tables(wires_by_plane):
    widest = max(wires_by_plane)
    coarse_rows, fine_rows = [], []
    for wires in wires_by_plane[1:]:
        base = padded(wires // 2)
        m = np.arange(wires, dtype=np.int64)
        step = np.arange(2 * base // LANES, dtype=np.int64)[:, None] * LANES - base
        turn = 2.0 * math.pi / wires
        coarse = step * m[None, :] % wires * turn
        fine = m[:, None] * np.arange(LANES, dtype=np.int64)[None, :] % wires * turn
        for table in (np.cos(coarse), np.sin(coarse)):
            full = np.zeros((2, step.shape[0], widest), np.float32)
            full[0, :, :wires:2] = table[:, ::2]
            full[1, :, 1:wires:2] = table[:, 1::2]
            coarse_rows.append(full.reshape(-1, widest))
        fine_rows.append(np.concatenate([np.cos(fine), np.sin(fine)], 1).astype(np.float32))
    fine = np.concatenate(fine_rows, 0)
    high = fine.astype(jnp.bfloat16)
    low = (fine - high.astype(np.float32)).astype(jnp.bfloat16)
    return np.concatenate(coarse_rows, 0), np.concatenate([high, low], 1)


def lane_roll(row, rows):
    r = lax.broadcasted_iota(jnp.int32, (rows, LANES), 0)
    l = lax.broadcasted_iota(jnp.int32, (rows, LANES), 1)
    spread = jnp.broadcast_to(row, (rows, LANES))
    return jnp.take_along_axis(spread, (l - r) & (LANES - 1), axis=1, mode="promise_in_bounds")


def split_dot(left, high, low):
    upper = left.astype(jnp.bfloat16)
    lower = (left - upper.astype(jnp.float32)).astype(jnp.bfloat16)
    rows = left.shape[0]
    both = jnp.dot(
        jnp.concatenate([upper, lower], 0), high, preferred_element_type=jnp.float32
    )
    return both[:rows] + both[rows:] + jnp.dot(upper, low, preferred_element_type=jnp.float32)


def make_responses(wires_by_plane, induction, collection, coarse, fine, outs):
    r = lax.broadcasted_iota(jnp.int32, (LANES, LANES), 0)
    l = lax.broadcasted_iota(jnp.int32, (LANES, LANES), 1)
    for plane, wires in enumerate(wires_by_plane):
        out = outs[plane]
        spans = out.shape[1] // LANES
        first = 0 if plane < 2 else coarse.shape[0] - 4 * spans
        ca = coarse[first : first + 2 * spans, :wires]
        sa = coarse[first + 2 * spans : first + 4 * spans, :wires]
        first = 0 if plane < 2 else wires_by_plane[0]
        rows = slice(first, first + wires)
        if plane < 2:
            real, imag, gain = (ref[plane : plane + 1, :] for ref in induction)
        else:
            real, imag, gain = (ref[...] for ref in collection)
        scale = gain / (real * real + imag * imag) * (1.0 / wires)
        ratio_re = real * scale
        ratio_im = -imag * scale
        u = ca * ratio_re + sa * ratio_im
        v = ca * ratio_im - sa * ratio_re
        taps = split_dot(u, fine[rows, :LANES], fine[rows, 2 * LANES : 3 * LANES])
        taps = taps + split_dot(v, fine[rows, LANES : 2 * LANES], fine[rows, 3 * LANES :])
        for parity in range(2):
            top = slice(parity * LANES, (parity + 1) * LANES)
            previous = None
            for span in range(spans):
                row = parity * spans + span
                here = lane_roll(taps[row : row + 1, :], LANES)
                before = here if previous is None else previous
                out[top, span * LANES : (span + 1) * LANES] = jnp.where(l >= r, here, before).astype(
                    jnp.bfloat16
                )
                previous = here


def rotated(block, offsets):
    l = lax.broadcasted_iota(jnp.int32, block.shape, 1)
    return jnp.take_along_axis(
        block.astype(jnp.float32), (l - offsets) & (LANES - 1), axis=1, mode="promise_in_bounds"
    )


def by_plane(sums, planes):
    zero = jnp.zeros_like(planes, dtype=jnp.float32)
    picked = jnp.where(planes == 2, sums[:, 2 * LANES :], zero)
    picked = jnp.where(planes == 1, sums[:, LANES : 2 * LANES], picked)
    return jnp.where(planes == 0, sums[:, :LANES], picked)


def cut_kernel(wave, *refs):
    tails, sem = refs[:-1], refs[-1]
    first = 0
    copies = []
    for i, tail in enumerate(tails):
        rows = pl.ds(first, tail.shape[0])
        copies.append(pltpu.make_async_copy(wave.at[rows, LANES:], tail, sem.at[i]))
        copies[-1].start()
        first += tail.shape[0]
    for copy in copies:
        copy.wait()


def window_kernel(wires_by_plane, step, side, *refs):
    count = 13
    sources, refs = refs[:count], refs[count:]
    high_out, low_out, table_out, code_out, near_out, far_out = refs[:6]
    responses = refs[6:9]
    held, refs = refs[9 : 9 + count], refs[9 + count :]
    words, wide_taps, sems = refs
    copies = [
        pltpu.make_async_copy(source, target, sems.at[i])
        for i, (source, target) in enumerate(zip(sources, held))
    ]
    for copy in copies:
        copy.start()
    slots, offset_rows, bad_rows, kernel_taps, wave = held[:5]
    induction, collection = held[5:8], held[8:11]
    coarse, fine = held[11:13]
    for copy in copies[:5]:
        copy.wait()
    r = lax.broadcasted_iota(jnp.int32, (LANES, LANES), 0)
    l = lax.broadcasted_iota(jnp.int32, (LANES, LANES), 1)

    wide_taps[...] = jnp.zeros_like(wide_taps)
    wide_taps[0:3, 0 : kernel_taps.shape[1]] = kernel_taps[...].astype(jnp.float32)
    for plane in range(3):
        rolled = lane_roll(wide_taps[plane : plane + 1, :], LANES)
        cols = slice(plane * LANES, (plane + 1) * LANES)
        table_out[:LANES, cols] = jnp.where(l < r, rolled, 0.0).astype(jnp.bfloat16)
        table_out[LANES:, cols] = jnp.where(l >= r, rolled, 0.0).astype(jnp.bfloat16)

    slot = slots[...]
    one, two = wires_by_plane[0], wires_by_plane[0] + wires_by_plane[1]
    planes = (slot >= one).astype(jnp.int32) + (slot >= two).astype(jnp.int32)
    planes = jnp.where(bad_rows[...] == 0, planes, 3)
    words[...] = offset_rows[...] + OFFSET_RANGE * planes

    groups = wave.shape[0] // LANES
    first_group = side[0] * groups

    near_out[0:groups, :] = slots[pl.ds(first_group, groups), :]
    far_out[0:groups, :] = slots[pl.ds((1 - side[0]) * groups, groups), :]

    def spread(i, carry):
        row = jnp.broadcast_to(words[pl.ds(first_group + i, 1), :], (LANES, LANES))
        code_out[pl.ds(pl.multiple_of(i * LANES, LANES), LANES), :] = row.T
        return carry

    lax.fori_loop(0, groups, spread, 0)

    def body(i, carry):
        rows = pl.ds(pl.multiple_of(i * step, step), step)
        word = code_out[rows, :]
        offsets = word & (OFFSET_RANGE - 1)
        plane = word // OFFSET_RANGE
        lane = lax.broadcasted_iota(jnp.int32, word.shape, 1)
        early = rotated(wave[rows, :LANES], offsets)
        late = rotated(wave[rows, LANES:], offsets)
        wrapped = lane < offsets
        low = jnp.where(wrapped, 0.0, early).astype(jnp.bfloat16)
        both = jnp.concatenate([early, jnp.where(wrapped, early, late)], 1).astype(jnp.bfloat16)
        table = table_out[...]
        low_sum = jnp.dot(low, table[LANES:, :], preferred_element_type=jnp.float32)
        high_sum = jnp.dot(both, table, preferred_element_type=jnp.float32)
        low_out[rows, :] = by_plane(low_sum, plane)
        high_out[rows, :] = by_plane(high_sum, plane).astype(jnp.bfloat16)
        return carry

    lax.fori_loop(0, wave.shape[0] // step, body, 0)
    for copy in copies[5:]:
        copy.wait()
    make_responses(wires_by_plane, induction, collection, coarse, fine, responses)


def halo_kernel(step, first, side, halo, code, table_ref, low_main, high, own_out, other_out):
    def body(i, carry):
        here = pl.ds(pl.multiple_of(i * step, step), step)
        rows = pl.ds(pl.multiple_of(first + i * step, step), step)
        word = code[rows, :]
        offsets = word & (OFFSET_RANGE - 1)
        planes = word // OFFSET_RANGE
        lane = lax.broadcasted_iota(jnp.int32, word.shape, 1)
        early = rotated(halo[here, :], offsets)
        both = jnp.concatenate([early, jnp.where(lane < offsets, early, 0.0)], 1).astype(
            jnp.bfloat16
        )
        sums = jnp.dot(both, table_ref[...], preferred_element_type=jnp.float32)
        low = low_main[rows, :] + by_plane(sums, planes)
        upper = high[rows, :].astype(jnp.float32)
        inner = side[0] == 0
        own_out[here, :] = jnp.where(inner, low, upper).astype(jnp.bfloat16)
        other_out[here, :] = jnp.where(inner, upper, low).astype(jnp.bfloat16)
        return carry

    lax.fori_loop(0, halo.shape[0] // step, body, 0)


def place_rows(source, wide, slots, first, target):
    count = source.shape[0]
    wide[0:count, :] = source[...].astype(jnp.float32)
    for k in range(count):
        slot = slots[(first + k) // LANES, (first + k) % LANES]
        target[pl.ds(slot, 1), :] = wide[k : k + 1, :]


def start_kernel(near, own, placed, wide):
    place_rows(own, wide, near, 0, placed)


def middle_kernel(near, far, own, other, before, placed, wide):
    del before
    place_rows(own, wide, near, other.shape[0], placed)
    place_rows(other, wide, far, 0, placed)


def final_kernel(layout, first, far, other, before, *refs):
    responses, out, ordered, wide, mixed, sems = refs[:3], *refs[3:]
    del before
    place_rows(other, wide, far, first, ordered)
    copies = []
    for plane, ((start, wires), resp) in enumerate(zip(layout, responses)):
        half = wires // 2
        base = padded(half)
        front = ordered[start : start + half, :]
        back = ordered[start + half : start + wires, :]
        total = (front + back).astype(jnp.bfloat16)
        change = (front - back).astype(jnp.bfloat16)
        for block in range(base // LANES):
            valid = min(LANES, half - block * LANES)
            columns = slice(base - block * LANES, base - block * LANES + half)
            even = jnp.dot(resp[:valid, columns], total, preferred_element_type=jnp.float32)
            odd = jnp.dot(
                resp[LANES : LANES + valid, columns], change, preferred_element_type=jnp.float32
            )
            top = start + block * LANES
            mixed[top : top + valid, :] = even + odd
            mixed[top + half : top + half + valid, :] = even - odd
        for part in range(2):
            span = pl.ds(start + part * half, half)
            copies.append(
                pltpu.make_async_copy(mixed.at[span], out.at[span], sems.at[2 * plane + part])
            )
            copies[-1].start()
    for copy in copies:
        copy.wait()


def deconvolve(
    waveforms,
    time_kernel,
    wire_slot,
    tick_offset,
    bad_channel,
    induction_real,
    induction_imaginary,
    induction_filter,
    collection_real,
    collection_imaginary,
    collection_filter,
):
    induction = induction_real.shape[1]
    collection = collection_real.shape[0]
    wires_by_plane = (induction, induction, collection)
    taps = time_kernel.shape[1]
    rows, ticks = waveforms.shape
    channels = wire_slot.shape[0]
    assert ticks == 2 * LANES and taps + OFFSET_RANGE == LANES
    assert channels == 2 * rows and channels == 2 * induction + collection

    ring = lax.axis_size("tm")
    hbm = pl.BlockSpec(memory_space=pltpu.HBM)
    keep = functools.partial(pltpu.with_memory_space_constraint, memory_space=pltpu.HBM)
    params = pltpu.CompilerParams(vmem_limit_bytes=KERNEL_VMEM)
    parts = (rows - LAST_ROWS, LAST_ROWS)
    tails = pl.pallas_call(
        cut_kernel,
        out_shape=[jax.ShapeDtypeStruct((part, LANES), jnp.bfloat16) for part in parts],
        in_specs=[hbm],
        out_specs=[pl.BlockSpec(memory_space=VMEM)] * 2,
        scratch_shapes=[pltpu.SemaphoreType.DMA((2,))],
        compiler_params=params,
        name="cut_tail",
    )(keep(waveforms))
    onward = [(i, (i + 1) % ring) for i in range(ring)]
    first_halo = lax.ppermute(tails[0], "tm", onward)
    last_halo = lax.ppermute(tails[1], "tm", onward)

    side = lax.axis_index("apa")
    side_word = side.reshape(1).astype(jnp.int32)
    vm = pl.BlockSpec(memory_space=VMEM)
    sm = pl.BlockSpec(memory_space=SMEM)
    shape = jax.ShapeDtypeStruct

    def by_lanes(vector):
        return vector.reshape(channels // LANES, LANES)

    inputs = [
        by_lanes(wire_slot),
        by_lanes(tick_offset),
        by_lanes(bad_channel),
        time_kernel,
        waveforms,
        induction_real,
        induction_imaginary,
        induction_filter,
        collection_real[None],
        collection_imaginary[None],
        collection_filter[None],
        *(jnp.asarray(t) for t in wire_tables(wires_by_plane)),
    ]
    window = pl.pallas_call(
        functools.partial(window_kernel, wires_by_plane, 256),
        out_shape=[
            shape((rows, LANES), jnp.bfloat16),
            shape((rows, LANES), jnp.float32),
            shape((2 * LANES, 3 * LANES), jnp.bfloat16),
            shape((rows, LANES), jnp.int32),
            shape((rows // LANES, LANES), jnp.int32),
            shape((rows // LANES, LANES), jnp.int32),
        ]
        + [shape((2 * LANES, 2 * padded(w // 2)), jnp.bfloat16) for w in wires_by_plane],
        in_specs=[sm] + [hbm] * len(inputs),
        out_specs=[vm] * 9,
        scratch_shapes=[pltpu.VMEM(x.shape, x.dtype) for x in inputs]
        + [
            pltpu.VMEM((channels // LANES, LANES), jnp.int32),
            pltpu.VMEM((8, LANES), jnp.float32),
            pltpu.SemaphoreType.DMA((len(inputs),)),
        ],
        compiler_params=params,
        cost_estimate=pl.CostEstimate(flops=10**9, bytes_accessed=8 * 10**6, transcendentals=0),
        name="own_window",
    )(side_word, *map(keep, inputs))
    high, low_main, table, code, near, far = window[:6]
    responses = window[6:]

    def finish(halo, first):
        count = halo.shape[0]
        return pl.pallas_call(
            functools.partial(halo_kernel, STEP, first),
            out_shape=[shape((count, LANES), jnp.bfloat16)] * 2,
            in_specs=[sm] + [vm] * 5,
            out_specs=[vm] * 2,
            compiler_params=params,
            cost_estimate=pl.CostEstimate(
                flops=10**5 * count, bytes_accessed=10**3 * count, transcendentals=0
            ),
            name="halo_window",
        )(side_word, halo, code, table, low_main, high)

    def place(kernel, aliases, *operands):
        return pl.pallas_call(
            kernel,
            out_shape=shape((channels, LANES), jnp.float32),
            in_specs=[sm if x.dtype == jnp.int32 else vm for x in operands],
            out_specs=vm,
            scratch_shapes=[pltpu.VMEM((rows, LANES), jnp.float32)],
            input_output_aliases=aliases,
            compiler_params=params,
            cost_estimate=pl.CostEstimate(flops=10**6, bytes_accessed=10**6, transcendentals=0),
        )(*operands)

    partner = [(0, 1), (1, 0)]
    own_first, other_first = finish(first_halo, 0)
    received_first = lax.ppermute(other_first, "apa", partner)
    placed = place(start_kernel, {}, near, own_first)
    own_last, other_last = finish(last_halo, parts[0])
    received_last = lax.ppermute(other_last, "apa", partner)
    placed = place(middle_kernel, {4: 0}, near, far, own_last, received_first, placed)

    layout = []
    start = 0
    for wires in wires_by_plane:
        layout.append((start, wires))
        start += wires
    return pl.pallas_call(
        functools.partial(final_kernel, layout, parts[0]),
        out_shape=[shape((channels, LANES), jnp.float32)] * 2,
        in_specs=[sm] + [vm] * 5,
        out_specs=[pl.BlockSpec(memory_space=pl.ANY), vm],
        scratch_shapes=[
            pltpu.VMEM((rows, LANES), jnp.float32),
            pltpu.VMEM((channels, LANES), jnp.float32),
            pltpu.SemaphoreType.DMA((6,)),
        ],
        input_output_aliases={2: 1},
        compiler_params=params,
        name="place_and_mix",
    )(far, received_last, placed, *responses)[0]


def solution(mesh):
    placed = (P(("grp", "apa"), "tm"), P(), P("grp"), P("grp"), P("grp")) + (P(),) * 6
    return jax.shard_map(
        deconvolve, mesh=mesh, in_specs=placed, out_specs=P("grp", ("tm", "apa")), check_vma=False
    )
```

time: 23 us -> 21.1 us (0.917)
  waiting for transfers between devices: 4.51 us -> 2.66 us
  starting transfers between devices: 3.09 us -> 4.71 us
  Pallas kernels: 15.1 us -> 13.5 us
    ppermute x2 -> x4, waiting for transfers between devices: 4.51 us -> 2.66 us  [the longest x1 1.92 us: deconvolve(): last_halo = lax.ppermute(tails[1], 'tm', onward)]
    ppermute x2 -> x4, starting transfers between devices: 3.09 us -> 4.71 us  [the longest x1 3.02 us: deconvolve(): first_halo = lax.ppermute(tails[0], 'tm', onward)]
    pallas_call x5 -> x7, Pallas kernels: 15.1 us -> 13.5 us  [the longest x1 5.79 us: deconvolve(): pl.pallas_call(functools.partial(window_kernel, wires_by_plane, 256), out...]
  transfers between devices with their start and end apart: 2 -> 4, of which waited for: 1 -> 2; matrix products, arithmetic and copies ran while one was open for 0% -> 0% of each run, Pallas kernels for 36% -> 46%
where the time goes in v3:
time: 21.1 us; the launch traced here: 20.9 us
  Pallas kernels  13.5 us (64%)
  starting transfers between devices  4.71 us (22%)
  waiting for transfers between devices  2.66 us (13%)
    pallas_call x1, Pallas kernels, deconvolve(): pl.pallas_call(functools.partial(window_kernel, wires_by_plane, 256), out...  5.79 us
    ppermute x1, starting transfers between devices, deconvolve(): first_halo = lax.ppermute(tails[0], 'tm', onward)  3.02 us
    pallas_call x1, Pallas kernels, deconvolve(): pl.pallas_call(functools.partial(final_kernel, layout, parts[0]), out_sha...  2.82 us
    pallas_call x2, Pallas kernels, place(): pl.pallas_call(kernel, out_shape=shape((channels, LANES), jnp.float32), i...  2.54 us
    ppermute x1, waiting for transfers between devices, deconvolve(): last_halo = lax.ppermute(tails[1], 'tm', onward)  1.92 us
    ppermute x1, starting transfers between devices, deconvolve(): last_halo = lax.ppermute(tails[1], 'tm', onward)  1.55 us
    pallas_call x2, Pallas kernels, finish(): pl.pallas_call(functools.partial(halo_kernel, STEP, first), out_shape=[sh...  1.31 us
    pallas_call x1, Pallas kernels, deconvolve(): pl.pallas_call(cut_kernel, out_shape=[jax.ShapeDtypeStruct((part, LANES),...  1.01 us
  transfers between devices with their start and end apart: 4, of which 2 were waited for; matrix products, arithmetic and copies ran while one was open for 0% of the time, Pallas kernels for 46%

profile of v3, /device:TPU:0, one launch (start us, length us, event | category | flops | bytes accessed | tf_op | source)
XLA Modules:
  0.0 20.9 jit_solution(13734296151259472664)
XLA Ops:
  0.0 1.0 %cut_tail.1 = (bf16[640,128]{1,0:T(8,128)(2,1)S(1)}, bf16[640,128]{1,0:T(8,128)(2,1)S(1)}) custom-call(bf16[1280,256]{1,0:T(8,128)(2,1)} %wave.1), custom_call_target="tpu_custom_call" | custom-call | tf_op jit(solution)/shard_map/cut_tail/pallas_call | solution.py:299
  1.0 3.0 %collective-permute-start.2 = (bf16[640,128]{1,0:T(8,128)(2,1)S(1)}, bf16[640,128]{1,0:T(8,128)(2,1)S(1)}, u32[]{:S(2)}, u32[]{:S(2)}) collective-permute-start(bf16[640,128]{1,0:T(8,128)(2,1)S(1)} %get-tuple-element.30), channel_id=1, source_target_pairs={{0,2},{2,4},{4,6},{6,8},{8,10},{10,12},{12,14},{14,0},{1,3},{3,5},... | collective-permute-start | bytes 491528 | tf_op jit(solution)/shard_map/ppermute | solution.py:309
  4.0 1.5 %collective-permute-start = (bf16[640,128]{1,0:T(8,128)(2,1)S(1)}, bf16[640,128]{1,0:T(8,128)(2,1)S(1)}, u32[]{:S(2)}, u32[]{:S(2)}) collective-permute-start(bf16[640,128]{1,0:T(8,128)(2,1)S(1)} %get-tuple-element.22), channel_id=1, source_target_pairs={{0,2},{2,4},{4,6},{6,8},{8,10},{10,12},{12,14},{14,0},{1,3},{3,5},... | collective-permute-start | bytes 491528 | tf_op jit(solution)/shard_map/ppermute | solution.py:310
  5.6 5.8 %own_window.1 = (bf16[1280,128]{1,0:T(8,128)(2,1)S(1)}, f32[1280,128]{1,0:T(8,128)S(1)}, bf16[256,384]{1,0:T(8,128)(2,1)S(1)}, s32[1280,128]{1,0:T(8,128)S(1)}, ...) custom-call(s32[1]{0:T(128)} %bitcast.side, ...), custom_call_target="tpu_custom_call" | custom-call | flops 1000000000 | bytes 8000000 | tf_op jit(solution)/shard_map/own_window/pallas_call | solution.py:335
  11.4 0.7 %collective-permute-done.2.halo = bf16[640,128]{1,0:T(8,128)(2,1)S(1)} collective-permute-done((bf16[640,128]{1,0:T(8,128)(2,1)S(1)}, bf16[640,128]{1,0:T(8,128)(2,1)S(1)}, u32[]{:S(2)}, u32[]{:S(2)}) %collective-permute-start.2) | collective-permute-done | bytes 163872 | tf_op jit(solution)/shard_map/ppermute | solution.py:309
  12.1 0.7 %halo_window.3 = (bf16[640,128]{1,0:T(8,128)(2,1)S(1)}, bf16[640,128]{1,0:T(8,128)(2,1)S(1)}) custom-call(s32[1]{0:T(128)} %bitcast.side, bf16[640,128]{1,0:T(8,128)(2,1)S(1)} %collective-permute-done.2.halo, s32[1280,128]{1,0:T(8,128)S(1)} %get-tuple-element.23.code, bf16[256,384]{1,0:T(8,128)(2,1)S(1)} %get-tuple-element.24.table_ref, ...), custom_call_target="tpu_custom_call" | custom-call | flops 64000000 | bytes 640000 | tf_op jit(solution)/shard_map/halo_window/pallas_call | solution.py:363
  12.8 0.1 collective-permute-start.3
  12.9 1.9 %collective-permute-done.halo = bf16[640,128]{1,0:T(8,128)(2,1)S(1)} collective-permute-done((bf16[640,128]{1,0:T(8,128)(2,1)S(1)}, bf16[640,128]{1,0:T(8,128)(2,1)S(1)}, u32[]{:S(2)}, u32[]{:S(2)}) %collective-permute-start) | collective-permute-done | bytes 163872 | tf_op jit(solution)/shard_map/ppermute | solution.py:310
  14.8 0.7 %halo_window.2 = (bf16[640,128]{1,0:T(8,128)(2,1)S(1)}, bf16[640,128]{1,0:T(8,128)(2,1)S(1)}) custom-call(s32[1]{0:T(128)} %bitcast.side, bf16[640,128]{1,0:T(8,128)(2,1)S(1)} %collective-permute-done.halo, s32[1280,128]{1,0:T(8,128)S(1)} %get-tuple-element.23.code, bf16[256,384]{1,0:T(8,128)(2,1)S(1)} %get-tuple-element.24.table_ref, ...), custom_call_target="tpu_custom_call" | custom-call | flops 64000000 | bytes 640000 | tf_op jit(solution)/shard_map/halo_window/pallas_call | solution.py:363
  15.4 0.1 collective-permute-start.1
  15.5 1.0 %shard_map.127.before = f32[2560,128]{1,0:T(8,128)S(1)} custom-call(s32[10,128]{1,0:T(8,128)S(1)} %get-tuple-element.28.near, bf16[640,128]{1,0:T(8,128)(2,1)S(1)} %get-tuple-element.32.own), custom_call_target="tpu_custom_call" | custom-call | flops 1000000 | bytes 1000000 | tf_op jit(solution)/shard_map/pallas_call | solution.py:376
  16.6 0.0 collective-permute-done.3.other
  16.6 1.5 %shard_map.128.before = f32[2560,128]{1,0:T(8,128)S(1)} custom-call(s32[10,128]{1,0:T(8,128)S(1)} %get-tuple-element.28.near, s32[10,128]{1,0:T(8,128)S(1)} %get-tuple-element.21.far, bf16[640,128]{1,0:T(8,128)(2,1)S(1)} %get-tuple-element.29.own, bf16[640,128]{1,0:T(8,128)(2,1)S(1)} %collective-permute-done.3.other, ...), custom_call_target="tpu_custom_call", output_to_operand_aliasing={{}: (4, {})} | custom-call | flops 1000000 | bytes 1000000 | tf_op jit(solution)/shard_map/pallas_call | solution.py:376
  18.1 0.0 collective-permute-done.1.other
  18.1 2.8 %place_and_mix.1 = (f32[2560,128]{1,0:T(8,128)}, f32[2560,128]{1,0:T(8,128)S(1)}) custom-call(s32[10,128]{1,0:T(8,128)S(1)} %get-tuple-element.21.far, bf16[640,128]{1,0:T(8,128)(2,1)S(1)} %collective-permute-done.1.other, f32[2560,128]{1,0:T(8,128)S(1)} %shard_map.128.before, ...), custom_call_target="tpu_custom_call", output_to_operand_aliasing={{1}: (2, {})} | custom-call | tf_op jit(solution)/shard_map/place_and_mix/pallas_call | solution.py:400
Async XLA Ops:
  1.0 11.1 %collective-permute-start.2 = (bf16[640,128]{1,0:T(8,128)(2,1)S(1)}, bf16[640,128]{1,0:T(8,128)(2,1)S(1)}, u32[]{:S(2)}, u32[]{:S(2)}) collective-permute-start(bf16[640,128]{1,0:T(8,128)(2,1)S(1)} %get-tuple-element.30), channel_id=1, source_target_pairs={{0,2},{2,4},{4,6},{6,8},{8,10},{10,12},{12,14},{14,0},{1,3},{3,5},... | collective-permute-start | bytes 491528 | tf_op jit(solution)/shard_map/ppermute | solution.py:309
  4.0 10.7 %collective-permute-start = (bf16[640,128]{1,0:T(8,128)(2,1)S(1)}, bf16[640,128]{1,0:T(8,128)(2,1)S(1)}, u32[]{:S(2)}, u32[]{:S(2)}) collective-permute-start(bf16[640,128]{1,0:T(8,128)(2,1)S(1)} %get-tuple-element.22), channel_id=1, source_target_pairs={{0,2},{2,4},{4,6},{6,8},{8,10},{10,12},{12,14},{14,0},{1,3},{3,5},... | collective-permute-start | bytes 491528 | tf_op jit(solution)/shard_map/ppermute | solution.py:310
  12.8 3.8 %collective-permute-start.3 = (bf16[640,128]{1,0:T(8,128)(2,1)S(1)}, bf16[640,128]{1,0:T(8,128)(2,1)S(1)}, u32[]{:S(2)}, u32[]{:S(2)}) collective-permute-start(bf16[640,128]{1,0:T(8,128)(2,1)S(1)} %get-tuple-element.31), channel_id=1, source_target_pairs={{0,1},{1,0},{2,3},{3,2},{4,5},{5,4},{6,7},{7,6},{8,9},{9,8},{10,11... | collective-permute-start | bytes 491528 | tf_op jit(solution)/shard_map/ppermute | solution.py:389
  15.4 2.6 %collective-permute-start.1 = (bf16[640,128]{1,0:T(8,128)(2,1)S(1)}, bf16[640,128]{1,0:T(8,128)(2,1)S(1)}, u32[]{:S(2)}, u32[]{:S(2)}) collective-permute-start(bf16[640,128]{1,0:T(8,128)(2,1)S(1)} %get-tuple-element.27), channel_id=1, source_target_pairs={{0,1},{1,0},{2,3},{3,2},{4,5},{5,4},{6,7},{7,6},{8,9},{9,8},{10,11... | collective-permute-start | bytes 491528 | tf_op jit(solution)/shard_map/ppermute | solution.py:392

commit v4 on v3

v4 whole, which is shorter than its diff:
```python
import functools
import math

import jax
import jax.numpy as jnp
import numpy as np
from jax import lax
from jax.experimental import pallas as pl
from jax.experimental.pallas import tpu as pltpu
from jax.sharding import PartitionSpec as P


OFFSET_RANGE = 64
LANES = 128
VMEM = pltpu.VMEM
SMEM = pltpu.SMEM
KERNEL_VMEM = 16 * 2**20
STEP = 256
LAST_ROWS = 512


def padded(count):
    return -(-count // LANES) * LANES


def wire_tables(wires_by_plane):
    widest = max(wires_by_plane)
    coarse_rows, fine_rows = [], []
    for wires in wires_by_plane[1:]:
        base = padded(wires // 2)
        m = np.arange(wires, dtype=np.int64)
        step = np.arange(2 * base // LANES, dtype=np.int64)[:, None] * LANES - base
        turn = 2.0 * math.pi / wires
        coarse = step * m[None, :] % wires * turn
        fine = m[:, None] * np.arange(LANES, dtype=np.int64)[None, :] % wires * turn
        for table in (np.cos(coarse), np.sin(coarse)):
            full = np.zeros((2, step.shape[0], widest), np.float32)
            full[0, :, :wires:2] = table[:, ::2]
            full[1, :, 1:wires:2] = table[:, 1::2]
            coarse_rows.append(full.reshape(-1, widest))
        fine_rows.append(np.concatenate([np.cos(fine), np.sin(fine)], 1).astype(np.float32))
    fine = np.concatenate(fine_rows, 0)
    high = fine.astype(jnp.bfloat16)
    low = (fine - high.astype(np.float32)).astype(jnp.bfloat16)
    return np.concatenate(coarse_rows, 0), np.concatenate([high, low], 1)


def take_lanes(rows, lanes):
    return lax.gather(
        rows,
        lanes[..., None],
        lax.GatherDimensionNumbers(
            offset_dims=(),
            collapsed_slice_dims=(1,),
            start_index_map=(1,),
            operand_batching_dims=(0,),
            start_indices_batching_dims=(0,),
        ),
        slice_sizes=(1, 1),
        mode=lax.GatherScatterMode.PROMISE_IN_BOUNDS,
    )


def lane_roll(row, rows):
    r = lax.broadcasted_iota(jnp.int32, (rows, LANES), 0)
    l = lax.broadcasted_iota(jnp.int32, (rows, LANES), 1)
    return take_lanes(jnp.broadcast_to(row, (rows, LANES)), (l - r) & (LANES - 1))


def split_dot(left, high, low):
    upper = left.astype(jnp.bfloat16)
    lower = (left - upper.astype(jnp.float32)).astype(jnp.bfloat16)
    rows = left.shape[0]
    both = jnp.dot(
        jnp.concatenate([upper, lower], 0), high, preferred_element_type=jnp.float32
    )
    return both[:rows] + both[rows:] + jnp.dot(upper, low, preferred_element_type=jnp.float32)


def make_responses(wires_by_plane, induction, collection, coarse, fine, outs):
    r = lax.broadcasted_iota(jnp.int32, (LANES, LANES), 0)
    l = lax.broadcasted_iota(jnp.int32, (LANES, LANES), 1)
    for plane, wires in enumerate(wires_by_plane):
        out = outs[plane]
        spans = out.shape[1] // LANES
        first = 0 if plane < 2 else coarse.shape[0] - 4 * spans
        ca = coarse[first : first + 2 * spans, :wires]
        sa = coarse[first + 2 * spans : first + 4 * spans, :wires]
        first = 0 if plane < 2 else wires_by_plane[0]
        rows = slice(first, first + wires)
        if plane < 2:
            real, imag, gain = (ref[plane : plane + 1, :] for ref in induction)
        else:
            real, imag, gain = (ref[...] for ref in collection)
        scale = gain / (real * real + imag * imag) * (1.0 / wires)
        ratio_re = real * scale
        ratio_im = -imag * scale
        u = ca * ratio_re + sa * ratio_im
        v = ca * ratio_im - sa * ratio_re
        taps = split_dot(u, fine[rows, :LANES], fine[rows, 2 * LANES : 3 * LANES])
        taps = taps + split_dot(v, fine[rows, LANES : 2 * LANES], fine[rows, 3 * LANES :])
        for parity in range(2):
            top = slice(parity * LANES, (parity + 1) * LANES)
            previous = None
            for span in range(spans):
                row = parity * spans + span
                here = lane_roll(taps[row : row + 1, :], LANES)
                before = here if previous is None else previous
                out[top, span * LANES : (span + 1) * LANES] = jnp.where(l >= r, here, before).astype(
                    jnp.bfloat16
                )
                previous = here


def delays(word):
    lane = lax.broadcasted_iota(jnp.int32, word.shape, 1)
    source = (lane - word) & (LANES - 1)
    return source, source > lane


def by_plane(sums, word):
    picked = jnp.where(word < 3 * LANES, sums[:, 2 * LANES :], 0.0)
    picked = jnp.where(word < 2 * LANES, sums[:, LANES : 2 * LANES], picked)
    return jnp.where(word < LANES, sums[:, :LANES], picked)


def start_all(pairs, sems):
    copies = [
        pltpu.make_async_copy(source, target, sems.at[i])
        for i, (source, target) in enumerate(pairs)
    ]
    for copy in copies:
        copy.start()
    return copies


def cut_kernel(wave, *refs):
    tails, sems = refs[:-1], refs[-1]
    pairs = []
    first = 0
    for tail in tails:
        pairs.append((wave.at[pl.ds(first, tail.shape[0]), LANES:], tail))
        first += tail.shape[0]
    for copy in start_all(pairs, sems):
        copy.wait()


def response_kernel(wires_by_plane, *refs):
    make_responses(wires_by_plane, refs[0:3], refs[3:6], refs[6], refs[7], refs[8:11])


def fill_table(kernel_taps, wide_taps, table_out):
    r = lax.broadcasted_iota(jnp.int32, (LANES, LANES), 0)
    l = lax.broadcasted_iota(jnp.int32, (LANES, LANES), 1)
    wide_taps[...] = jnp.zeros_like(wide_taps)
    wide_taps[0:3, 0 : kernel_taps.shape[1]] = kernel_taps[...].astype(jnp.float32)
    for plane in range(3):
        rolled = lane_roll(wide_taps[plane : plane + 1, :], LANES)
        cols = slice(plane * LANES, (plane + 1) * LANES)
        table_out[:LANES, cols] = jnp.where(l < r, rolled, 0.0).astype(jnp.bfloat16)
        table_out[LANES:, cols] = jnp.where(l >= r, rolled, 0.0).astype(jnp.bfloat16)


def filter_window(wires_by_plane, side, front, tails, small, table, outs, words):
    high_out, low_out, code_out = outs
    slots, offset_rows, bad_rows = small
    one, two = wires_by_plane[0], wires_by_plane[0] + wires_by_plane[1]
    slot = slots[...]
    planes = (slot >= one).astype(jnp.int32) + (slot >= two).astype(jnp.int32)
    planes = jnp.where(bad_rows[...] == 0, planes, 3)
    words[...] = offset_rows[...] + LANES * planes
    groups = front.shape[0] // LANES
    for i in range(groups):
        row = jnp.broadcast_to(words[pl.ds(side[0] * groups + i, 1), :], (LANES, LANES))
        code_out[i * LANES : (i + 1) * LANES, :] = row.T

    first = 0
    for tail in tails:
        step = math.gcd(tail.shape[0], STEP)
        for top in range(0, tail.shape[0], step):
            rows = slice(first + top, first + top + step)
            word = code_out[rows, :]
            source, wrapped = delays(word)
            early = take_lanes(front[rows, :].astype(jnp.float32), source)
            late = take_lanes(tail[top : top + step, :].astype(jnp.float32), source)
            low = jnp.where(wrapped, 0.0, early).astype(jnp.bfloat16)
            both = jnp.concatenate([early, jnp.where(wrapped, early, late)], 1)
            low_sum = jnp.dot(low, table[LANES:, :], preferred_element_type=jnp.float32)
            high_sum = jnp.dot(
                both.astype(jnp.bfloat16), table[...], preferred_element_type=jnp.float32
            )
            low_out[rows, :] = by_plane(low_sum, word)
            high_out[rows, :] = by_plane(high_sum, word).astype(jnp.bfloat16)
        first += tail.shape[0]


def window_kernel(wires_by_plane, count, side, first_tail, last_tail, wave, *refs):
    sources, refs = refs[:count], refs[count:]
    high_out, low_out, code_out, table_out, near_out, far_out = refs[:6]
    kept = refs[6 : 6 + count - 4]
    front, slots, offset_rows, bad_rows, kernel_taps, words, wide_taps, sems = refs[6 + count - 4 :]
    held = (slots, offset_rows, bad_rows, kernel_taps)
    copies = start_all(
        [*zip(sources[:4], held), (wave.at[:, :LANES], front), *zip(sources[4:], kept)], sems
    )
    for copy in copies[:5]:
        copy.wait()
    fill_table(kernel_taps, wide_taps, table_out)
    groups = front.shape[0] // LANES
    near_out[...] = slots[pl.ds(side[0] * groups, groups), :]
    far_out[...] = slots[pl.ds((1 - side[0]) * groups, groups), :]
    small = (slots, offset_rows, bad_rows)
    outs = (high_out, low_out, code_out)
    filter_window(wires_by_plane, side, front, (first_tail, last_tail), small, table_out, outs, words)
    for copy in copies[5:]:
        copy.wait()


def finish_early(halo, code, table, low_main, write):
    step = STEP

    def body(i, carry):
        rows = pl.ds(pl.multiple_of(i * step, step), step)
        word = code[rows, :]
        source, wrapped = delays(word)
        early = take_lanes(halo[rows, :].astype(jnp.float32), source)
        both = jnp.concatenate([early, jnp.where(wrapped, early, 0.0)], 1).astype(jnp.bfloat16)
        sums = jnp.dot(both, table[...], preferred_element_type=jnp.float32)
        write(rows, (low_main[rows, :] + by_plane(sums, word)).astype(jnp.bfloat16))
        return carry

    lax.fori_loop(0, halo.shape[0] // step, body, 0, unroll=True)


def other_kernel(first, side, halo, table, high, low_main, code, out):
    rows = pl.ds(first, out.shape[0])

    @pl.when(side[0] == 0)
    def _():
        out[...] = high[rows, :]

    @pl.when(side[0] != 0)
    def _():
        def write(here, value):
            out[here, :] = value

        finish_early(halo, code.at[rows], table, low_main.at[rows], write)


def finish_own(side, halo, table, high, low_main, code, wide):
    @pl.when(side[0] == 0)
    def _():
        def write(rows, value):
            wide[rows, :] = value.astype(jnp.float32)

        finish_early(halo, code, table, low_main, write)

    @pl.when(side[0] != 0)
    def _():
        wide[0 : high.shape[0], :] = high[...].astype(jnp.float32)


def place_rows(count, wide, slots, first, target):
    for k in range(count):
        slot = slots[(first + k) // LANES, (first + k) % LANES]
        target[pl.ds(slot, 1), :] = wide[k : k + 1, :]


def middle_kernel(side, near, far, other, halo, table, high, low_main, code, target, *refs):
    wide, wide_other, near_slots, far_slots, sems = refs
    loads = start_all([(near, near_slots), (far, far_slots)], sems)
    count = halo.shape[0]
    wide_other[...] = other[...].astype(jnp.float32)
    finish_own(side, halo, table, high.at[pl.ds(0, count)], low_main, code, wide)
    for load in loads:
        load.wait()
    place_rows(count, wide_other, far_slots, 0, target)
    place_rows(count, wide, near_slots, 0, target)


def final_kernel(layout, first, side, near, far, other, halo, table, high, low_main, code, before, *refs):
    responses, out, ordered = refs[:3], refs[3], refs[4]
    wide, wide_other, mixed, near_slots, far_slots, sems = refs[5:]
    del before
    own = pl.ds(first, halo.shape[0])
    high, low_main, code = high.at[own], low_main.at[own], code.at[own]
    loads = [
        pltpu.make_async_copy(near, near_slots, sems.at[0]),
        pltpu.make_async_copy(far, far_slots, sems.at[1]),
    ]
    for load in loads:
        load.start()
    wide_other[...] = other[...].astype(jnp.float32)
    finish_own(side, halo, table, high, low_main, code, wide)
    for load in loads:
        load.wait()
    place_rows(other.shape[0], wide_other, far_slots, first, ordered)
    place_rows(halo.shape[0], wide, near_slots, first, ordered)
    copies = []
    for (start, wires), resp in zip(layout, responses):
        half = wires // 2
        base = padded(half)
        front = ordered[start : start + half, :]
        back = ordered[start + half : start + wires, :]
        total = (front + back).astype(jnp.bfloat16)
        change = (front - back).astype(jnp.bfloat16)
        for block in range(base // LANES):
            valid = min(LANES, half - block * LANES)
            columns = slice(base - block * LANES, base - block * LANES + half)
            even = jnp.dot(resp[:valid, columns], total, preferred_element_type=jnp.float32)
            odd = jnp.dot(
                resp[LANES : LANES + valid, columns], change, preferred_element_type=jnp.float32
            )
            top = start + block * LANES
            mixed[top : top + valid, :] = even + odd
            mixed[top + half : top + half + valid, :] = even - odd
        span = pl.ds(start, wires)
        copies.append(pltpu.make_async_copy(mixed.at[span], out.at[span], sems.at[2 + len(copies)]))
        copies[-1].start()
    for copy in copies:
        copy.wait()


def deconvolve(
    waveforms,
    time_kernel,
    wire_slot,
    tick_offset,
    bad_channel,
    induction_real,
    induction_imaginary,
    induction_filter,
    collection_real,
    collection_imaginary,
    collection_filter,
):
    induction = induction_real.shape[1]
    collection = collection_real.shape[0]
    wires_by_plane = (induction, induction, collection)
    taps = time_kernel.shape[1]
    rows, ticks = waveforms.shape
    channels = wire_slot.shape[0]
    assert ticks == 2 * LANES and taps + OFFSET_RANGE == LANES
    assert channels == 2 * rows and channels == 2 * induction + collection
    parts = (rows - LAST_ROWS, LAST_ROWS)

    vm = pl.BlockSpec(memory_space=VMEM)
    sm = pl.BlockSpec(memory_space=SMEM)
    hbm = pl.BlockSpec(memory_space=pltpu.HBM)
    keep = functools.partial(pltpu.with_memory_space_constraint, memory_space=pltpu.HBM)
    shape = jax.ShapeDtypeStruct
    side = lax.axis_index("apa")
    side_word = side.reshape(1).astype(jnp.int32)

    def call(kernel, outs, operands, specs, scratch, flops, **more):
        return pl.pallas_call(
            kernel,
            out_shape=outs,
            in_specs=specs,
            out_specs=more.pop("out_specs", [vm] * len(outs)),
            scratch_shapes=scratch,
            compiler_params=pltpu.CompilerParams(vmem_limit_bytes=KERNEL_VMEM),
            cost_estimate=pl.CostEstimate(flops=flops, bytes_accessed=10**6, transcendentals=0),
            **more,
        )(*operands)

    def by_lanes(vector):
        return vector.reshape(channels // LANES, LANES)

    def like(array):
        return shape(array.shape, array.dtype)

    small = [
        by_lanes(wire_slot),
        by_lanes(tick_offset),
        by_lanes(bad_channel),
        time_kernel,
        induction_real,
        induction_imaginary,
        induction_filter,
        collection_real[None],
        collection_imaginary[None],
        collection_filter[None],
    ]
    first_tail, last_tail = call(
        cut_kernel,
        [shape((count, LANES), waveforms.dtype) for count in parts],
        [keep(waveforms)],
        [hbm],
        [pltpu.SemaphoreType.DMA((2,))],
        10**5,
    )

    groups, ring = lax.axis_size("grp"), lax.axis_size("tm")
    axes = ("grp", "tm", "apa")

    def onward(core):
        pairs = []
        for g in range(groups):
            for t in range(ring):
                here = 2 * (g * ring + t)
                pairs.append((here + core, 2 * (g * ring + (t + 1) % ring) + core))
                pairs.append((here + 1 - core, 2 * ((g + 1) % groups * ring + t) + 1 - core))
        return pairs

    halos = {}
    for name, part in (("first", first_tail), ("last", last_tail)):
        for core, whose in ((1, "other"), (0, "own")):
            halos[whose, name] = lax.ppermute(part, axes, onward(core))

    constants = [jnp.asarray(t) for t in wire_tables(wires_by_plane)]
    sources = [*small, *constants]
    slot_shape = shape((rows // LANES, LANES), jnp.int32)
    window = call(
        functools.partial(window_kernel, wires_by_plane, len(sources)),
        [
            shape((rows, LANES), jnp.bfloat16),
            shape((rows, LANES), jnp.float32),
            shape((rows, LANES), jnp.int32),
            shape((2 * LANES, 3 * LANES), jnp.bfloat16),
            slot_shape,
            slot_shape,
        ]
        + [like(x) for x in sources[4:]],
        [side_word, first_tail, last_tail, *map(keep, [waveforms, *sources])],
        [sm, vm, vm] + [hbm] * (1 + len(sources)),
        [pltpu.VMEM((rows, LANES), jnp.bfloat16)]
        + [pltpu.VMEM(x.shape, x.dtype) for x in small[:4]]
        + [
            pltpu.VMEM((channels // LANES, LANES), jnp.int32),
            pltpu.VMEM((8, LANES), jnp.float32),
            pltpu.SemaphoreType.DMA((1 + len(sources),)),
        ],
        10**9,
    )
    own_part = window[:3]
    table, near, far = window[3:6]
    responses = call(
        functools.partial(response_kernel, wires_by_plane),
        [shape((2 * LANES, 2 * padded(w // 2)), jnp.bfloat16) for w in wires_by_plane],
        list(window[6:]),
        [vm] * 8,
        [],
        10**9,
    )

    received = []
    for name, first in (("first", 0), ("last", parts[0])):
        halo = halos["other", name]
        (other,) = call(
            functools.partial(other_kernel, first),
            [shape(halo.shape, halo.dtype)],
            [side_word, halo, table, *own_part],
            [sm] + [vm] * 5,
            [],
            10**8,
        )
        received.append(lax.ppermute(other, "apa", [(0, 1), (1, 0)]))
    (placed,) = call(
        middle_kernel,
        [shape((channels, LANES), jnp.float32)],
        [side_word, near, far, received[0], halos["own", "first"], table, *own_part],
        [sm] + [vm] * 8,
        [
            pltpu.VMEM((parts[0], LANES), jnp.float32),
            pltpu.VMEM((parts[0], LANES), jnp.float32),
            pltpu.SMEM(slot_shape.shape, jnp.int32),
            pltpu.SMEM(slot_shape.shape, jnp.int32),
            pltpu.SemaphoreType.DMA((2,)),
        ],
        10**8,
    )

    layout = []
    start = 0
    for wires in wires_by_plane:
        layout.append((start, wires))
        start += wires
    return call(
        functools.partial(final_kernel, layout, parts[0]),
        [shape((channels, LANES), jnp.float32)] * 2,
        [side_word, near, far, received[1], halos["own", "last"], table, *own_part, placed, *responses],
        [sm] + [vm] * 12,
        [
            pltpu.VMEM((parts[1], LANES), jnp.float32),
            pltpu.VMEM((parts[1], LANES), jnp.float32),
            pltpu.VMEM((channels, LANES), jnp.float32),
            pltpu.SMEM(slot_shape.shape, jnp.int32),
            pltpu.SMEM(slot_shape.shape, jnp.int32),
            pltpu.SemaphoreType.DMA((5,)),
        ],
        10**9,
        out_specs=[pl.BlockSpec(memory_space=pl.ANY), vm],
        input_output_aliases={9: 1},
    )[0]


def solution(mesh):
    placed = (P(("grp", "apa"), "tm"), P(), P("grp"), P("grp"), P("grp")) + (P(),) * 6
    return jax.shard_map(
        deconvolve, mesh=mesh, in_specs=placed, out_specs=P("grp", ("tm", "apa")), check_vma=False
    )
```

time: 21.1 us -> 21.2 us (level)
  starting transfers between devices: 4.71 us -> 9.01 us
  Pallas kernels: 13.5 us -> 9.45 us
  waiting for transfers between devices: 2.66 us -> 2.42 us
    ppermute x4 -> x6, starting transfers between devices: 4.71 us -> 9.01 us  [the longest x4 6.62 us: deconvolve(): halos[whose, name] = lax.ppermute(part, axes, onward(core))]
    pallas_call x7, Pallas kernels: 13.5 us -> 9.45 us  [call(): pl.pallas_call(kernel, out_shape=outs, in_specs=specs, out_specs=more.pop...]
    ppermute x4 -> x6, waiting for transfers between devices: 2.66 us -> 2.42 us  [the longest x4 2.42 us: deconvolve(): halos[whose, name] = lax.ppermute(part, axes, onward(core))]
  transfers between devices with their start and end apart: 4 -> 6, of which waited for: 2 -> 2; matrix products, arithmetic and copies ran while one was open for 0% -> 0% of each run, Pallas kernels for 46% -> 26%
where the time goes in v4:
time: 21.2 us; the launch traced here: 21 us
  Pallas kernels  9.45 us (45%)
  starting transfers between devices  9.01 us (42%)
  waiting for transfers between devices  2.42 us (11%)
    pallas_call x7, Pallas kernels, call(): pl.pallas_call(kernel, out_shape=outs, in_specs=specs, out_specs=more.pop...  9.45 us
    ppermute x4, starting transfers between devices, deconvolve(): halos[whose, name] = lax.ppermute(part, axes, onward(core))  6.62 us
    ppermute x4, waiting for transfers between devices, deconvolve(): halos[whose, name] = lax.ppermute(part, axes, onward(core))  2.42 us
    ppermute x2, starting transfers between devices, deconvolve(): received.append(lax.ppermute(other, 'apa', [(0, 1), (1, 0)]))  2.39 us
  transfers between devices with their start and end apart: 6, of which 2 were waited for; matrix products, arithmetic and copies ran while one was open for 0% of the time, Pallas kernels for 26%

profile of v4, /device:TPU:0, one launch (start us, length us, event | category | flops | bytes accessed | tf_op | source)
XLA Modules:
  0.0 21.0 jit_solution(15653138160396776849)
XLA Ops:
  0.0 1.0 %shard_map.127 = (bf16[768,128]{1,0:T(8,128)(2,1)S(1)}, bf16[512,128]{1,0:T(8,128)(2,1)S(1)}) custom-call(bf16[1280,256]{1,0:T(8,128)(2,1)} %wave.3), custom_call_target="tpu_custom_call" | custom-call | flops 100000 | bytes 1000000 | tf_op jit(solution)/shard_map/pallas_call | solution.py:356
  1.0 3.0 %collective-permute-start.3 = (bf16[768,128]{1,0:T(8,128)(2,1)S(1)}, bf16[768,128]{1,0:T(8,128)(2,1)S(1)}, u32[]{:S(2)}, u32[]{:S(2)}) collective-permute-start(bf16[768,128]{1,0:T(8,128)(2,1)S(1)} %get-tuple-element.25.first_tail), channel_id=1, source_target_pairs={{1,3},{0,16},{3,5},{2,18},{5,7},{4,20},{7,9},{6,22},{9,11},{8,24},... | collective-permute-start | bytes 589832 | tf_op jit(solution)/shard_map/ppermute | solution.py:409
  4.1 1.5 %collective-permute-start.5 = (bf16[768,128]{1,0:T(8,128)(2,1)S(1)}, bf16[768,128]{1,0:T(8,128)(2,1)S(1)}, u32[]{:S(2)}, u32[]{:S(2)}) collective-permute-start(bf16[768,128]{1,0:T(8,128)(2,1)S(1)} %get-tuple-element.25.first_tail), channel_id=1, source_target_pairs={{0,2},{1,17},{2,4},{3,19},{4,6},{5,21},{6,8},{7,23},{8,10},{9,25},... | collective-permute-start | bytes 589832 | tf_op jit(solution)/shard_map/ppermute | solution.py:409
  5.6 0.5 %collective-permute-start = (bf16[512,128]{1,0:T(8,128)(2,1)S(1)}, bf16[512,128]{1,0:T(8,128)(2,1)S(1)}, u32[]{:S(2)}, u32[]{:S(2)}) collective-permute-start(bf16[512,128]{1,0:T(8,128)(2,1)S(1)} %get-tuple-element.26.last_tail), channel_id=1, source_target_pairs={{1,3},{0,16},{3,5},{2,18},{5,7},{4,20},{7,9},{6,22},{9,11},{8,24},... | collective-permute-start | bytes 393224 | tf_op jit(solution)/shard_map/ppermute | solution.py:409
  6.1 2.4 %shard_map.128 = (bf16[1280,128]{1,0:T(8,128)(2,1)S(1)}, f32[1280,128]{1,0:T(8,128)S(1)}, s32[1280,128]{1,0:T(8,128)S(1)}, bf16[256,384]{1,0:T(8,128)(2,1)S(1)},...) custom-call(s32[1]{0:T(128)} %bitcast.side, ...), custom_call_target="tpu_custom_call" | custom-call | flops 1000000000 | bytes 1000000 | tf_op jit(solution)/shard_map/pallas_call | solution.py:356
  8.5 0.8 %collective-permute-done.3.halo = bf16[768,128]{1,0:T(8,128)(2,1)S(1)} collective-permute-done((bf16[768,128]{1,0:T(8,128)(2,1)S(1)}, bf16[768,128]{1,0:T(8,128)(2,1)S(1)}, u32[]{:S(2)}, u32[]{:S(2)}) %collective-permute-start.3) | collective-permute-done | bytes 196640 | tf_op jit(solution)/shard_map/ppermute | solution.py:409
  9.3 0.9 %collective-permute-start.4 = (bf16[768,128]{1,0:T(8,128)(2,1)S(1)}, bf16[768,128]{1,0:T(8,128)(2,1)S(1)}, u32[]{:S(2)}, u32[]{:S(2)}) collective-permute-start(bf16[768,128]{1,0:T(8,128)(2,1)S(1)} %shard_map.130), channel_id=1, source_target_pairs={{0,1},{1,0},{2,3},{3,2},{4,5},{5,4},{6,7},{7,6},{8,9},{9,8},{10,11... | collective-permute-start | bytes 589832 | tf_op jit(solution)/shard_map/ppermute | solution.py:458
  10.3 1.6 %collective-permute-start.2 = (bf16[512,128]{1,0:T(8,128)(2,1)S(1)}, bf16[512,128]{1,0:T(8,128)(2,1)S(1)}, u32[]{:S(2)}, u32[]{:S(2)}) collective-permute-start(bf16[512,128]{1,0:T(8,128)(2,1)S(1)} %get-tuple-element.26.last_tail), channel_id=1, source_target_pairs={{0,2},{1,17},{2,4},{3,19},{4,6},{5,21},{6,8},{7,23},{8,10},{9,25},... | collective-permute-start | bytes 393224 | tf_op jit(solution)/shard_map/ppermute | solution.py:409
  11.8 0.0 collective-permute-done.halo
  11.9 1.4 %collective-permute-start.1 = (bf16[512,128]{1,0:T(8,128)(2,1)S(1)}, bf16[512,128]{1,0:T(8,128)(2,1)S(1)}, u32[]{:S(2)}, u32[]{:S(2)}) collective-permute-start(bf16[512,128]{1,0:T(8,128)(2,1)S(1)} %shard_map.129), channel_id=1, source_target_pairs={{0,1},{1,0},{2,3},{3,2},{4,5},{5,4},{6,7},{7,6},{8,9},{9,8},{10,11... | collective-permute-start | bytes 393224 | tf_op jit(solution)/shard_map/ppermute | solution.py:458
  13.3 1.4 %shard_map.132 = (bf16[256,1024]{1,0:T(8,128)(2,1)S(1)}, bf16[256,1024]{1,0:T(8,128)(2,1)S(1)}, bf16[256,1024]{1,0:T(8,128)(2,1)S(1)}) custom-call(f32[2,800]{1,0:T(2,128)S(1)} %get-tuple-element.33.refs_0_, f32[2,800]{1,0:T(2,128)S(1)} %get-tuple-element.34.refs_1_, f32[2,800]{1,0:T(2,128)S(1)} %get-tuple-element.35.refs_2_, ...), custom_call_target="tpu_custom_call" | custom-call | flops 1000000000 | bytes 1000000 | tf_op jit(solution)/shard_map/pallas_call | solution.py:356
  14.7 0.0 collective-permute-done.5.halo
  14.7 0.0 collective-permute-done.4.other
  14.8 1.5 %shard_map.131.before = f32[2560,128]{1,0:T(8,128)S(1)} custom-call(s32[1]{0:T(128)} %bitcast.side, s32[10,128]{1,0:T(8,128)S(1)} %get-tuple-element.27.near, s32[10,128]{1,0:T(8,128)S(1)} %get-tuple-element.28.far, bf16[768,128]{1,0:T(8,128)(2,1)S(1)} %collective-permute-done.4.other, bf16[768,128]{1,0:T(8,128)(2,1)S(1)} %collective-permute-done.5.halo, ...), custom_call_target="tpu_custom_call" | custom-call | flops 100000000 | bytes 1000000 | tf_op jit(solution)/shard_map/pallas_call | solution.py:356
  16.3 1.6 %collective-permute-done.2.halo = bf16[512,128]{1,0:T(8,128)(2,1)S(1)} collective-permute-done((bf16[512,128]{1,0:T(8,128)(2,1)S(1)}, bf16[512,128]{1,0:T(8,128)(2,1)S(1)}, u32[]{:S(2)}, u32[]{:S(2)}) %collective-permute-start.2) | collective-permute-done | bytes 131104 | tf_op jit(solution)/shard_map/ppermute | solution.py:409
  17.9 0.0 collective-permute-done.1.other
  17.9 3.0 %shard_map.133 = (f32[2560,128]{1,0:T(8,128)}, f32[2560,128]{1,0:T(8,128)S(1)}) custom-call(s32[1]{0:T(128)} %bitcast.side, s32[10,128]{1,0:T(8,128)S(1)} %get-tuple-element.27.near, s32[10,128]{1,0:T(8,128)S(1)} %get-tuple-element.28.far, bf16[512,128]{1,0:T(8,128)(2,1)S(1)} %collective-permute-done.1.other, ...), custom_call_target="tpu_custom_call", output_to_operand_aliasing={{1}: (9, {})} | custom-call | flops 1000000000 | bytes 1000000 | tf_op jit(solution)/shard_map/pallas_call | solution.py:356
  (2 shorter events, 0.0 us)
Async XLA Ops:
  1.0 8.3 %collective-permute-start.3 = (bf16[768,128]{1,0:T(8,128)(2,1)S(1)}, bf16[768,128]{1,0:T(8,128)(2,1)S(1)}, u32[]{:S(2)}, u32[]{:S(2)}) collective-permute-start(bf16[768,128]{1,0:T(8,128)(2,1)S(1)} %get-tuple-element.25.first_tail), channel_id=1, source_target_pairs={{1,3},{0,16},{3,5},{2,18},{5,7},{4,20},{7,9},{6,22},{9,11},{8,24},... | collective-permute-start | bytes 589832 | tf_op jit(solution)/shard_map/ppermute | solution.py:409
  4.1 10.7 %collective-permute-start.5 = (bf16[768,128]{1,0:T(8,128)(2,1)S(1)}, bf16[768,128]{1,0:T(8,128)(2,1)S(1)}, u32[]{:S(2)}, u32[]{:S(2)}) collective-permute-start(bf16[768,128]{1,0:T(8,128)(2,1)S(1)} %get-tuple-element.25.first_tail), channel_id=1, source_target_pairs={{0,2},{1,17},{2,4},{3,19},{4,6},{5,21},{6,8},{7,23},{8,10},{9,25},... | collective-permute-start | bytes 589832 | tf_op jit(solution)/shard_map/ppermute | solution.py:409
  5.6 6.3 %collective-permute-start = (bf16[512,128]{1,0:T(8,128)(2,1)S(1)}, bf16[512,128]{1,0:T(8,128)(2,1)S(1)}, u32[]{:S(2)}, u32[]{:S(2)}) collective-permute-start(bf16[512,128]{1,0:T(8,128)(2,1)S(1)} %get-tuple-element.26.last_tail), channel_id=1, source_target_pairs={{1,3},{0,16},{3,5},{2,18},{5,7},{4,20},{7,9},{6,22},{9,11},{8,24},... | collective-permute-start | bytes 393224 | tf_op jit(solution)/shard_map/ppermute | solution.py:409
  9.3 5.4 %collective-permute-start.4 = (bf16[768,128]{1,0:T(8,128)(2,1)S(1)}, bf16[768,128]{1,0:T(8,128)(2,1)S(1)}, u32[]{:S(2)}, u32[]{:S(2)}) collective-permute-start(bf16[768,128]{1,0:T(8,128)(2,1)S(1)} %shard_map.130), channel_id=1, source_target_pairs={{0,1},{1,0},{2,3},{3,2},{4,5},{5,4},{6,7},{7,6},{8,9},{9,8},{10,11... | collective-permute-start | bytes 589832 | tf_op jit(solution)/shard_map/ppermute | solution.py:458
  10.3 7.7 %collective-permute-start.2 = (bf16[512,128]{1,0:T(8,128)(2,1)S(1)}, bf16[512,128]{1,0:T(8,128)(2,1)S(1)}, u32[]{:S(2)}, u32[]{:S(2)}) collective-permute-start(bf16[512,128]{1,0:T(8,128)(2,1)S(1)} %get-tuple-element.26.last_tail), channel_id=1, source_target_pairs={{0,2},{1,17},{2,4},{3,19},{4,6},{5,21},{6,8},{7,23},{8,10},{9,25},... | collective-permute-start | bytes 393224 | tf_op jit(solution)/shard_map/ppermute | solution.py:409
  11.9 6.1 %collective-permute-start.1 = (bf16[512,128]{1,0:T(8,128)(2,1)S(1)}, bf16[512,128]{1,0:T(8,128)(2,1)S(1)}, u32[]{:S(2)}, u32[]{:S(2)}) collective-permute-start(bf16[512,128]{1,0:T(8,128)(2,1)S(1)} %shard_map.129), channel_id=1, source_target_pairs={{0,1},{1,0},{2,3},{3,2},{4,5},{5,4},{6,7},{7,6},{8,9},{9,8},{10,11... | collective-permute-start | bytes 393224 | tf_op jit(solution)/shard_map/ppermute | solution.py:458

commit v5 on v4

--- a/solution.py
+++ b/solution.py
@@ -16,7 +16,7 @@
 SMEM = pltpu.SMEM
 KERNEL_VMEM = 16 * 2**20
 STEP = 256
-LAST_ROWS = 512
+LAST_ROWS = 384
 
 
 def padded(count):
@@ -217,7 +217,7 @@
 
 
 def finish_early(halo, code, table, low_main, write):
-    step = STEP
+    step = math.gcd(halo.shape[0], STEP)
 
     def body(i, carry):
         rows = pl.ds(pl.multiple_of(i * step, step), step)
@@ -266,16 +266,21 @@
         target[pl.ds(slot, 1), :] = wide[k : k + 1, :]
 
 
-def middle_kernel(side, near, far, other, halo, table, high, low_main, code, target, *refs):
-    wide, wide_other, near_slots, far_slots, sems = refs
-    loads = start_all([(near, near_slots), (far, far_slots)], sems)
-    count = halo.shape[0]
-    wide_other[...] = other[...].astype(jnp.float32)
-    finish_own(side, halo, table, high.at[pl.ds(0, count)], low_main, code, wide)
-    for load in loads:
-        load.wait()
-    place_rows(count, wide_other, far_slots, 0, target)
-    place_rows(count, wide, near_slots, 0, target)
+def place_kernel(far, other, target, wide, slots, sem):
+    copy = pltpu.make_async_copy(far, slots, sem.at[0])
+    copy.start()
+    wide[...] = other[...].astype(jnp.float32)
+    copy.wait()
+    place_rows(other.shape[0], wide, slots, 0, target)
+
+
+def own_kernel(side, near, halo, table, high, low_main, code, before, target, wide, slots, sem):
+    del before
+    copy = pltpu.make_async_copy(near, slots, sem.at[0])
+    copy.start()
+    finish_own(side, halo, table, high.at[pl.ds(0, halo.shape[0])], low_main, code, wide)
+    copy.wait()
+    place_rows(halo.shape[0], wide, slots, 0, target)
 
 
 def final_kernel(layout, first, side, near, far, other, halo, table, high, low_main, code, before, *refs):
@@ -456,19 +461,27 @@
             10**8,
         )
         received.append(lax.ppermute(other, "apa", [(0, 1), (1, 0)]))
+    placing = [
+        pltpu.VMEM((parts[0], LANES), jnp.float32),
+        pltpu.SMEM(slot_shape.shape, jnp.int32),
+        pltpu.SemaphoreType.DMA((1,)),
+    ]
     (placed,) = call(
-        middle_kernel,
+        place_kernel,
         [shape((channels, LANES), jnp.float32)],
-        [side_word, near, far, received[0], halos["own", "first"], table, *own_part],
-        [sm] + [vm] * 8,
-        [
-            pltpu.VMEM((parts[0], LANES), jnp.float32),
-            pltpu.VMEM((parts[0], LANES), jnp.float32),
-            pltpu.SMEM(slot_shape.shape, jnp.int32),
-            pltpu.SMEM(slot_shape.shape, jnp.int32),
-            pltpu.SemaphoreType.DMA((2,)),
-        ],
+        [far, received[0]],
+        [vm] * 2,
+        placing,
         10**8,
+    )
+    (placed,) = call(
+        own_kernel,
+        [shape((channels, LANES), jnp.float32)],
+        [side_word, near, halos["own", "first"], table, *own_part, placed],
+        [sm] + [vm] * 7,
+        placing,
+        10**8,
+        input_output_aliases={7: 0},
     )
 
     layout = []

time: 21.2 us -> 26.7 us (1.26)
  starting transfers between devices: 9.01 us -> 11.8 us
  waiting for transfers between devices: 2.42 us -> 4.47 us
  Pallas kernels: 9.45 us -> 10.1 us
    ppermute x2, starting transfers between devices: 2.39 us -> 6.12 us  [deconvolve(): received.append(lax.ppermute(other, 'apa', [(0, 1), (1, 0)]))]
    ppermute x4, waiting for transfers between devices: 2.42 us -> 4.47 us  [deconvolve(): halos[whose, name] = lax.ppermute(part, axes, onward(core))]
    ppermute x4, starting transfers between devices: 6.62 us -> 5.72 us  [deconvolve(): halos[whose, name] = lax.ppermute(part, axes, onward(core))]
    pallas_call x7 -> x8, Pallas kernels: 9.45 us -> 10.1 us  [call(): pl.pallas_call(kernel, out_shape=outs, in_specs=specs, out_specs=more.pop...]
  transfers between devices with their start and end apart: 6 -> 6, of which waited for: 2 -> 2; matrix products, arithmetic and copies ran while one was open for 0% -> 0% of each run, Pallas kernels for 26% -> 23%
where the time goes in v5:
time: 26.7 us; the launch traced here: 26.5 us
  starting transfers between devices  11.8 us (44%)
  Pallas kernels  10.1 us (38%)
  waiting for transfers between devices  4.47 us (17%)
    pallas_call x8, Pallas kernels, call(): pl.pallas_call(kernel, out_shape=outs, in_specs=specs, out_specs=more.pop...  10.1 us
    ppermute x2, starting transfers between devices, deconvolve(): received.append(lax.ppermute(other, 'apa', [(0, 1), (1, 0)]))  6.12 us
    ppermute x4, starting transfers between devices, deconvolve(): halos[whose, name] = lax.ppermute(part, axes, onward(core))  5.72 us
    ppermute x4, waiting for transfers between devices, deconvolve(): halos[whose, name] = lax.ppermute(part, axes, onward(core))  4.47 us
  transfers between devices with their start and end apart: 6, of which 2 were waited for; matrix products, arithmetic and copies ran while one was open for 0% of the time, Pallas kernels for 23%

profile of v5, /device:TPU:0, one launch (start us, length us, event | category | flops | bytes accessed | tf_op | source)
XLA Modules:
  0.0 26.5 jit_solution(7567365413608671480)
XLA Ops:
  0.0 1.0 %shard_map.127 = (bf16[896,128]{1,0:T(8,128)(2,1)S(1)}, bf16[384,128]{1,0:T(8,128)(2,1)S(1)}) custom-call(bf16[1280,256]{1,0:T(8,128)(2,1)} %wave.3), custom_call_target="tpu_custom_call" | custom-call | flops 100000 | bytes 1000000 | tf_op jit(solution)/shard_map/pallas_call | solution.py:361
  1.0 3.0 %collective-permute-start.4 = (bf16[896,128]{1,0:T(8,128)(2,1)S(1)}, bf16[896,128]{1,0:T(8,128)(2,1)S(1)}, u32[]{:S(2)}, u32[]{:S(2)}) collective-permute-start(bf16[896,128]{1,0:T(8,128)(2,1)S(1)} %get-tuple-element.25.first_tail), channel_id=1, source_target_pairs={{1,3},{0,16},{3,5},{2,18},{5,7},{4,20},{7,9},{6,22},{9,11},{8,24},... | collective-permute-start | bytes 688136 | tf_op jit(solution)/shard_map/ppermute | solution.py:414
  4.1 2.5 %shard_map.128 = (bf16[1280,128]{1,0:T(8,128)(2,1)S(1)}, f32[1280,128]{1,0:T(8,128)S(1)}, s32[1280,128]{1,0:T(8,128)S(1)}, bf16[256,384]{1,0:T(8,128)(2,1)S(1)},...) custom-call(s32[1]{0:T(128)} %bitcast.side, ...), custom_call_target="tpu_custom_call" | custom-call | flops 1000000000 | bytes 1000000 | tf_op jit(solution)/shard_map/pallas_call | solution.py:361
  6.6 1.5 %collective-permute-done.4.halo = bf16[896,128]{1,0:T(8,128)(2,1)S(1)} collective-permute-done((bf16[896,128]{1,0:T(8,128)(2,1)S(1)}, bf16[896,128]{1,0:T(8,128)(2,1)S(1)}, u32[]{:S(2)}, u32[]{:S(2)}) %collective-permute-start.4) | collective-permute-done | bytes 229408 | tf_op jit(solution)/shard_map/ppermute | solution.py:414
  8.1 2.6 %collective-permute-start.5 = (bf16[896,128]{1,0:T(8,128)(2,1)S(1)}, bf16[896,128]{1,0:T(8,128)(2,1)S(1)}, u32[]{:S(2)}, u32[]{:S(2)}) collective-permute-start(bf16[896,128]{1,0:T(8,128)(2,1)S(1)} %shard_map.130), channel_id=1, source_target_pairs={{0,1},{1,0},{2,3},{3,2},{4,5},{5,4},{6,7},{7,6},{8,9},{9,8},{10,11... | collective-permute-start | bytes 688136 | tf_op jit(solution)/shard_map/ppermute | solution.py:463
  10.7 0.0 collective-permute-start.3
  10.7 1.5 %collective-permute-start = (bf16[384,128]{1,0:T(8,128)(2,1)S(1)}, bf16[384,128]{1,0:T(8,128)(2,1)S(1)}, u32[]{:S(2)}, u32[]{:S(2)}) collective-permute-start(bf16[384,128]{1,0:T(8,128)(2,1)S(1)} %get-tuple-element.26.last_tail), channel_id=1, source_target_pairs={{1,3},{0,16},{3,5},{2,18},{5,7},{4,20},{7,9},{6,22},{9,11},{8,24},... | collective-permute-start | bytes 294920 | tf_op jit(solution)/shard_map/ppermute | solution.py:414
  12.2 1.1 %collective-permute-start.2 = (bf16[384,128]{1,0:T(8,128)(2,1)S(1)}, bf16[384,128]{1,0:T(8,128)(2,1)S(1)}, u32[]{:S(2)}, u32[]{:S(2)}) collective-permute-start(bf16[384,128]{1,0:T(8,128)(2,1)S(1)} %get-tuple-element.26.last_tail), channel_id=1, source_target_pairs={{0,2},{1,17},{2,4},{3,19},{4,6},{5,21},{6,8},{7,23},{8,10},{9,25},... | collective-permute-start | bytes 294920 | tf_op jit(solution)/shard_map/ppermute | solution.py:414
  13.3 3.0 %collective-permute-done.halo = bf16[384,128]{1,0:T(8,128)(2,1)S(1)} collective-permute-done((bf16[384,128]{1,0:T(8,128)(2,1)S(1)}, bf16[384,128]{1,0:T(8,128)(2,1)S(1)}, u32[]{:S(2)}, u32[]{:S(2)}) %collective-permute-start) | collective-permute-done | bytes 98336 | tf_op jit(solution)/shard_map/ppermute | solution.py:414
  16.3 3.6 %collective-permute-start.1 = (bf16[384,128]{1,0:T(8,128)(2,1)S(1)}, bf16[384,128]{1,0:T(8,128)(2,1)S(1)}, u32[]{:S(2)}, u32[]{:S(2)}) collective-permute-start(bf16[384,128]{1,0:T(8,128)(2,1)S(1)} %shard_map.129), channel_id=1, source_target_pairs={{0,1},{1,0},{2,3},{3,2},{4,5},{5,4},{6,7},{7,6},{8,9},{9,8},{10,11... | collective-permute-start | bytes 294920 | tf_op jit(solution)/shard_map/ppermute | solution.py:463
  19.9 1.4 %shard_map.133 = (bf16[256,1024]{1,0:T(8,128)(2,1)S(1)}, bf16[256,1024]{1,0:T(8,128)(2,1)S(1)}, bf16[256,1024]{1,0:T(8,128)(2,1)S(1)}) custom-call(f32[2,800]{1,0:T(2,128)S(1)} %get-tuple-element.33.refs_0_, f32[2,800]{1,0:T(2,128)S(1)} %get-tuple-element.34.refs_1_, f32[2,800]{1,0:T(2,128)S(1)} %get-tuple-element.35.refs_2_, ...), custom_call_target="tpu_custom_call" | custom-call | flops 1000000000 | bytes 1000000 | tf_op jit(solution)/shard_map/pallas_call | solution.py:361
  21.3 0.0 collective-permute-done.5.other
  21.3 1.1 %shard_map.131.before = f32[2560,128]{1,0:T(8,128)S(1)} custom-call(s32[10,128]{1,0:T(8,128)S(1)} %get-tuple-element.28.far, bf16[896,128]{1,0:T(8,128)(2,1)S(1)} %collective-permute-done.5.other), custom_call_target="tpu_custom_call" | custom-call | flops 100000000 | bytes 1000000 | tf_op jit(solution)/shard_map/pallas_call | solution.py:361
  22.4 0.0 collective-permute-done.3.halo
  22.5 1.1 %shard_map.132.before = f32[2560,128]{1,0:T(8,128)S(1)} custom-call(s32[1]{0:T(128)} %bitcast.side, s32[10,128]{1,0:T(8,128)S(1)} %get-tuple-element.27.near, bf16[896,128]{1,0:T(8,128)(2,1)S(1)} %collective-permute-done.3.halo, bf16[256,384]{1,0:T(8,128)(2,1)S(1)} %get-tuple-element.29.table, ...), custom_call_target="tpu_custom_call", output_to_operand_aliasing={{}: (7, {})} | custom-call | flops 100000000 | bytes 1000000 | tf_op jit(solution)/shard_map/pallas_call | solution.py:361
  23.6 0.0 collective-permute-done.2.halo
  23.6 0.0 collective-permute-done.1.other
  23.6 2.9 %shard_map.134 = (f32[2560,128]{1,0:T(8,128)}, f32[2560,128]{1,0:T(8,128)S(1)}) custom-call(s32[1]{0:T(128)} %bitcast.side, s32[10,128]{1,0:T(8,128)S(1)} %get-tuple-element.27.near, s32[10,128]{1,0:T(8,128)S(1)} %get-tuple-element.28.far, bf16[384,128]{1,0:T(8,128)(2,1)S(1)} %collective-permute-done.1.other, ...), custom_call_target="tpu_custom_call", output_to_operand_aliasing={{1}: (9, {})} | custom-call | flops 1000000000 | bytes 1000000 | tf_op jit(solution)/shard_map/pallas_call | solution.py:361
  (2 shorter events, 0.0 us)
Async XLA Ops:
  1.0 7.0 %collective-permute-start.4 = (bf16[896,128]{1,0:T(8,128)(2,1)S(1)}, bf16[896,128]{1,0:T(8,128)(2,1)S(1)}, u32[]{:S(2)}, u32[]{:S(2)}) collective-permute-start(bf16[896,128]{1,0:T(8,128)(2,1)S(1)} %get-tuple-element.25.first_tail), channel_id=1, source_target_pairs={{1,3},{0,16},{3,5},{2,18},{5,7},{4,20},{7,9},{6,22},{9,11},{8,24},... | collective-permute-start | bytes 688136 | tf_op jit(solution)/shard_map/ppermute | solution.py:414
  8.1 13.2 %collective-permute-start.5 = (bf16[896,128]{1,0:T(8,128)(2,1)S(1)}, bf16[896,128]{1,0:T(8,128)(2,1)S(1)}, u32[]{:S(2)}, u32[]{:S(2)}) collective-permute-start(bf16[896,128]{1,0:T(8,128)(2,1)S(1)} %shard_map.130), channel_id=1, source_target_pairs={{0,1},{1,0},{2,3},{3,2},{4,5},{5,4},{6,7},{7,6},{8,9},{9,8},{10,11... | collective-permute-start | bytes 688136 | tf_op jit(solution)/shard_map/ppermute | solution.py:463
  10.7 11.8 %collective-permute-start.3 = (bf16[896,128]{1,0:T(8,128)(2,1)S(1)}, bf16[896,128]{1,0:T(8,128)(2,1)S(1)}, u32[]{:S(2)}, u32[]{:S(2)}) collective-permute-start(bf16[896,128]{1,0:T(8,128)(2,1)S(1)} %get-tuple-element.25.first_tail), channel_id=1, source_target_pairs={{0,2},{1,17},{2,4},{3,19},{4,6},{5,21},{6,8},{7,23},{8,10},{9,25},... | collective-permute-start | bytes 688136 | tf_op jit(solution)/shard_map/ppermute | solution.py:414
  10.7 5.7 %collective-permute-start = (bf16[384,128]{1,0:T(8,128)(2,1)S(1)}, bf16[384,128]{1,0:T(8,128)(2,1)S(1)}, u32[]{:S(2)}, u32[]{:S(2)}) collective-permute-start(bf16[384,128]{1,0:T(8,128)(2,1)S(1)} %get-tuple-element.26.last_tail), channel_id=1, source_target_pairs={{1,3},{0,16},{3,5},{2,18},{5,7},{4,20},{7,9},{6,22},{9,11},{8,24},... | collective-permute-start | bytes 294920 | tf_op jit(solution)/shard_map/ppermute | solution.py:414
  12.2 11.4 %collective-permute-start.2 = (bf16[384,128]{1,0:T(8,128)(2,1)S(1)}, bf16[384,128]{1,0:T(8,128)(2,1)S(1)}, u32[]{:S(2)}, u32[]{:S(2)}) collective-permute-start(bf16[384,128]{1,0:T(8,128)(2,1)S(1)} %get-tuple-element.26.last_tail), channel_id=1, source_target_pairs={{0,2},{1,17},{2,4},{3,19},{4,6},{5,21},{6,8},{7,23},{8,10},{9,25},... | collective-permute-start | bytes 294920 | tf_op jit(solution)/shard_map/ppermute | solution.py:414
  16.3 7.2 %collective-permute-start.1 = (bf16[384,128]{1,0:T(8,128)(2,1)S(1)}, bf16[384,128]{1,0:T(8,128)(2,1)S(1)}, u32[]{:S(2)}, u32[]{:S(2)}) collective-permute-start(bf16[384,128]{1,0:T(8,128)(2,1)S(1)} %shard_map.129), channel_id=1, source_target_pairs={{0,1},{1,0},{2,3},{3,2},{4,5},{5,4},{6,7},{7,6},{8,9},{9,8},{10,11... | collective-permute-start | bytes 294920 | tf_op jit(solution)/shard_map/ppermute | solution.py:463

commit v6 on v5

--- a/solution.py
+++ b/solution.py
@@ -15,8 +15,12 @@
 VMEM = pltpu.VMEM
 SMEM = pltpu.SMEM
 KERNEL_VMEM = 16 * 2**20
-STEP = 256
+BLOCKS = (448, 384, 320, 256, 128)
 LAST_ROWS = 384
+
+
+def block_rows(count):
+    return next(size for size in BLOCKS if count % size == 0)
 
 
 def padded(count):
@@ -176,7 +180,7 @@
 
     first = 0
     for tail in tails:
-        step = math.gcd(tail.shape[0], STEP)
+        step = block_rows(tail.shape[0])
         for top in range(0, tail.shape[0], step):
             rows = slice(first + top, first + top + step)
             word = code_out[rows, :]
@@ -217,7 +221,7 @@
 
 
 def finish_early(halo, code, table, low_main, write):
-    step = math.gcd(halo.shape[0], STEP)
+    step = block_rows(halo.shape[0])
 
     def body(i, carry):
         rows = pl.ds(pl.multiple_of(i * step, step), step)
@@ -309,16 +313,20 @@
         back = ordered[start + half : start + wires, :]
         total = (front + back).astype(jnp.bfloat16)
         change = (front - back).astype(jnp.bfloat16)
-        for block in range(base // LANES):
-            valid = min(LANES, half - block * LANES)
-            columns = slice(base - block * LANES, base - block * LANES + half)
-            even = jnp.dot(resp[:valid, columns], total, preferred_element_type=jnp.float32)
-            odd = jnp.dot(
-                resp[LANES : LANES + valid, columns], change, preferred_element_type=jnp.float32
-            )
-            top = start + block * LANES
-            mixed[top : top + valid, :] = even + odd
-            mixed[top + half : top + half + valid, :] = even - odd
+        sizes = [min(LANES, half - top) for top in range(0, half, LANES)]
+
+        def rows_of(part):
+            lefts = [base - block * LANES for block in range(len(sizes))]
+            pieces = [
+                resp[part * LANES : part * LANES + size, left : left + half]
+                for size, left in zip(sizes, lefts)
+            ]
+            return jnp.concatenate(pieces, 0)
+
+        even = jnp.dot(rows_of(0), total, preferred_element_type=jnp.float32)
+        odd = jnp.dot(rows_of(1), change, preferred_element_type=jnp.float32)
+        mixed[start : start + half, :] = even + odd
+        mixed[start + half : start + wires, :] = even - odd
         span = pl.ds(start, wires)
         copies.append(pltpu.make_async_copy(mixed.at[span], out.at[span], sems.at[2 + len(copies)]))
         copies[-1].start()

time: 26.7 us -> 26.5 us (level)
  no operation moved by 1% of the time
where the time goes in v6:
time: 26.5 us; the launch traced here: 26.3 us
  starting transfers between devices  11.8 us (45%)
  Pallas kernels  9.93 us (37%)
  waiting for transfers between devices  4.52 us (17%)
    pallas_call x8, Pallas kernels, call(): pl.pallas_call(kernel, out_shape=outs, in_specs=specs, out_specs=more.pop...  9.93 us
    ppermute x2, starting transfers between devices, deconvolve(): received.append(lax.ppermute(other, 'apa', [(0, 1), (1, 0)]))  6.08 us
    ppermute x4, starting transfers between devices, deconvolve(): halos[whose, name] = lax.ppermute(part, axes, onward(core))  5.72 us
    ppermute x4, waiting for transfers between devices, deconvolve(): halos[whose, name] = lax.ppermute(part, axes, onward(core))  4.51 us
  transfers between devices with their start and end apart: 6, of which 2 were waited for; matrix products, arithmetic and copies ran while one was open for 0% of the time, Pallas kernels for 23%

profile of v6, /device:TPU:0, one launch (start us, length us, event | category | flops | bytes accessed | tf_op | source)
XLA Modules:
  0.0 26.3 jit_solution(4089385454375600623)
XLA Ops:
  0.0 1.0 %shard_map.127 = (bf16[896,128]{1,0:T(8,128)(2,1)S(1)}, bf16[384,128]{1,0:T(8,128)(2,1)S(1)}) custom-call(bf16[1280,256]{1,0:T(8,128)(2,1)} %wave.3), custom_call_target="tpu_custom_call" | custom-call | flops 100000 | bytes 1000000 | tf_op jit(solution)/shard_map/pallas_call | solution.py:369
  1.0 3.0 %collective-permute-start.4 = (bf16[896,128]{1,0:T(8,128)(2,1)S(1)}, bf16[896,128]{1,0:T(8,128)(2,1)S(1)}, u32[]{:S(2)}, u32[]{:S(2)}) collective-permute-start(bf16[896,128]{1,0:T(8,128)(2,1)S(1)} %get-tuple-element.25.first_tail), channel_id=1, source_target_pairs={{1,3},{0,16},{3,5},{2,18},{5,7},{4,20},{7,9},{6,22},{9,11},{8,24},... | collective-permute-start | bytes 688136 | tf_op jit(solution)/shard_map/ppermute | solution.py:422
  4.1 2.5 %shard_map.128 = (bf16[1280,128]{1,0:T(8,128)(2,1)S(1)}, f32[1280,128]{1,0:T(8,128)S(1)}, s32[1280,128]{1,0:T(8,128)S(1)}, bf16[256,384]{1,0:T(8,128)(2,1)S(1)},...) custom-call(s32[1]{0:T(128)} %bitcast.side, ...), custom_call_target="tpu_custom_call" | custom-call | flops 1000000000 | bytes 1000000 | tf_op jit(solution)/shard_map/pallas_call | solution.py:369
  6.6 1.5 %collective-permute-done.4.halo = bf16[896,128]{1,0:T(8,128)(2,1)S(1)} collective-permute-done((bf16[896,128]{1,0:T(8,128)(2,1)S(1)}, bf16[896,128]{1,0:T(8,128)(2,1)S(1)}, u32[]{:S(2)}, u32[]{:S(2)}) %collective-permute-start.4) | collective-permute-done | bytes 229408 | tf_op jit(solution)/shard_map/ppermute | solution.py:422
  8.1 2.5 %collective-permute-start.5 = (bf16[896,128]{1,0:T(8,128)(2,1)S(1)}, bf16[896,128]{1,0:T(8,128)(2,1)S(1)}, u32[]{:S(2)}, u32[]{:S(2)}) collective-permute-start(bf16[896,128]{1,0:T(8,128)(2,1)S(1)} %shard_map.130), channel_id=1, source_target_pairs={{0,1},{1,0},{2,3},{3,2},{4,5},{5,4},{6,7},{7,6},{8,9},{9,8},{10,11... | collective-permute-start | bytes 688136 | tf_op jit(solution)/shard_map/ppermute | solution.py:471
  10.6 0.0 collective-permute-start.3
  10.6 1.5 %collective-permute-start = (bf16[384,128]{1,0:T(8,128)(2,1)S(1)}, bf16[384,128]{1,0:T(8,128)(2,1)S(1)}, u32[]{:S(2)}, u32[]{:S(2)}) collective-permute-start(bf16[384,128]{1,0:T(8,128)(2,1)S(1)} %get-tuple-element.26.last_tail), channel_id=1, source_target_pairs={{1,3},{0,16},{3,5},{2,18},{5,7},{4,20},{7,9},{6,22},{9,11},{8,24},... | collective-permute-start | bytes 294920 | tf_op jit(solution)/shard_map/ppermute | solution.py:422
  12.2 1.1 %collective-permute-start.2 = (bf16[384,128]{1,0:T(8,128)(2,1)S(1)}, bf16[384,128]{1,0:T(8,128)(2,1)S(1)}, u32[]{:S(2)}, u32[]{:S(2)}) collective-permute-start(bf16[384,128]{1,0:T(8,128)(2,1)S(1)} %get-tuple-element.26.last_tail), channel_id=1, source_target_pairs={{0,2},{1,17},{2,4},{3,19},{4,6},{5,21},{6,8},{7,23},{8,10},{9,25},... | collective-permute-start | bytes 294920 | tf_op jit(solution)/shard_map/ppermute | solution.py:422
  13.3 3.0 %collective-permute-done.halo = bf16[384,128]{1,0:T(8,128)(2,1)S(1)} collective-permute-done((bf16[384,128]{1,0:T(8,128)(2,1)S(1)}, bf16[384,128]{1,0:T(8,128)(2,1)S(1)}, u32[]{:S(2)}, u32[]{:S(2)}) %collective-permute-start) | collective-permute-done | bytes 98336 | tf_op jit(solution)/shard_map/ppermute | solution.py:422
  16.3 3.5 %collective-permute-start.1 = (bf16[384,128]{1,0:T(8,128)(2,1)S(1)}, bf16[384,128]{1,0:T(8,128)(2,1)S(1)}, u32[]{:S(2)}, u32[]{:S(2)}) collective-permute-start(bf16[384,128]{1,0:T(8,128)(2,1)S(1)} %shard_map.129), channel_id=1, source_target_pairs={{0,1},{1,0},{2,3},{3,2},{4,5},{5,4},{6,7},{7,6},{8,9},{9,8},{10,11... | collective-permute-start | bytes 294920 | tf_op jit(solution)/shard_map/ppermute | solution.py:471
  19.9 1.4 %shard_map.133 = (bf16[256,1024]{1,0:T(8,128)(2,1)S(1)}, bf16[256,1024]{1,0:T(8,128)(2,1)S(1)}, bf16[256,1024]{1,0:T(8,128)(2,1)S(1)}) custom-call(f32[2,800]{1,0:T(2,128)S(1)} %get-tuple-element.33.refs_0_, f32[2,800]{1,0:T(2,128)S(1)} %get-tuple-element.34.refs_1_, f32[2,800]{1,0:T(2,128)S(1)} %get-tuple-element.35.refs_2_, ...), custom_call_target="tpu_custom_call" | custom-call | flops 1000000000 | bytes 1000000 | tf_op jit(solution)/shard_map/pallas_call | solution.py:369
  21.3 0.0 collective-permute-done.5.other
  21.3 1.1 %shard_map.131.before = f32[2560,128]{1,0:T(8,128)S(1)} custom-call(s32[10,128]{1,0:T(8,128)S(1)} %get-tuple-element.28.far, bf16[896,128]{1,0:T(8,128)(2,1)S(1)} %collective-permute-done.5.other), custom_call_target="tpu_custom_call" | custom-call | flops 100000000 | bytes 1000000 | tf_op jit(solution)/shard_map/pallas_call | solution.py:369
  22.4 0.0 collective-permute-done.3.halo
  22.4 1.1 %shard_map.132.before = f32[2560,128]{1,0:T(8,128)S(1)} custom-call(s32[1]{0:T(128)} %bitcast.side, s32[10,128]{1,0:T(8,128)S(1)} %get-tuple-element.27.near, bf16[896,128]{1,0:T(8,128)(2,1)S(1)} %collective-permute-done.3.halo, bf16[256,384]{1,0:T(8,128)(2,1)S(1)} %get-tuple-element.29.table, ...), custom_call_target="tpu_custom_call", output_to_operand_aliasing={{}: (7, {})} | custom-call | flops 100000000 | bytes 1000000 | tf_op jit(solution)/shard_map/pallas_call | solution.py:369
  23.5 0.0 collective-permute-done.2.halo
  23.5 0.0 collective-permute-done.1.other
  23.5 2.8 %shard_map.134 = (f32[2560,128]{1,0:T(8,128)}, f32[2560,128]{1,0:T(8,128)S(1)}) custom-call(s32[1]{0:T(128)} %bitcast.side, s32[10,128]{1,0:T(8,128)S(1)} %get-tuple-element.27.near, s32[10,128]{1,0:T(8,128)S(1)} %get-tuple-element.28.far, bf16[384,128]{1,0:T(8,128)(2,1)S(1)} %collective-permute-done.1.other, ...), custom_call_target="tpu_custom_call", output_to_operand_aliasing={{1}: (9, {})} | custom-call | flops 1000000000 | bytes 1000000 | tf_op jit(solution)/shard_map/pallas_call | solution.py:369
  (2 shorter events, 0.0 us)
Async XLA Ops:
  1.0 7.0 %collective-permute-start.4 = (bf16[896,128]{1,0:T(8,128)(2,1)S(1)}, bf16[896,128]{1,0:T(8,128)(2,1)S(1)}, u32[]{:S(2)}, u32[]{:S(2)}) collective-permute-start(bf16[896,128]{1,0:T(8,128)(2,1)S(1)} %get-tuple-element.25.first_tail), channel_id=1, source_target_pairs={{1,3},{0,16},{3,5},{2,18},{5,7},{4,20},{7,9},{6,22},{9,11},{8,24},... | collective-permute-start | bytes 688136 | tf_op jit(solution)/shard_map/ppermute | solution.py:422
  8.1 13.2 %collective-permute-start.5 = (bf16[896,128]{1,0:T(8,128)(2,1)S(1)}, bf16[896,128]{1,0:T(8,128)(2,1)S(1)}, u32[]{:S(2)}, u32[]{:S(2)}) collective-permute-start(bf16[896,128]{1,0:T(8,128)(2,1)S(1)} %shard_map.130), channel_id=1, source_target_pairs={{0,1},{1,0},{2,3},{3,2},{4,5},{5,4},{6,7},{7,6},{8,9},{9,8},{10,11... | collective-permute-start | bytes 688136 | tf_op jit(solution)/shard_map/ppermute | solution.py:471
  10.6 11.8 %collective-permute-start.3 = (bf16[896,128]{1,0:T(8,128)(2,1)S(1)}, bf16[896,128]{1,0:T(8,128)(2,1)S(1)}, u32[]{:S(2)}, u32[]{:S(2)}) collective-permute-start(bf16[896,128]{1,0:T(8,128)(2,1)S(1)} %get-tuple-element.25.first_tail), channel_id=1, source_target_pairs={{0,2},{1,17},{2,4},{3,19},{4,6},{5,21},{6,8},{7,23},{8,10},{9,25},... | collective-permute-start | bytes 688136 | tf_op jit(solution)/shard_map/ppermute | solution.py:422
  10.6 5.7 %collective-permute-start = (bf16[384,128]{1,0:T(8,128)(2,1)S(1)}, bf16[384,128]{1,0:T(8,128)(2,1)S(1)}, u32[]{:S(2)}, u32[]{:S(2)}) collective-permute-start(bf16[384,128]{1,0:T(8,128)(2,1)S(1)} %get-tuple-element.26.last_tail), channel_id=1, source_target_pairs={{1,3},{0,16},{3,5},{2,18},{5,7},{4,20},{7,9},{6,22},{9,11},{8,24},... | collective-permute-start | bytes 294920 | tf_op jit(solution)/shard_map/ppermute | solution.py:422
  12.2 11.4 %collective-permute-start.2 = (bf16[384,128]{1,0:T(8,128)(2,1)S(1)}, bf16[384,128]{1,0:T(8,128)(2,1)S(1)}, u32[]{:S(2)}, u32[]{:S(2)}) collective-permute-start(bf16[384,128]{1,0:T(8,128)(2,1)S(1)} %get-tuple-element.26.last_tail), channel_id=1, source_target_pairs={{0,2},{1,17},{2,4},{3,19},{4,6},{5,21},{6,8},{7,23},{8,10},{9,25},... | collective-permute-start | bytes 294920 | tf_op jit(solution)/shard_map/ppermute | solution.py:422
  16.3 7.2 %collective-permute-start.1 = (bf16[384,128]{1,0:T(8,128)(2,1)S(1)}, bf16[384,128]{1,0:T(8,128)(2,1)S(1)}, u32[]{:S(2)}, u32[]{:S(2)}) collective-permute-start(bf16[384,128]{1,0:T(8,128)(2,1)S(1)} %shard_map.129), channel_id=1, source_target_pairs={{0,1},{1,0},{2,3},{3,2},{4,5},{5,4},{6,7},{7,6},{8,9},{9,8},{10,11... | collective-permute-start | bytes 294920 | tf_op jit(solution)/shard_map/ppermute | solution.py:471

commit v7 on v6

--- a/solution.py
+++ b/solution.py
@@ -200,7 +200,8 @@
 
 def window_kernel(wires_by_plane, count, side, first_tail, last_tail, wave, *refs):
     sources, refs = refs[:count], refs[count:]
-    high_out, low_out, code_out, table_out, near_out, far_out = refs[:6]
+    high_out, low_out, code_out, table_out = refs[:4]
+    slot_outs, refs = refs[4:8], refs[2:]
     kept = refs[6 : 6 + count - 4]
     front, slots, offset_rows, bad_rows, kernel_taps, words, wide_taps, sems = refs[6 + count - 4 :]
     held = (slots, offset_rows, bad_rows, kernel_taps)
@@ -211,8 +212,10 @@
         copy.wait()
     fill_table(kernel_taps, wide_taps, table_out)
     groups = front.shape[0] // LANES
-    near_out[...] = slots[pl.ds(side[0] * groups, groups), :]
-    far_out[...] = slots[pl.ds((1 - side[0]) * groups, groups), :]
+    for i, out in enumerate(slot_outs):
+        own = side[0] if i < 2 else 1 - side[0]
+        skipped = slot_outs[0].shape[0] if i % 2 else 0
+        out[...] = slots[pl.ds(own * groups + skipped, out.shape[0]), :]
     small = (slots, offset_rows, bad_rows)
     outs = (high_out, low_out, code_out)
     filter_window(wires_by_plane, side, front, (first_tail, last_tail), small, table_out, outs, words)
@@ -303,8 +306,8 @@
     finish_own(side, halo, table, high, low_main, code, wide)
     for load in loads:
         load.wait()
-    place_rows(other.shape[0], wide_other, far_slots, first, ordered)
-    place_rows(halo.shape[0], wide, near_slots, first, ordered)
+    place_rows(other.shape[0], wide_other, far_slots, 0, ordered)
+    place_rows(halo.shape[0], wide, near_slots, 0, ordered)
     copies = []
     for (start, wires), resp in zip(layout, responses):
         half = wires // 2
@@ -423,7 +426,7 @@
 
     constants = [jnp.asarray(t) for t in wire_tables(wires_by_plane)]
     sources = [*small, *constants]
-    slot_shape = shape((rows // LANES, LANES), jnp.int32)
+    slot_shapes = [shape((count // LANES, LANES), jnp.int32) for count in parts] * 2
     window = call(
         functools.partial(window_kernel, wires_by_plane, len(sources)),
         [
@@ -431,8 +434,7 @@
             shape((rows, LANES), jnp.float32),
             shape((rows, LANES), jnp.int32),
             shape((2 * LANES, 3 * LANES), jnp.bfloat16),
-            slot_shape,
-            slot_shape,
+            *slot_shapes,
         ]
         + [like(x) for x in sources[4:]],
         [side_word, first_tail, last_tail, *map(keep, [waveforms, *sources])],
@@ -447,11 +449,11 @@
         10**9,
     )
     own_part = window[:3]
-    table, near, far = window[3:6]
+    table, near_first, near_last, far_first, far_last = window[3:8]
     responses = call(
         functools.partial(response_kernel, wires_by_plane),
         [shape((2 * LANES, 2 * padded(w // 2)), jnp.bfloat16) for w in wires_by_plane],
-        list(window[6:]),
+        list(window[8:]),
         [vm] * 8,
         [],
         10**9,
@@ -471,13 +473,13 @@
         received.append(lax.ppermute(other, "apa", [(0, 1), (1, 0)]))
     placing = [
         pltpu.VMEM((parts[0], LANES), jnp.float32),
-        pltpu.SMEM(slot_shape.shape, jnp.int32),
+        pltpu.SMEM(slot_shapes[0].shape, jnp.int32),
         pltpu.SemaphoreType.DMA((1,)),
     ]
     (placed,) = call(
         place_kernel,
         [shape((channels, LANES), jnp.float32)],
-        [far, received[0]],
+        [far_first, received[0]],
         [vm] * 2,
         placing,
         10**8,
@@ -485,7 +487,7 @@
     (placed,) = call(
         own_kernel,
         [shape((channels, LANES), jnp.float32)],
-        [side_word, near, halos["own", "first"], table, *own_part, placed],
+        [side_word, near_first, halos["own", "first"], table, *own_part, placed],
         [sm] + [vm] * 7,
         placing,
         10**8,
@@ -500,14 +502,14 @@
     return call(
         functools.partial(final_kernel, layout, parts[0]),
         [shape((channels, LANES), jnp.float32)] * 2,
-        [side_word, near, far, received[1], halos["own", "last"], table, *own_part, placed, *responses],
+        [side_word, near_last, far_last, received[1], halos["own", "last"], table, *own_part, placed, *responses],
         [sm] + [vm] * 12,
         [
             pltpu.VMEM((parts[1], LANES), jnp.float32),
             pltpu.VMEM((parts[1], LANES), jnp.float32),
             pltpu.VMEM((channels, LANES), jnp.float32),
-            pltpu.SMEM(slot_shape.shape, jnp.int32),
-            pltpu.SMEM(slot_shape.shape, jnp.int32),
+            pltpu.SMEM(slot_shapes[1].shape, jnp.int32),
+            pltpu.SMEM(slot_shapes[1].shape, jnp.int32),
             pltpu.SemaphoreType.DMA((5,)),
         ],
         10**9,

time: 26.5 us -> 26.4 us (level)
  no operation moved by 1% of the time
where the time goes in v7:
time: 26.4 us; the launch traced here: 26.2 us
  starting transfers between devices  11.8 us (45%)
  Pallas kernels  9.76 us (37%)
  waiting for transfers between devices  4.52 us (17%)
    pallas_call x8, Pallas kernels, call(): pl.pallas_call(kernel, out_shape=outs, in_specs=specs, out_specs=more.pop...  9.76 us
    ppermute x2, starting transfers between devices, deconvolve(): received.append(lax.ppermute(other, 'apa', [(0, 1), (1, 0)]))  6.08 us
    ppermute x4, starting transfers between devices, deconvolve(): halos[whose, name] = lax.ppermute(part, axes, onward(core))  5.72 us
    ppermute x4, waiting for transfers between devices, deconvolve(): halos[whose, name] = lax.ppermute(part, axes, onward(core))  4.52 us
  transfers between devices with their start and end apart: 6, of which 2 were waited for; matrix products, arithmetic and copies ran while one was open for 0% of the time, Pallas kernels for 23%

profile of v7, /device:TPU:0, one launch (start us, length us, event | category | flops | bytes accessed | tf_op | source)
XLA Modules:
  0.0 26.2 jit_solution(13364270743328359100)
XLA Ops:
  0.0 1.0 %shard_map.127 = (bf16[896,128]{1,0:T(8,128)(2,1)S(1)}, bf16[384,128]{1,0:T(8,128)(2,1)S(1)}) custom-call(bf16[1280,256]{1,0:T(8,128)(2,1)} %wave.3), custom_call_target="tpu_custom_call" | custom-call | flops 100000 | bytes 1000000 | tf_op jit(solution)/shard_map/pallas_call | solution.py:372
  1.0 3.0 %collective-permute-start.4 = (bf16[896,128]{1,0:T(8,128)(2,1)S(1)}, bf16[896,128]{1,0:T(8,128)(2,1)S(1)}, u32[]{:S(2)}, u32[]{:S(2)}) collective-permute-start(bf16[896,128]{1,0:T(8,128)(2,1)S(1)} %get-tuple-element.27.first_tail), channel_id=1, source_target_pairs={{1,3},{0,16},{3,5},{2,18},{5,7},{4,20},{7,9},{6,22},{9,11},{8,24},... | collective-permute-start | bytes 688136 | tf_op jit(solution)/shard_map/ppermute | solution.py:425
  4.1 2.5 %shard_map.128 = (bf16[1280,128]{1,0:T(8,128)(2,1)S(1)}, f32[1280,128]{1,0:T(8,128)S(1)}, s32[1280,128]{1,0:T(8,128)S(1)}, bf16[256,384]{1,0:T(8,128)(2,1)S(1)},...) custom-call(s32[1]{0:T(128)} %bitcast.side, ...), custom_call_target="tpu_custom_call" | custom-call | flops 1000000000 | bytes 1000000 | tf_op jit(solution)/shard_map/pallas_call | solution.py:372
  6.6 1.5 %collective-permute-done.4.halo = bf16[896,128]{1,0:T(8,128)(2,1)S(1)} collective-permute-done((bf16[896,128]{1,0:T(8,128)(2,1)S(1)}, bf16[896,128]{1,0:T(8,128)(2,1)S(1)}, u32[]{:S(2)}, u32[]{:S(2)}) %collective-permute-start.4) | collective-permute-done | bytes 229408 | tf_op jit(solution)/shard_map/ppermute | solution.py:425
  8.1 2.5 %collective-permute-start.5 = (bf16[896,128]{1,0:T(8,128)(2,1)S(1)}, bf16[896,128]{1,0:T(8,128)(2,1)S(1)}, u32[]{:S(2)}, u32[]{:S(2)}) collective-permute-start(bf16[896,128]{1,0:T(8,128)(2,1)S(1)} %shard_map.130), channel_id=1, source_target_pairs={{0,1},{1,0},{2,3},{3,2},{4,5},{5,4},{6,7},{7,6},{8,9},{9,8},{10,11... | collective-permute-start | bytes 688136 | tf_op jit(solution)/shard_map/ppermute | solution.py:473
  10.6 0.0 collective-permute-start.3
  10.6 1.5 %collective-permute-start = (bf16[384,128]{1,0:T(8,128)(2,1)S(1)}, bf16[384,128]{1,0:T(8,128)(2,1)S(1)}, u32[]{:S(2)}, u32[]{:S(2)}) collective-permute-start(bf16[384,128]{1,0:T(8,128)(2,1)S(1)} %get-tuple-element.28.last_tail), channel_id=1, source_target_pairs={{1,3},{0,16},{3,5},{2,18},{5,7},{4,20},{7,9},{6,22},{9,11},{8,24},... | collective-permute-start | bytes 294920 | tf_op jit(solution)/shard_map/ppermute | solution.py:425
  12.2 1.1 %collective-permute-start.2 = (bf16[384,128]{1,0:T(8,128)(2,1)S(1)}, bf16[384,128]{1,0:T(8,128)(2,1)S(1)}, u32[]{:S(2)}, u32[]{:S(2)}) collective-permute-start(bf16[384,128]{1,0:T(8,128)(2,1)S(1)} %get-tuple-element.28.last_tail), channel_id=1, source_target_pairs={{0,2},{1,17},{2,4},{3,19},{4,6},{5,21},{6,8},{7,23},{8,10},{9,25},... | collective-permute-start | bytes 294920 | tf_op jit(solution)/shard_map/ppermute | solution.py:425
  13.3 3.0 %collective-permute-done.halo = bf16[384,128]{1,0:T(8,128)(2,1)S(1)} collective-permute-done((bf16[384,128]{1,0:T(8,128)(2,1)S(1)}, bf16[384,128]{1,0:T(8,128)(2,1)S(1)}, u32[]{:S(2)}, u32[]{:S(2)}) %collective-permute-start) | collective-permute-done | bytes 98336 | tf_op jit(solution)/shard_map/ppermute | solution.py:425
  16.3 3.5 %collective-permute-start.1 = (bf16[384,128]{1,0:T(8,128)(2,1)S(1)}, bf16[384,128]{1,0:T(8,128)(2,1)S(1)}, u32[]{:S(2)}, u32[]{:S(2)}) collective-permute-start(bf16[384,128]{1,0:T(8,128)(2,1)S(1)} %shard_map.129), channel_id=1, source_target_pairs={{0,1},{1,0},{2,3},{3,2},{4,5},{5,4},{6,7},{7,6},{8,9},{9,8},{10,11... | collective-permute-start | bytes 294920 | tf_op jit(solution)/shard_map/ppermute | solution.py:473
  19.9 1.4 %shard_map.133 = (bf16[256,1024]{1,0:T(8,128)(2,1)S(1)}, bf16[256,1024]{1,0:T(8,128)(2,1)S(1)}, bf16[256,1024]{1,0:T(8,128)(2,1)S(1)}) custom-call(f32[2,800]{1,0:T(2,128)S(1)} %get-tuple-element.37.refs_0_, f32[2,800]{1,0:T(2,128)S(1)} %get-tuple-element.38.refs_1_, f32[2,800]{1,0:T(2,128)S(1)} %get-tuple-element.39.refs_2_, ...), custom_call_target="tpu_custom_call" | custom-call | flops 1000000000 | bytes 1000000 | tf_op jit(solution)/shard_map/pallas_call | solution.py:372
  21.3 0.0 collective-permute-done.5.other
  21.3 1.1 %shard_map.131.before = f32[2560,128]{1,0:T(8,128)S(1)} custom-call(s32[7,128]{1,0:T(8,128)S(1)} %get-tuple-element.36.far, bf16[896,128]{1,0:T(8,128)(2,1)S(1)} %collective-permute-done.5.other), custom_call_target="tpu_custom_call" | custom-call | flops 100000000 | bytes 1000000 | tf_op jit(solution)/shard_map/pallas_call | solution.py:372
  22.4 0.0 collective-permute-done.3.halo
  22.4 1.1 %shard_map.132.before = f32[2560,128]{1,0:T(8,128)S(1)} custom-call(s32[1]{0:T(128)} %bitcast.side, s32[7,128]{1,0:T(8,128)S(1)} %get-tuple-element.35.near, bf16[896,128]{1,0:T(8,128)(2,1)S(1)} %collective-permute-done.3.halo, bf16[256,384]{1,0:T(8,128)(2,1)S(1)} %get-tuple-element.31.table, ...), custom_call_target="tpu_custom_call", output_to_operand_aliasing={{}: (7, {})} | custom-call | flops 100000000 | bytes 1000000 | tf_op jit(solution)/shard_map/pallas_call | solution.py:372
  23.5 0.0 collective-permute-done.2.halo
  23.5 0.0 collective-permute-done.1.other
  23.5 2.7 %shard_map.134 = (f32[2560,128]{1,0:T(8,128)}, f32[2560,128]{1,0:T(8,128)S(1)}) custom-call(s32[1]{0:T(128)} %bitcast.side, s32[3,128]{1,0:T(4,128)S(1)} %get-tuple-element.29.near, s32[3,128]{1,0:T(4,128)S(1)} %get-tuple-element.30.far, bf16[384,128]{1,0:T(8,128)(2,1)S(1)} %collective-permute-done.1.other, ...), custom_call_target="tpu_custom_call", output_to_operand_aliasing={{1}: (9, {})} | custom-call | flops 1000000000 | bytes 1000000 | tf_op jit(solution)/shard_map/pallas_call | solution.py:372
  (2 shorter events, 0.0 us)
Async XLA Ops:
  1.0 7.0 %collective-permute-start.4 = (bf16[896,128]{1,0:T(8,128)(2,1)S(1)}, bf16[896,128]{1,0:T(8,128)(2,1)S(1)}, u32[]{:S(2)}, u32[]{:S(2)}) collective-permute-start(bf16[896,128]{1,0:T(8,128)(2,1)S(1)} %get-tuple-element.27.first_tail), channel_id=1, source_target_pairs={{1,3},{0,16},{3,5},{2,18},{5,7},{4,20},{7,9},{6,22},{9,11},{8,24},... | collective-permute-start | bytes 688136 | tf_op jit(solution)/shard_map/ppermute | solution.py:425
  8.1 13.2 %collective-permute-start.5 = (bf16[896,128]{1,0:T(8,128)(2,1)S(1)}, bf16[896,128]{1,0:T(8,128)(2,1)S(1)}, u32[]{:S(2)}, u32[]{:S(2)}) collective-permute-start(bf16[896,128]{1,0:T(8,128)(2,1)S(1)} %shard_map.130), channel_id=1, source_target_pairs={{0,1},{1,0},{2,3},{3,2},{4,5},{5,4},{6,7},{7,6},{8,9},{9,8},{10,11... | collective-permute-start | bytes 688136 | tf_op jit(solution)/shard_map/ppermute | solution.py:473
  10.6 11.7 %collective-permute-start.3 = (bf16[896,128]{1,0:T(8,128)(2,1)S(1)}, bf16[896,128]{1,0:T(8,128)(2,1)S(1)}, u32[]{:S(2)}, u32[]{:S(2)}) collective-permute-start(bf16[896,128]{1,0:T(8,128)(2,1)S(1)} %get-tuple-element.27.first_tail), channel_id=1, source_target_pairs={{0,2},{1,17},{2,4},{3,19},{4,6},{5,21},{6,8},{7,23},{8,10},{9,25},... | collective-permute-start | bytes 688136 | tf_op jit(solution)/shard_map/ppermute | solution.py:425
  10.6 5.7 %collective-permute-start = (bf16[384,128]{1,0:T(8,128)(2,1)S(1)}, bf16[384,128]{1,0:T(8,128)(2,1)S(1)}, u32[]{:S(2)}, u32[]{:S(2)}) collective-permute-start(bf16[384,128]{1,0:T(8,128)(2,1)S(1)} %get-tuple-element.28.last_tail), channel_id=1, source_target_pairs={{1,3},{0,16},{3,5},{2,18},{5,7},{4,20},{7,9},{6,22},{9,11},{8,24},... | collective-permute-start | bytes 294920 | tf_op jit(solution)/shard_map/ppermute | solution.py:425
  12.2 11.3 %collective-permute-start.2 = (bf16[384,128]{1,0:T(8,128)(2,1)S(1)}, bf16[384,128]{1,0:T(8,128)(2,1)S(1)}, u32[]{:S(2)}, u32[]{:S(2)}) collective-permute-start(bf16[384,128]{1,0:T(8,128)(2,1)S(1)} %get-tuple-element.28.last_tail), channel_id=1, source_target_pairs={{0,2},{1,17},{2,4},{3,19},{4,6},{5,21},{6,8},{7,23},{8,10},{9,25},... | collective-permute-start | bytes 294920 | tf_op jit(solution)/shard_map/ppermute | solution.py:425
  16.3 7.2 %collective-permute-start.1 = (bf16[384,128]{1,0:T(8,128)(2,1)S(1)}, bf16[384,128]{1,0:T(8,128)(2,1)S(1)}, u32[]{:S(2)}, u32[]{:S(2)}) collective-permute-start(bf16[384,128]{1,0:T(8,128)(2,1)S(1)} %shard_map.129), channel_id=1, source_target_pairs={{0,1},{1,0},{2,3},{3,2},{4,5},{5,4},{6,7},{7,6},{8,9},{9,8},{10,11... | collective-permute-start | bytes 294920 | tf_op jit(solution)/shard_map/ppermute | solution.py:473

commit v8 on v7

--- a/solution.py
+++ b/solution.py
@@ -27,21 +27,28 @@
     return -(-count // LANES) * LANES
 
 
+def frequency_classes(wires):
+    return [(0, 4, wires // 4), (2, 4, wires // 4), (1, 2, wires // 2)]
+
+
 def wire_tables(wires_by_plane):
     widest = max(wires_by_plane)
     coarse_rows, fine_rows = [], []
     for wires in wires_by_plane[1:]:
-        base = padded(wires // 2)
         m = np.arange(wires, dtype=np.int64)
-        step = np.arange(2 * base // LANES, dtype=np.int64)[:, None] * LANES - base
         turn = 2.0 * math.pi / wires
-        coarse = step * m[None, :] % wires * turn
+        parts = []
+        for first, step, length in frequency_classes(wires):
+            base = padded(length)
+            k = np.arange(2 * base // LANES, dtype=np.int64)[:, None] * LANES - base
+            angle = k * m[None, :] % wires * turn
+            parts.append((angle, (m % step == first)[None, :]))
+        for function in (np.cos, np.sin):
+            for angle, chosen in parts:
+                full = np.zeros((angle.shape[0], widest), np.float32)
+                full[:, :wires] = function(angle) * chosen
+                coarse_rows.append(full)
         fine = m[:, None] * np.arange(LANES, dtype=np.int64)[None, :] % wires * turn
-        for table in (np.cos(coarse), np.sin(coarse)):
-            full = np.zeros((2, step.shape[0], widest), np.float32)
-            full[0, :, :wires:2] = table[:, ::2]
-            full[1, :, 1:wires:2] = table[:, 1::2]
-            coarse_rows.append(full.reshape(-1, widest))
         fine_rows.append(np.concatenate([np.cos(fine), np.sin(fine)], 1).astype(np.float32))
     fine = np.concatenate(fine_rows, 0)
     high = fine.astype(jnp.bfloat16)
@@ -86,10 +93,11 @@
     l = lax.broadcasted_iota(jnp.int32, (LANES, LANES), 1)
     for plane, wires in enumerate(wires_by_plane):
         out = outs[plane]
-        spans = out.shape[1] // LANES
-        first = 0 if plane < 2 else coarse.shape[0] - 4 * spans
-        ca = coarse[first : first + 2 * spans, :wires]
-        sa = coarse[first + 2 * spans : first + 4 * spans, :wires]
+        spans = [2 * padded(length) // LANES for _, _, length in frequency_classes(wires)]
+        total = sum(spans)
+        first = 0 if plane < 2 else coarse.shape[0] - 2 * total
+        ca = coarse[first : first + total, :wires]
+        sa = coarse[first + total : first + 2 * total, :wires]
         first = 0 if plane < 2 else wires_by_plane[0]
         rows = slice(first, first + wires)
         if plane < 2:
@@ -103,17 +111,18 @@
         v = ca * ratio_im - sa * ratio_re
         taps = split_dot(u, fine[rows, :LANES], fine[rows, 2 * LANES : 3 * LANES])
         taps = taps + split_dot(v, fine[rows, LANES : 2 * LANES], fine[rows, 3 * LANES :])
-        for parity in range(2):
-            top = slice(parity * LANES, (parity + 1) * LANES)
+        row = 0
+        for part, count in enumerate(spans):
+            top = slice(part * LANES, (part + 1) * LANES)
             previous = None
-            for span in range(spans):
-                row = parity * spans + span
+            for span in range(count):
                 here = lane_roll(taps[row : row + 1, :], LANES)
                 before = here if previous is None else previous
                 out[top, span * LANES : (span + 1) * LANES] = jnp.where(l >= r, here, before).astype(
                     jnp.bfloat16
                 )
                 previous = here
+                row += 1
 
 
 def delays(word):
@@ -309,25 +318,25 @@
     place_rows(other.shape[0], wide_other, far_slots, 0, ordered)
     place_rows(halo.shape[0], wide, near_slots, 0, ordered)
     copies = []
+
+    def product(resp, part, length, data):
+        pieces = []
+        for top in range(0, length, LANES):
+            rows = slice(part * LANES, part * LANES + min(LANES, length - top))
+            left = padded(length) - top
+            pieces.append(resp[rows, left : left + length])
+        return jnp.dot(jnp.concatenate(pieces, 0), data, preferred_element_type=jnp.float32)
+
     for (start, wires), resp in zip(layout, responses):
-        half = wires // 2
-        base = padded(half)
+        half, quarter = wires // 2, wires // 4
         front = ordered[start : start + half, :]
         back = ordered[start + half : start + wires, :]
-        total = (front + back).astype(jnp.bfloat16)
+        total = front + back
         change = (front - back).astype(jnp.bfloat16)
-        sizes = [min(LANES, half - top) for top in range(0, half, LANES)]
-
-        def rows_of(part):
-            lefts = [base - block * LANES for block in range(len(sizes))]
-            pieces = [
-                resp[part * LANES : part * LANES + size, left : left + half]
-                for size, left in zip(sizes, lefts)
-            ]
-            return jnp.concatenate(pieces, 0)
-
-        even = jnp.dot(rows_of(0), total, preferred_element_type=jnp.float32)
-        odd = jnp.dot(rows_of(1), change, preferred_element_type=jnp.float32)
+        plus = product(resp, 0, quarter, (total[:quarter] + total[quarter:]).astype(jnp.bfloat16))
+        minus = product(resp, 1, quarter, (total[:quarter] - total[quarter:]).astype(jnp.bfloat16))
+        even = jnp.concatenate([plus + minus, plus - minus], 0)
+        odd = product(resp, 2, half, change)
         mixed[start : start + half, :] = even + odd
         mixed[start + half : start + wires, :] = even - odd
         span = pl.ds(start, wires)
@@ -358,6 +367,7 @@
     channels = wire_slot.shape[0]
     assert ticks == 2 * LANES and taps + OFFSET_RANGE == LANES
     assert channels == 2 * rows and channels == 2 * induction + collection
+    assert induction % 4 == 0 and collection % 4 == 0
     parts = (rows - LAST_ROWS, LAST_ROWS)
 
     vm = pl.BlockSpec(memory_space=VMEM)
@@ -452,7 +462,7 @@
     table, near_first, near_last, far_first, far_last = window[3:8]
     responses = call(
         functools.partial(response_kernel, wires_by_plane),
-        [shape((2 * LANES, 2 * padded(w // 2)), jnp.bfloat16) for w in wires_by_plane],
+        [shape((3 * LANES, 2 * padded(w // 2)), jnp.bfloat16) for w in wires_by_plane],
         list(window[8:]),
         [vm] * 8,
         [],

time: 26.4 us -> 26.3 us (level)
  no operation moved by 1% of the time
where the time goes in v8:
time: 26.3 us; the launch traced here: 26.1 us
  starting transfers between devices  11.8 us (45%)
  Pallas kernels  9.66 us (37%)
  waiting for transfers between devices  4.52 us (17%)
    pallas_call x8, Pallas kernels, call(): pl.pallas_call(kernel, out_shape=outs, in_specs=specs, out_specs=more.pop...  9.66 us
    ppermute x2, starting transfers between devices, deconvolve(): received.append(lax.ppermute(other, 'apa', [(0, 1), (1, 0)]))  6.08 us
    ppermute x4, starting transfers between devices, deconvolve(): halos[whose, name] = lax.ppermute(part, axes, onward(core))  5.72 us
    ppermute x4, waiting for transfers between devices, deconvolve(): halos[whose, name] = lax.ppermute(part, axes, onward(core))  4.52 us
  transfers between devices with their start and end apart: 6, of which 2 were waited for; matrix products, arithmetic and copies ran while one was open for 0% of the time, Pallas kernels for 23%

profile of v8, /device:TPU:0, one launch (start us, length us, event | category | flops | bytes accessed | tf_op | source)
XLA Modules:
  0.0 26.1 jit_solution(2404550252004336084)
XLA Ops:
  0.0 1.0 %shard_map.127 = (bf16[896,128]{1,0:T(8,128)(2,1)S(1)}, bf16[384,128]{1,0:T(8,128)(2,1)S(1)}) custom-call(bf16[1280,256]{1,0:T(8,128)(2,1)} %wave.3), custom_call_target="tpu_custom_call" | custom-call | flops 100000 | bytes 1000000 | tf_op jit(solution)/shard_map/pallas_call | solution.py:382
  1.0 3.0 %collective-permute-start.4 = (bf16[896,128]{1,0:T(8,128)(2,1)S(1)}, bf16[896,128]{1,0:T(8,128)(2,1)S(1)}, u32[]{:S(2)}, u32[]{:S(2)}) collective-permute-start(bf16[896,128]{1,0:T(8,128)(2,1)S(1)} %get-tuple-element.27.first_tail), channel_id=1, source_target_pairs={{1,3},{0,16},{3,5},{2,18},{5,7},{4,20},{7,9},{6,22},{9,11},{8,24},... | collective-permute-start | bytes 688136 | tf_op jit(solution)/shard_map/ppermute | solution.py:435
  4.1 2.5 %shard_map.128 = (bf16[1280,128]{1,0:T(8,128)(2,1)S(1)}, f32[1280,128]{1,0:T(8,128)S(1)}, s32[1280,128]{1,0:T(8,128)S(1)}, bf16[256,384]{1,0:T(8,128)(2,1)S(1)},...) custom-call(s32[1]{0:T(128)} %bitcast.side, ...), custom_call_target="tpu_custom_call" | custom-call | flops 1000000000 | bytes 1000000 | tf_op jit(solution)/shard_map/pallas_call | solution.py:382
  6.6 1.5 %collective-permute-done.4.halo = bf16[896,128]{1,0:T(8,128)(2,1)S(1)} collective-permute-done((bf16[896,128]{1,0:T(8,128)(2,1)S(1)}, bf16[896,128]{1,0:T(8,128)(2,1)S(1)}, u32[]{:S(2)}, u32[]{:S(2)}) %collective-permute-start.4) | collective-permute-done | bytes 229408 | tf_op jit(solution)/shard_map/ppermute | solution.py:435
  8.1 2.5 %collective-permute-start.5 = (bf16[896,128]{1,0:T(8,128)(2,1)S(1)}, bf16[896,128]{1,0:T(8,128)(2,1)S(1)}, u32[]{:S(2)}, u32[]{:S(2)}) collective-permute-start(bf16[896,128]{1,0:T(8,128)(2,1)S(1)} %shard_map.130), channel_id=1, source_target_pairs={{0,1},{1,0},{2,3},{3,2},{4,5},{5,4},{6,7},{7,6},{8,9},{9,8},{10,11... | collective-permute-start | bytes 688136 | tf_op jit(solution)/shard_map/ppermute | solution.py:483
  10.6 0.0 collective-permute-start.3
  10.6 1.5 %collective-permute-start = (bf16[384,128]{1,0:T(8,128)(2,1)S(1)}, bf16[384,128]{1,0:T(8,128)(2,1)S(1)}, u32[]{:S(2)}, u32[]{:S(2)}) collective-permute-start(bf16[384,128]{1,0:T(8,128)(2,1)S(1)} %get-tuple-element.28.last_tail), channel_id=1, source_target_pairs={{1,3},{0,16},{3,5},{2,18},{5,7},{4,20},{7,9},{6,22},{9,11},{8,24},... | collective-permute-start | bytes 294920 | tf_op jit(solution)/shard_map/ppermute | solution.py:435
  12.2 1.1 %collective-permute-start.2 = (bf16[384,128]{1,0:T(8,128)(2,1)S(1)}, bf16[384,128]{1,0:T(8,128)(2,1)S(1)}, u32[]{:S(2)}, u32[]{:S(2)}) collective-permute-start(bf16[384,128]{1,0:T(8,128)(2,1)S(1)} %get-tuple-element.28.last_tail), channel_id=1, source_target_pairs={{0,2},{1,17},{2,4},{3,19},{4,6},{5,21},{6,8},{7,23},{8,10},{9,25},... | collective-permute-start | bytes 294920 | tf_op jit(solution)/shard_map/ppermute | solution.py:435
  13.3 3.0 %collective-permute-done.halo = bf16[384,128]{1,0:T(8,128)(2,1)S(1)} collective-permute-done((bf16[384,128]{1,0:T(8,128)(2,1)S(1)}, bf16[384,128]{1,0:T(8,128)(2,1)S(1)}, u32[]{:S(2)}, u32[]{:S(2)}) %collective-permute-start) | collective-permute-done | bytes 98336 | tf_op jit(solution)/shard_map/ppermute | solution.py:435
  16.3 3.5 %collective-permute-start.1 = (bf16[384,128]{1,0:T(8,128)(2,1)S(1)}, bf16[384,128]{1,0:T(8,128)(2,1)S(1)}, u32[]{:S(2)}, u32[]{:S(2)}) collective-permute-start(bf16[384,128]{1,0:T(8,128)(2,1)S(1)} %shard_map.129), channel_id=1, source_target_pairs={{0,1},{1,0},{2,3},{3,2},{4,5},{5,4},{6,7},{7,6},{8,9},{9,8},{10,11... | collective-permute-start | bytes 294920 | tf_op jit(solution)/shard_map/ppermute | solution.py:483
  19.9 1.4 %shard_map.133 = (bf16[384,1024]{1,0:T(8,128)(2,1)S(1)}, bf16[384,1024]{1,0:T(8,128)(2,1)S(1)}, bf16[384,1024]{1,0:T(8,128)(2,1)S(1)}) custom-call(f32[2,800]{1,0:T(2,128)S(1)} %get-tuple-element.37.refs_0_, f32[2,800]{1,0:T(2,128)S(1)} %get-tuple-element.38.refs_1_, f32[2,800]{1,0:T(2,128)S(1)} %get-tuple-element.39.refs_2_, ...), custom_call_target="tpu_custom_call" | custom-call | flops 1000000000 | bytes 1000000 | tf_op jit(solution)/shard_map/pallas_call | solution.py:382
  21.3 0.0 collective-permute-done.5.other
  21.3 1.1 %shard_map.131.before = f32[2560,128]{1,0:T(8,128)S(1)} custom-call(s32[7,128]{1,0:T(8,128)S(1)} %get-tuple-element.36.far, bf16[896,128]{1,0:T(8,128)(2,1)S(1)} %collective-permute-done.5.other), custom_call_target="tpu_custom_call" | custom-call | flops 100000000 | bytes 1000000 | tf_op jit(solution)/shard_map/pallas_call | solution.py:382
  22.4 0.0 collective-permute-done.3.halo
  22.4 1.1 %shard_map.132.before = f32[2560,128]{1,0:T(8,128)S(1)} custom-call(s32[1]{0:T(128)} %bitcast.side, s32[7,128]{1,0:T(8,128)S(1)} %get-tuple-element.35.near, bf16[896,128]{1,0:T(8,128)(2,1)S(1)} %collective-permute-done.3.halo, bf16[256,384]{1,0:T(8,128)(2,1)S(1)} %get-tuple-element.31.table, ...), custom_call_target="tpu_custom_call", output_to_operand_aliasing={{}: (7, {})} | custom-call | flops 100000000 | bytes 1000000 | tf_op jit(solution)/shard_map/pallas_call | solution.py:382
  23.5 0.0 collective-permute-done.2.halo
  23.5 0.0 collective-permute-done.1.other
  23.5 2.6 %shard_map.134 = (f32[2560,128]{1,0:T(8,128)}, f32[2560,128]{1,0:T(8,128)S(1)}) custom-call(s32[1]{0:T(128)} %bitcast.side, s32[3,128]{1,0:T(4,128)S(1)} %get-tuple-element.29.near, s32[3,128]{1,0:T(4,128)S(1)} %get-tuple-element.30.far, bf16[384,128]{1,0:T(8,128)(2,1)S(1)} %collective-permute-done.1.other, ...), custom_call_target="tpu_custom_call", output_to_operand_aliasing={{1}: (9, {})} | custom-call | flops 1000000000 | bytes 1000000 | tf_op jit(solution)/shard_map/pallas_call | solution.py:382
  (2 shorter events, 0.0 us)
Async XLA Ops:
  1.0 7.0 %collective-permute-start.4 = (bf16[896,128]{1,0:T(8,128)(2,1)S(1)}, bf16[896,128]{1,0:T(8,128)(2,1)S(1)}, u32[]{:S(2)}, u32[]{:S(2)}) collective-permute-start(bf16[896,128]{1,0:T(8,128)(2,1)S(1)} %get-tuple-element.27.first_tail), channel_id=1, source_target_pairs={{1,3},{0,16},{3,5},{2,18},{5,7},{4,20},{7,9},{6,22},{9,11},{8,24},... | collective-permute-start | bytes 688136 | tf_op jit(solution)/shard_map/ppermute | solution.py:435
  8.1 13.2 %collective-permute-start.5 = (bf16[896,128]{1,0:T(8,128)(2,1)S(1)}, bf16[896,128]{1,0:T(8,128)(2,1)S(1)}, u32[]{:S(2)}, u32[]{:S(2)}) collective-permute-start(bf16[896,128]{1,0:T(8,128)(2,1)S(1)} %shard_map.130), channel_id=1, source_target_pairs={{0,1},{1,0},{2,3},{3,2},{4,5},{5,4},{6,7},{7,6},{8,9},{9,8},{10,11... | collective-permute-start | bytes 688136 | tf_op jit(solution)/shard_map/ppermute | solution.py:483
  10.6 11.7 %collective-permute-start.3 = (bf16[896,128]{1,0:T(8,128)(2,1)S(1)}, bf16[896,128]{1,0:T(8,128)(2,1)S(1)}, u32[]{:S(2)}, u32[]{:S(2)}) collective-permute-start(bf16[896,128]{1,0:T(8,128)(2,1)S(1)} %get-tuple-element.27.first_tail), channel_id=1, source_target_pairs={{0,2},{1,17},{2,4},{3,19},{4,6},{5,21},{6,8},{7,23},{8,10},{9,25},... | collective-permute-start | bytes 688136 | tf_op jit(solution)/shard_map/ppermute | solution.py:435
  10.6 5.7 %collective-permute-start = (bf16[384,128]{1,0:T(8,128)(2,1)S(1)}, bf16[384,128]{1,0:T(8,128)(2,1)S(1)}, u32[]{:S(2)}, u32[]{:S(2)}) collective-permute-start(bf16[384,128]{1,0:T(8,128)(2,1)S(1)} %get-tuple-element.28.last_tail), channel_id=1, source_target_pairs={{1,3},{0,16},{3,5},{2,18},{5,7},{4,20},{7,9},{6,22},{9,11},{8,24},... | collective-permute-start | bytes 294920 | tf_op jit(solution)/shard_map/ppermute | solution.py:435
  12.2 11.3 %collective-permute-start.2 = (bf16[384,128]{1,0:T(8,128)(2,1)S(1)}, bf16[384,128]{1,0:T(8,128)(2,1)S(1)}, u32[]{:S(2)}, u32[]{:S(2)}) collective-permute-start(bf16[384,128]{1,0:T(8,128)(2,1)S(1)} %get-tuple-element.28.last_tail), channel_id=1, source_target_pairs={{0,2},{1,17},{2,4},{3,19},{4,6},{5,21},{6,8},{7,23},{8,10},{9,25},... | collective-permute-start | bytes 294920 | tf_op jit(solution)/shard_map/ppermute | solution.py:435
  16.3 7.2 %collective-permute-start.1 = (bf16[384,128]{1,0:T(8,128)(2,1)S(1)}, bf16[384,128]{1,0:T(8,128)(2,1)S(1)}, u32[]{:S(2)}, u32[]{:S(2)}) collective-permute-start(bf16[384,128]{1,0:T(8,128)(2,1)S(1)} %shard_map.129), channel_id=1, source_target_pairs={{0,1},{1,0},{2,3},{3,2},{4,5},{5,4},{6,7},{7,6},{8,9},{9,8},{10,11... | collective-permute-start | bytes 294920 | tf_op jit(solution)/shard_map/ppermute | solution.py:483
